TPU v7x, 256 devices: a whole 4x4x8 slice. The times are simulated.
256 devices in a mesh: dom: 32 (over y, x, core), blk: 8 (over z).
Axes of the slice: x: 4, y: 4, z: 8, core: 2. Of those that a mesh axis runs over, the one named last changes fastest.
Arguments:
- displacement: float32 [3, 256, 64, 128], P(None, 'dom', 'blk'), may hold values from -6 to 6
- velocity: float32 [3, 256, 64, 128], P(None, 'dom', 'blk'), may hold values from -6 to 6
- load: float32 [3, 256, 64, 128], P(None, 'dom', 'blk'), may hold values from -6 to 6
- density: float32 [256, 64, 128], P('dom', 'blk'), may hold values from 0.5 to 1.5
- block_class: int32 [32, 8, 16], P('dom', 'blk'), may hold values from 0 to 2
- host_element: int32 [8, 131072], P('blk', 'dom'), may hold values from 0 to 7038, as said below
- host_coords: float32 [3, 8, 131072], P(None, 'blk', 'dom'), may hold values from 0 to 1
- fibre_slot: int32 [512, 8, 128], P('dom', 'blk'), may hold values from 0 to 4095, as said below
- fibre_angles: float32 [2, 512, 8, 128], P(None, 'dom', 'blk'), may hold values from -3.140625 to 3.140625
- fibre_stiffness: float32 [512, 8], P('dom', 'blk'), may hold values from 0.5 to 4
Outputs:
- new_displacement: float32 [3, 256, 64, 128], P(None, 'dom', 'blk')
- new_velocity: float32 [3, 256, 64, 128], P(None, 'dom', 'blk')
Inputs may be any that keep to these rules, and one draw needn't show every extreme that they name: `host_element`: each entry is (i * 8 + j) * 128 + k with i < 7, j < 7, k < 127, a voxel element of the device's own block; a device's entries are laid out as 128 slots for each owner index along dom, in order. `fibre_slot`: the entries of one device are distinct; value // 128 is the dom index of the host device in the same blk column and value % 128 the slot among that host's 128 slots for this owner; on every device all 128 slots of one host are used.
All inputs are finite; a program needn't handle non-finite values.
Results may differ from a plain program's by a relative error of at most 0.0003.
Values sent between devices are 32-bit elements; how exact they have to be, the bound alone decides.
No kernel may reach another device: no remote copies, remote signals or barrier semaphores. Data moves between devices by JAX's collectives and lax.ppermute only.
A program may use at most 64 MiB of HBM per device.

v0:
```python
import math

import jax
import jax.numpy as jnp
import numpy as np
from jax import lax
from jax.sharding import Mesh
from jax.sharding import PartitionSpec as P

DOM = ("dom_0", "dom_1", "dom_2")


class_values = (1.0, 0.45, 0.12)
time_step = 0.25
damping = 0.5


def split_up(shard, dim, size):
    shape = shard.shape
    parts = shard.reshape(*shape[:dim], size, shape[dim] // size, *shape[dim + 1 :])
    return jnp.moveaxis(parts, dim, 0)


def in_order(parts, dim):
    parts = jnp.moveaxis(parts, 0, dim)
    shape = parts.shape
    return parts.reshape(*shape[:dim], shape[dim] * shape[dim + 1], *shape[dim + 2 :])


def moved_by_axis(parts, axes, order):
    shape = [lax.axis_size(a) for a in axes]
    parts = parts.reshape(*shape, *parts.shape[1:])
    for k in order:
        parts = lax.all_to_all(parts, axes[k], split_axis=k, concat_axis=k, tiled=True)
    return parts.reshape(-1, *parts.shape[len(axes) :])


def two_step_exchange(shard, groups, order, split_dim, concat_dim):
    size = lax.axis_size(groups[0]) * lax.axis_size(groups[1])
    parts = split_up(shard, split_dim, size)
    return in_order(moved_by_axis(parts, groups, order), concat_dim)


def from_behind(shard, axis, by):
    size = lax.axis_size(axis)
    pairs = [(i, i + by) for i in range(size) if 0 <= i + by < size]
    return lax.ppermute(shard, axis, pairs)


def stiffness_table():
    poisson = 0.3
    lame = poisson / ((1 + poisson) * (1 - 2 * poisson))
    shear = 0.5 / (1 + poisson)
    elastic = np.zeros((6, 6))
    elastic[:3, :3] = lame
    for place in range(3):
        elastic[place, place] += 2 * shear
        elastic[place + 3, place + 3] = shear
    points = [0.5 - 0.5 / np.sqrt(3.0), 0.5 + 0.5 / np.sqrt(3.0)]
    table = np.zeros((24, 24))
    for gauss_r in points:
        for gauss_p in points:
            for gauss_q in points:
                strain = np.zeros((6, 24))
                for corner in range(8):
                    x_bit, y_bit, z_bit = (corner // 4, corner // 2 % 2, corner % 2)
                    along_r = gauss_r if x_bit else 1 - gauss_r
                    along_p = gauss_p if y_bit else 1 - gauss_p
                    along_q = gauss_q if z_bit else 1 - gauss_q
                    d_x = (2 * x_bit - 1) * along_p * along_q
                    d_y = along_r * (2 * y_bit - 1) * along_q
                    d_z = along_r * along_p * (2 * z_bit - 1)
                    column = 3 * corner
                    strain[0, column] = d_x
                    strain[1, column + 1] = d_y
                    strain[2, column + 2] = d_z
                    strain[3, column] = d_y
                    strain[3, column + 1] = d_x
                    strain[4, column + 1] = d_z
                    strain[4, column + 2] = d_y
                    strain[5, column] = d_z
                    strain[5, column + 2] = d_x
                table += 0.125 * strain.T @ elastic @ strain
    return table


def class_moduli(block_class):
    factor = jnp.zeros(block_class.shape, jnp.float32)
    for index, value in enumerate(class_values):
        factor = factor + jnp.where(block_class == index, jnp.float32(value), jnp.float32(0.0))
    bx, by, bz = block_class.shape
    wide = jnp.broadcast_to(factor[:, None, :, None, :, None], (bx, 8, by, 8, bz, 8))
    return wide.reshape(bx * 8, by * 8, bz * 8)


def lift_depth(local):
    return jnp.concatenate([local[..., 1:], jnp.zeros_like(local[..., :1])], axis=-1)


def own_forces(extended, moduli, density):
    width = extended.shape[1] - 1
    height = extended.shape[2] - 1
    depth = extended.shape[3]
    table = jnp.asarray(stiffness_table(), jnp.float32)
    element = jnp.zeros((24, width, height, depth), jnp.float32)
    for corner in range(8):
        x_bit, y_bit, z_bit = (corner // 4, corner // 2 % 2, corner % 2)
        local = extended[:, x_bit : x_bit + width, y_bit : y_bit + height, :]
        if z_bit:
            local = lift_depth(local)
        element = element + jnp.einsum(
            "ij,jxyz->ixyz",
            table[:, 3 * corner : 3 * corner + 3],
            local,
            precision=lax.Precision.HIGHEST,
        )
    element = element * moduli[None]
    force = jnp.zeros((3, width + 1, height + 1, depth), jnp.float32)
    mass = jnp.zeros((width + 1, height + 1, depth), jnp.float32)
    for corner in range(8):
        x_bit, y_bit, z_bit = (corner // 4, corner // 2 % 2, corner % 2)
        piece = jnp.pad(
            element[3 * corner : 3 * corner + 3],
            ((0, 0), (x_bit, 1 - x_bit), (y_bit, 1 - y_bit), (0, 0)),
        )
        share = jnp.pad(density, ((x_bit, 1 - x_bit), (y_bit, 1 - y_bit), (0, 0)))
        if z_bit:
            piece = jnp.pad(piece[..., :-1], ((0, 0), (0, 0), (0, 0), (1, 0)))
            share = jnp.pad(share[..., :-1], ((0, 0), (0, 0), (1, 0)))
        force = force + piece
        mass = mass + 0.125 * share
    return (force, mass)


def axis_weights(along, lowest, count):
    positions = lax.broadcasted_iota(jnp.int32, (count, along.shape[0]), 0)
    lower = jnp.where(positions == lowest[None], 1.0 - along[None], jnp.float32(0.0))
    upper = jnp.where(positions == lowest[None] + 1, along[None], jnp.float32(0.0))
    return lower + upper


def slot_weights(element, coords, width, height, depth):
    plane = height * depth
    along_x = element // plane
    along_y = element // depth % height
    along_z = element % depth
    weight_x = axis_weights(coords[0], along_x, width)
    weight_y = axis_weights(coords[1], along_y, height)
    weight_z = axis_weights(coords[2], along_z, depth)
    planar = (weight_x[:, None, :] * weight_y[None]).reshape(width * height, -1)
    return (planar, weight_z)


def interpolate(field, planar, weight_z):
    width, height, depth = (field.shape[1], field.shape[2], field.shape[3])
    partial_sums = jnp.dot(
        field.reshape(3 * width * height, depth), weight_z, precision=lax.Precision.HIGHEST
    )
    return jnp.sum(partial_sums.reshape(3, width * height, -1) * planar[None], axis=1)


def spread(force, planar, weight_z, width, height, depth):
    terms = (force[:, None, :] * planar[None]).reshape(3 * width * height, -1)
    summed = jnp.dot(terms, weight_z.T, precision=lax.Precision.HIGHEST)
    return summed.reshape(3, width, height, depth)


def pick_rows(places, wanted, span_rows):
    total = places.shape[1]
    groups = wanted.reshape(-1, span_rows)

    def pick_single(members):
        onehot = (
            members[:, None] == lax.broadcasted_iota(jnp.int32, (span_rows, total), 1)
        ).astype(jnp.float32)
        return jnp.dot(places, onehot.T, precision=lax.Precision.HIGHEST)

    picked = lax.map(pick_single, groups)
    return picked.transpose(1, 0, 2).reshape(3, -1)


def place_rows(values, wanted, total, span_rows):
    groups = wanted.reshape(-1, span_rows)
    pieces = values.reshape(3, -1, span_rows).transpose(1, 0, 2)

    def place_single(carry, item):
        members, stretch_values = item
        onehot = (
            members[:, None] == lax.broadcasted_iota(jnp.int32, (span_rows, total), 1)
        ).astype(jnp.float32)
        return (carry + jnp.dot(stretch_values, onehot, precision=lax.Precision.HIGHEST), None)

    result, _ = lax.scan(place_single, jnp.zeros((3, total), jnp.float32), (groups, pieces))
    return result


def fibre_forces(places, slots, angles, stiffness):
    total = places.shape[1]
    fibres, nodes = slots.shape
    wanted = slots.reshape(-1)
    span_rows = math.gcd(fibres * nodes, 512)
    node = pick_rows(places, wanted, span_rows).reshape(3, fibres, nodes)
    direction = jnp.stack(
        [
            jnp.cos(angles[0]) * jnp.cos(angles[1]),
            jnp.sin(angles[0]) * jnp.cos(angles[1]),
            jnp.sin(angles[1]),
        ]
    )
    ahead = jnp.concatenate([node[..., 1:], node[..., -1:]], axis=-1)
    strain = jnp.sum(direction * (ahead - node), axis=0)
    live = lax.broadcasted_iota(jnp.int32, strain.shape, 1) < strain.shape[1] - 1
    tension = jnp.where(live, stiffness * jnp.maximum(strain, 0.0), jnp.float32(0.0))
    pull = tension[None] * direction
    behind = jnp.concatenate([jnp.zeros_like(pull[..., :1]), pull[..., :-1]], axis=-1)
    return place_rows((pull - behind).reshape(3, -1), wanted, total, span_rows)


def shards(
    displacement,
    velocity,
    load,
    density,
    block_class,
    host_element,
    host_coords,
    fibre_slot,
    fibre_angles,
    fibre_stiffness,
):
    width, height, depth = (displacement.shape[1], displacement.shape[2], displacement.shape[3])
    parts = lax.axis_size(DOM)
    moduli = class_moduli(block_class) * density * density
    element = host_element[0]
    coords = host_coords[:, 0]
    planar, weight_z = slot_weights(element, coords, width, height, depth)
    places = interpolate(displacement, planar, weight_z)
    received = lax.all_to_all(
        places.reshape(3, parts, -1), DOM, split_axis=1, concat_axis=1, tiled=True
    )
    pulls = fibre_forces(
        received.reshape(3, -1), fibre_slot[:, 0], fibre_angles[:, :, 0], fibre_stiffness
    )
    returned = two_step_exchange(
        pulls.reshape(3, parts, -1), (("dom_0", "dom_1"), "dom_2"), (1, 0), 1, 1
    )
    fibre = spread(returned.reshape(3, -1), planar, weight_z, width, height, depth)
    top_row = from_behind(displacement[:, :1], DOM, -1)
    extended = jnp.concatenate([displacement, top_row], axis=1)
    side_col = from_behind(extended[:, :, :1], "blk", -1)
    extended = jnp.concatenate([extended, side_col], axis=2)
    force_ext, mass_ext = own_forces(extended, moduli, density)
    stacked = jnp.concatenate([force_ext, mass_ext[None]], axis=0)
    edge_col = from_behind(stacked[:, :, height:], "blk", 1)
    stacked = stacked[:, :, :height].at[:, :, :1].add(edge_col)
    edge_row = from_behind(stacked[:, width:], DOM, 1)
    stacked = stacked[:, :width].at[:, :1].add(edge_row)
    elastic = stacked[:3]
    mass = stacked[3]
    acceleration = (load - elastic + fibre) / mass[None] - damping * velocity
    new_velocity = velocity + time_step * acceleration
    new_displacement = displacement + time_step * new_velocity
    return (new_displacement, new_velocity)


def solution(mesh):
    finer = Mesh(
        mesh.devices.reshape(4, 4, 2, mesh.shape["blk"]), ("dom_0", "dom_1", "dom_2", "blk")
    )
    in_specs = (
        P(None, DOM, "blk", None),
        P(None, DOM, "blk", None),
        P(None, DOM, "blk", None),
        P(DOM, "blk", None),
        P(DOM, "blk", None),
        P("blk", DOM),
        P(None, "blk", DOM),
        P(DOM, "blk", None),
        P(None, DOM, "blk", None),
        P(DOM, "blk"),
    )
    out_specs = (P(None, DOM, "blk", None), P(None, DOM, "blk", None))
    return jax.shard_map(
        shards, mesh=finer, in_specs=in_specs, out_specs=out_specs, check_vma=False
    )
```

profile of v0, /device:TPU:136, one launch (start us, length us, event | category | flops | bytes accessed | tf_op | source)
XLA Modules:
  0.0 93.0 jit_solution(4350300715633540364)
XLA Ops:
  1.4 4.0 %collective-permute-start = (f32[3,1,8,128]{3,0,2,1:T(4,128)S(1)}, f32[3,1,8,128]{3,0,2,1:T(4,128)S(1)}, u32[]{:S(2)}, u32[]{:S(2)}) collective-permute-start(f32[3,1,8,128]{3,0,2,1:T(4,128)S(1)} %copy.164), channel_id=1, source_target_pairs={{8,0},{16,8},{24,16},{32,24},{40,32},{48,40},{56,48},{64,56},{72,6... | collective-permute-start | bytes 36872 | tf_op jit(solution)/shard_map/ppermute | solution.py:47
  7.4 3.3 %fusion.9 = f32[4096,192]{0,1:T(8,128)S(1)} fusion(f32[192,128]{1,0:T(8,128)S(1)} %bitcast.122, f32[4096]{0:T(1024)S(1)} %bitcast.146, s32[4096]{0:T(1024)S(1)} %bitcast.151, f32[4096]{0:T(1024)S(1)} %broadcast_subtract_fusion.2, s32[4096]{0:T(1024)S(1)} %bitcast.153), kind=kOutput, calls=%fused_computation.18 | convolution fusion | flops 1210580992 | bytes 3309568 | tf_op jit(solution)/shard_map/dot_general | solution.py:156
  10.7 1.0 %multiply_reduce_fusion = f32[3,4096]{1,0:T(4,128)} fusion(f32[3,64,4096]{2,1,0:T(8,128)S(1)} %bitcast.121, f32[64,4096]{1,0:T(8,128)S(1)} %get-tuple-element.142), kind=kLoop, calls=%fused_computation.14 | loop fusion | flops 1560576 | bytes 4243456 | tf_op jit(solution)/shard_map/reduce_sum | solution.py:159
  11.8 5.7 %all-to-all-start = ((f32[3,32,128]{2,0,1:T(4,128)}), f32[3,32,128]{2,0,1:T(4,128)S(1)}, u32[]{:S(2)}, u32[]{:S(2)}) async-start(f32[3,32,128]{2,0,1:T(4,128)} %bitcast.37), calls=%async_computation | async-start | bytes 131072 | tf_op jit(solution)/shard_map/all_to_all | solution.py:238
  21.6 2.2 %collective-permute-start.1 = (f32[3,9,1,128]{3,0,2,1:T(4,128)S(1)}, f32[3,9,1,128]{3,0,2,1:T(4,128)S(1)}, u32[]{:S(2)}, u32[]{:S(2)}) collective-permute-start(f32[3,9,1,128]{3,0,2,1:T(4,128)S(1)} %slice.275), channel_id=1, source_target_pairs={{1,0},{2,1},{3,2},{4,3},{5,4},{6,5},{7,6},{9,8},{10,9},{11,10},{12... | collective-permute-start | bytes 41480 | tf_op jit(solution)/shard_map/ppermute | solution.py:47
  24.7 2.6 %collective-permute-done.1 = f32[3,9,1,128]{3,0,2,1:T(4,128)S(1)} collective-permute-done((f32[3,9,1,128]{3,0,2,1:T(4,128)S(1)}, f32[3,9,1,128]{3,0,2,1:T(4,128)S(1)}, u32[]{:S(2)}, u32[]{:S(2)}) %collective-permute-start.1) | collective-permute-done | bytes 13856 | tf_op jit(solution)/shard_map/ppermute | solution.py:47
  29.3 1.0 %fusion.32 = f32[24,8,8,128]{3,0,2,1:T(8,128)S(1)} fusion(f32[24,3,1,1]{0,1,3,2:T(4,128)S(1)} %copy-done.6, f32[3,9,1,128]{3,0,2,1:T(4,128)S(1)} %collective-permute-done.1, f32[3,9,8,128]{3,0,2,1:T(4,128)S(1)} %constant_dynamic-update-slice_fusion), kind=kOutput, calls=%fused_computation.64 | convolution fusion | flops 7176192 | bytes 911136 | tf_op jit(solution)/shard_map/ij,jxyz->ixyz/dot_general | solution.py:111
  33.4 2.9 %collective-permute-start.2 = (f32[4,9,1,128]{3,2,1,0:T(1,128)S(1)}, f32[4,9,1,128]{3,2,1,0:T(1,128)S(1)}, u32[]{:S(2)}, u32[]{:S(2)}) collective-permute-start(f32[4,9,1,128]{3,2,1,0:T(1,128)S(1)} %pad_maximum_fusion.1), channel_id=1, source_target_pairs={{0,1},{1,2},{2,3},{3,4},{4,5},{5,6},{6,7},{8,9},{9,10},{10,11},{11... | collective-permute-start | bytes 55304 | tf_op jit(solution)/shard_map/ppermute | solution.py:47
  36.3 3.9 %collective-permute-done.2 = f32[4,9,1,128]{3,2,1,0:T(1,128)S(1)} collective-permute-done((f32[4,9,1,128]{3,2,1,0:T(1,128)S(1)}, f32[4,9,1,128]{3,2,1,0:T(1,128)S(1)}, u32[]{:S(2)}, u32[]{:S(2)}) %collective-permute-start.2) | collective-permute-done | bytes 18464 | tf_op jit(solution)/shard_map/ppermute | solution.py:47
  40.4 1.9 %collective-permute-start.3 = (f32[4,1,8,128]{3,2,1,0:T(8,128)S(1)}, f32[4,1,8,128]{3,2,1,0:T(8,128)S(1)}, u32[]{:S(2)}, u32[]{:S(2)}) collective-permute-start(f32[4,1,8,128]{3,2,1,0:T(8,128)S(1)} %slice.298), channel_id=1, source_target_pairs={{0,8},{8,16},{16,24},{24,32},{32,40},{40,48},{48,56},{56,64},{64,7... | collective-permute-start | bytes 49160 | tf_op jit(solution)/shard_map/ppermute | solution.py:47
  42.3 16.0 %while.23 = (s32[]{:T(128)}, f32[4,3,512]{2,0,1:T(4,128)S(1)}, s32[4,512]{1,0:T(4,128)S(1)}, f32[3,4096]{1,0:T(4,128)S(1)}, s32[]{:T(128)}, /*index=5*/s32[]{:T(128)}) while((s32[]{:T(128)}, f32[4,3,512]{2,0,1:T(4,128)S(1)}, s32[4,512]{1,0:T(4,128)S(1)}, f32[3,4096]{1,0:T(4,128)S(1)}, s32[]{:T(128)}, /*index=5*/s32[]{:T(128)}) %tuple.91), condition=%wide.region_2.3_spmd, body=%wide.region_1.2_spmd.sunk | while | flops 77594624 | bytes 86101 | solution.py:178
  42.4 3.9 %fusion.97 = f32[1,3,512]{2,1,0:T(4,128)S(1)} fusion(f32[3,4096]{1,0:T(4,128)S(1)} %get-tuple-element.234, s32[512]{0:T(512)S(1)} %bitcast.149), kind=kOutput, calls=%fused_computation.3.clone.1 | convolution fusion | flops 77594624 | bytes 57344 | tf_op jit(solution)/shard_map/while/body/eval_jaxpr/dot_general | solution.py:176
  46.3 3.9 %fusion.97 = f32[1,3,512]{2,1,0:T(4,128)S(1)} fusion(f32[3,4096]{1,0:T(4,128)S(1)} %get-tuple-element.234, s32[512]{0:T(512)S(1)} %bitcast.149), kind=kOutput, calls=%fused_computation.3.clone.1 | convolution fusion | flops 77594624 | bytes 57344 | tf_op jit(solution)/shard_map/while/body/eval_jaxpr/dot_general | solution.py:176
  50.3 3.9 %fusion.97 = f32[1,3,512]{2,1,0:T(4,128)S(1)} fusion(f32[3,4096]{1,0:T(4,128)S(1)} %get-tuple-element.234, s32[512]{0:T(512)S(1)} %bitcast.149), kind=kOutput, calls=%fused_computation.3.clone.1 | convolution fusion | flops 77594624 | bytes 57344 | tf_op jit(solution)/shard_map/while/body/eval_jaxpr/dot_general | solution.py:176
  54.3 3.9 %fusion.97 = f32[1,3,512]{2,1,0:T(4,128)S(1)} fusion(f32[3,4096]{1,0:T(4,128)S(1)} %get-tuple-element.234, s32[512]{0:T(512)S(1)} %bitcast.149), kind=kOutput, calls=%fused_computation.3.clone.1 | convolution fusion | flops 77594624 | bytes 57344 | tf_op jit(solution)/shard_map/while/body/eval_jaxpr/dot_general | solution.py:176
  58.8 11.3 %while.24 = (s32[]{:T(128)}, f32[3,4096]{1,0:T(4,128)S(1)}, f32[4,3,512]{2,0,1:T(4,128)S(1)}, s32[4,512]{1,0:T(4,128)S(1)}, s32[]{:T(128)}, /*index=5*/s32[]{:T(128)}) while((s32[]{:T(128)}, f32[3,4096]{1,0:T(4,128)S(1)}, f32[4,3,512]{2,0,1:T(4,128)S(1)}, s32[4,512]{1,0:T(4,128)S(1)}, s32[]{:T(128)}, /*index=5*/s32[]{:T(128)}) %tuple.90), condition=%wide.region_5.6_spmd.clone, body=%wide.region_4.5_spmd.clone.sunk | while | flops 77619200 | bytes 122975 | solution.py:193
  58.9 2.8 %fusion.98 = f32[3,4096]{1,0:T(4,128)S(1)} fusion(s32[512]{0:T(512)S(1)} %bitcast.148, f32[3,4096]{1,0:T(4,128)S(1)} %get-tuple-element.244, pred[]{:T(512)S(6)} %compare.60, f32[1,3,512]{2,0,1:T(1,128)S(1)} %constant_dynamic-slice_fusion.8), kind=kOutput, calls=%fused_computation.7.clone.1 | convolution fusion | flops 77619200 | bytes 106497 | tf_op jit(solution)/shard_map/while/body/eval_jaxpr/dot_general | solution.py:191
  61.7 2.8 %fusion.98 = f32[3,4096]{1,0:T(4,128)S(1)} fusion(s32[512]{0:T(512)S(1)} %bitcast.148, f32[3,4096]{1,0:T(4,128)S(1)} %get-tuple-element.244, pred[]{:T(512)S(6)} %compare.60, f32[1,3,512]{2,0,1:T(1,128)S(1)} %constant_dynamic-slice_fusion.8), kind=kOutput, calls=%fused_computation.7.clone.1 | convolution fusion | flops 77619200 | bytes 106497 | tf_op jit(solution)/shard_map/while/body/eval_jaxpr/dot_general | solution.py:191
  64.5 2.8 %fusion.98 = f32[3,4096]{1,0:T(4,128)S(1)} fusion(s32[512]{0:T(512)S(1)} %bitcast.148, f32[3,4096]{1,0:T(4,128)S(1)} %get-tuple-element.244, pred[]{:T(512)S(6)} %compare.60, f32[1,3,512]{2,0,1:T(1,128)S(1)} %constant_dynamic-slice_fusion.8), kind=kOutput, calls=%fused_computation.7.clone.1 | convolution fusion | flops 77619200 | bytes 106497 | tf_op jit(solution)/shard_map/while/body/eval_jaxpr/dot_general | solution.py:191
  67.3 2.8 %fusion.98 = f32[3,4096]{1,0:T(4,128)S(1)} fusion(s32[512]{0:T(512)S(1)} %bitcast.148, f32[3,4096]{1,0:T(4,128)S(1)} %get-tuple-element.244, pred[]{:T(512)S(6)} %compare.60, f32[1,3,512]{2,0,1:T(1,128)S(1)} %constant_dynamic-slice_fusion.8), kind=kOutput, calls=%fused_computation.7.clone.1 | convolution fusion | flops 77619200 | bytes 106497 | tf_op jit(solution)/shard_map/while/body/eval_jaxpr/dot_general | solution.py:191
  70.2 5.1 %all_to_all.15 = f32[16,2,3,1,128]{4,0,2,3,1:T(8,128)S(1)} all-to-all(f32[16,2,3,1,128]{4,0,2,3,1:T(8,128)S(1)} %copy.91), channel_id=1, replica_groups=mesh['dom_0'=4,'dom_1'=4,'dom_2'=2,'blk'=8] {'dom_2'}, dimensions={1} | all-to-all | bytes 98304 | tf_op jit(solution)/shard_map/all_to_all | solution.py:34
  75.8 7.0 %all-to-all-start.2 = ((f32[16,2,3,1,128]{4,1,2,3,0:T(2,128)}), f32[16,2,3,1,128]{4,1,2,3,0:T(2,128)S(1)}, u32[]{:S(2)}, u32[]{:S(2)}) async-start(f32[16,2,3,1,128]{4,1,2,3,0:T(2,128)} %copy.92), calls=%async_computation.2 | async-start | bytes 98304 | tf_op jit(solution)/shard_map/all_to_all | solution.py:34
  82.8 6.2 %all-to-all-done.2 = f32[16,2,3,1,128]{4,1,2,3,0:T(2,128)S(1)} async-done(((f32[16,2,3,1,128]{4,1,2,3,0:T(2,128)}), f32[16,2,3,1,128]{4,1,2,3,0:T(2,128)S(1)}, u32[]{:S(2)}, u32[]{:S(2)}) %all-to-all-start.2) | async-done | bytes 49184 | tf_op jit(solution)/shard_map/all_to_all | solution.py:34
  89.1 3.9 %multiply_add_fusion = (f32[3,8,8,128]{3,2,1,0:T(8,128)}, f32[3,8,8,128]{3,2,1,0:T(8,128)}) fusion(f32[3,8,8,128]{3,2,1,0:T(8,128)S(1)} %copy-done, f32[3,8,8,128]{3,2,1,0:T(8,128)S(1)} %copy-done.13, f32[8,8,128]{2,1,0:T(8,128)S(1)} %slice_bitcast_fusion, f32[4096]{0:T(1024)S(1)} %bitcast.147, s32[4096]{0:T(1024)S(1)} %bitcast.152, ...), kind=kOutput, calls=%fused_computation.89 | convolution fusion | flops 1211588608 | bytes 1785856 | tf_op jit(solution)/shard_map/dot_general | solution.py:164
  (125 shorter events, 14.3 us)
Async XLA Ops:
  0.6 6.8 %copy-start = (f32[3,8,8,128]{3,2,1,0:T(8,128)S(1)}, f32[3,8,8,128]{3,2,1,0:T(8,128)}, u32[]{:S(2)}) copy-start(f32[3,8,8,128]{3,2,1,0:T(8,128)} %param.19) | copy-start | bytes 294916
  1.4 20.2 %collective-permute-start = (f32[3,1,8,128]{3,0,2,1:T(4,128)S(1)}, f32[3,1,8,128]{3,0,2,1:T(4,128)S(1)}, u32[]{:S(2)}, u32[]{:S(2)}) collective-permute-start(f32[3,1,8,128]{3,0,2,1:T(4,128)S(1)} %copy.164), channel_id=1, source_target_pairs={{8,0},{16,8},{24,16},{32,24},{40,32},{48,40},{56,48},{64,56},{72,6... | collective-permute-start | bytes 36872 | tf_op jit(solution)/shard_map/ppermute | solution.py:47
  10.7 7.0 %copy-start.11 = (f32[24,3,1,1]{0,1,3,2:T(4,128)S(1)}, f32[24,3,1,1]{0,1,3,2:T(4,128)}, u32[]{:S(2)}) copy-start(f32[24,3,1,1]{0,1,3,2:T(4,128)} %constant.216) | copy-start | bytes 868
  10.7 7.9 %copy-start.15 = (s32[1,1,16]{2,1,0:T(1,128)S(1)}, s32[1,1,16]{2,1,0:T(1,128)}, u32[]{:S(2)}) copy-start(s32[1,1,16]{2,1,0:T(1,128)} %param.23) | copy-start | bytes 196
  10.7 8.1 %copy-start.1 = (f32[8,8,128]{2,1,0:T(8,128)S(1)}, f32[8,8,128]{2,1,0:T(8,128)}, u32[]{:S(2)}) copy-start(f32[8,8,128]{2,1,0:T(8,128)} %param.22) | copy-start | bytes 98308
  11.8 7.1 %copy-start.2 = (f32[2,16,1,128]{3,2,1,0:T(1,128)S(1)}, f32[2,16,1,128]{3,2,1,0:T(1,128)}, u32[]{:S(2)}) copy-start(f32[2,16,1,128]{3,2,1,0:T(1,128)} %param.27) | copy-start | bytes 49156
  11.8 7.4 %copy-start.10 = (f32[24,3,1,1]{0,1,3,2:T(4,128)S(1)}, f32[24,3,1,1]{0,1,3,2:T(4,128)}, u32[]{:S(2)}) copy-start(f32[24,3,1,1]{0,1,3,2:T(4,128)} %constant.217) | copy-start | bytes 868
  11.8 9.1 %copy-start.3 = (s32[16,1,128]{2,1,0:T(1,128)S(1)}, s32[16,1,128]{2,1,0:T(1,128)}, u32[]{:S(2)}) copy-start(s32[16,1,128]{2,1,0:T(1,128)} %param.26) | copy-start | bytes 24580
  11.8 12.1 %copy-start.9 = (f32[24,3,1,1]{0,1,3,2:T(4,128)S(1)}, f32[24,3,1,1]{0,1,3,2:T(4,128)}, u32[]{:S(2)}) copy-start(f32[24,3,1,1]{0,1,3,2:T(4,128)} %constant.220) | copy-start | bytes 868
  11.8 30.5 %all-to-all-start = ((f32[3,32,128]{2,0,1:T(4,128)}), f32[3,32,128]{2,0,1:T(4,128)S(1)}, u32[]{:S(2)}, u32[]{:S(2)}) async-start(f32[3,32,128]{2,0,1:T(4,128)} %bitcast.37), calls=%async_computation | async-start | bytes 131072 | tf_op jit(solution)/shard_map/all_to_all | solution.py:238
  17.7 9.8 %copy-start.8 = (f32[24,3,1,1]{0,1,3,2:T(4,128)S(1)}, f32[24,3,1,1]{0,1,3,2:T(4,128)}, u32[]{:S(2)}) copy-start(f32[24,3,1,1]{0,1,3,2:T(4,128)} %constant.221) | copy-start | bytes 868
  18.8 9.5 %copy-start.7 = (f32[24,3,1,1]{0,1,3,2:T(4,128)S(1)}, f32[24,3,1,1]{0,1,3,2:T(4,128)}, u32[]{:S(2)}) copy-start(f32[24,3,1,1]{0,1,3,2:T(4,128)} %constant.219) | copy-start | bytes 868
  20.0 9.3 %copy-start.6 = (f32[24,3,1,1]{0,1,3,2:T(4,128)S(1)}, f32[24,3,1,1]{0,1,3,2:T(4,128)}, u32[]{:S(2)}) copy-start(f32[24,3,1,1]{0,1,3,2:T(4,128)} %constant.223) | copy-start | bytes 868
  21.6 8.6 %copy-start.5 = (f32[24,3,1,1]{0,1,3,2:T(4,128)S(1)}, f32[24,3,1,1]{0,1,3,2:T(4,128)}, u32[]{:S(2)}) copy-start(f32[24,3,1,1]{0,1,3,2:T(4,128)} %constant.222) | copy-start | bytes 868
  21.6 5.7 %collective-permute-start.1 = (f32[3,9,1,128]{3,0,2,1:T(4,128)S(1)}, f32[3,9,1,128]{3,0,2,1:T(4,128)S(1)}, u32[]{:S(2)}, u32[]{:S(2)}) collective-permute-start(f32[3,9,1,128]{3,0,2,1:T(4,128)S(1)} %slice.275), channel_id=1, source_target_pairs={{1,0},{2,1},{3,2},{4,3},{5,4},{6,5},{7,6},{9,8},{10,9},{11,10},{12... | collective-permute-start | bytes 41480 | tf_op jit(solution)/shard_map/ppermute | solution.py:47
  24.7 6.4 %copy-start.4 = (f32[24,3,1,1]{0,1,3,2:T(4,128)S(1)}, f32[24,3,1,1]{0,1,3,2:T(4,128)}, u32[]{:S(2)}) copy-start(f32[24,3,1,1]{0,1,3,2:T(4,128)} %constant.218) | copy-start | bytes 868
  33.4 6.9 %collective-permute-start.2 = (f32[4,9,1,128]{3,2,1,0:T(1,128)S(1)}, f32[4,9,1,128]{3,2,1,0:T(1,128)S(1)}, u32[]{:S(2)}, u32[]{:S(2)}) collective-permute-start(f32[4,9,1,128]{3,2,1,0:T(1,128)S(1)} %pad_maximum_fusion.1), channel_id=1, source_target_pairs={{0,1},{1,2},{2,3},{3,4},{4,5},{5,6},{6,7},{8,9},{9,10},{10,11},{11... | collective-permute-start | bytes 55304 | tf_op jit(solution)/shard_map/ppermute | solution.py:47
  40.4 42.4 %collective-permute-start.3 = (f32[4,1,8,128]{3,2,1,0:T(8,128)S(1)}, f32[4,1,8,128]{3,2,1,0:T(8,128)S(1)}, u32[]{:S(2)}, u32[]{:S(2)}) collective-permute-start(f32[4,1,8,128]{3,2,1,0:T(8,128)S(1)} %slice.298), channel_id=1, source_target_pairs={{0,8},{8,16},{16,24},{24,32},{32,40},{40,48},{48,56},{56,64},{64,7... | collective-permute-start | bytes 49160 | tf_op jit(solution)/shard_map/ppermute | solution.py:47
  42.3 16.3 %copy-start.12 = (f32[16,1]{0,1:T(1,128)S(1)}, f32[16,1]{0,1:T(1,128)}, u32[]{:S(2)}) copy-start(f32[16,1]{0,1:T(1,128)} %param.28) | copy-start | bytes 196
  58.8 30.3 %copy-start.13 = (f32[3,8,8,128]{3,2,1,0:T(8,128)S(1)}, f32[3,8,8,128]{3,2,1,0:T(8,128)}, u32[]{:S(2)}) copy-start(f32[3,8,8,128]{3,2,1,0:T(8,128)} %param.20) | copy-start | bytes 294916
  58.8 30.3 %copy-start.14 = (f32[3,8,8,128]{3,2,1,0:T(8,128)S(1)}, f32[3,8,8,128]{3,2,1,0:T(8,128)}, u32[]{:S(2)}) copy-start(f32[3,8,8,128]{3,2,1,0:T(8,128)} %param.21) | copy-start | bytes 294916
  75.8 13.2 %all-to-all-start.2 = ((f32[16,2,3,1,128]{4,1,2,3,0:T(2,128)}), f32[16,2,3,1,128]{4,1,2,3,0:T(2,128)S(1)}, u32[]{:S(2)}, u32[]{:S(2)}) async-start(f32[16,2,3,1,128]{4,1,2,3,0:T(2,128)} %copy.92), calls=%async_computation.2 | async-start | bytes 98304 | tf_op jit(solution)/shard_map/all_to_all | solution.py:34
where the time goes:
time: 94.7 us; the launch traced here: 93 us
  matrix products  40.7 us (43%)
  starting transfers between devices  23.7 us (25%)
  waiting for transfers between devices  12.7 us (13%)
  blocking collectives  5.05 us (5%)
  other arithmetic  4.84 us (5%)
  local copies, waits for them, and re-layouts  4.52 us (5%)
  between operations  1.31 us (1%)
    dot_general x4, matrix products, pick_single(): return jnp.dot(places, onehot.T, precision=lax.Precision.HIGHEST)  15.4 us
    dot_general x4, matrix products, place_single(): jnp.dot(stretch_values, onehot, precision=lax.Precision.HIGHEST)  11.1 us
    ppermute x4, starting transfers between devices, from_behind(): return lax.ppermute(shard, axis, pairs)  11 us
    dot_general x8, matrix products, own_forces(): jnp.einsum('ij,jxyz->ixyz', table[:, 3 * corner:3 * corner + 3], local, p...  6.98 us
    all_to_all x1, starting transfers between devices, moved_by_axis(): lax.all_to_all(parts, axes[k], split_axis=k, concat_axis=k, tiled=True)  6.95 us
    ppermute x4, waiting for transfers between devices, from_behind(): return lax.ppermute(shard, axis, pairs)  6.49 us
    all_to_all x1, waiting for transfers between devices, moved_by_axis(): lax.all_to_all(parts, axes[k], split_axis=k, concat_axis=k, tiled=True)  6.22 us
    all_to_all x1, starting transfers between devices, shards(): lax.all_to_all(places.reshape(3, parts, -1), DOM, split_axis=1, concat_ax...  5.71 us
  transfers between devices with their start and end apart: 6, of which 3 were waited for; matrix products, arithmetic and copies ran while one was open for 49% of the time, Pallas kernels for 0%

commit v1 on v0

v1 whole, which is shorter than its diff:
```python
import jax
import jax.numpy as jnp
from jax import lax
from jax.experimental import pallas as pl
from jax.experimental.pallas import tpu as pltpu
from jax.sharding import Mesh
from jax.sharding import PartitionSpec as P

DOM = ("dom_0", "dom_1", "dom_2")
CLASS_VALUES = (1.0, 0.45, 0.12)
TIME_STEP = 0.25
DAMPING = 0.5
LAME = 0.3 / (1.3 * 0.4)
SHEAR = 0.5 / 1.3

F32 = jnp.float32
BF16 = jnp.bfloat16
LANES = 128
ROWS = 104
ROWS_PAD = 120


def sds(shape, dtype=F32):
    return jax.ShapeDtypeStruct(shape, dtype)


def split(value):
    high = value.astype(BF16)
    low = (value - high.astype(F32)).astype(BF16)
    return high, low


def iota(shape, axis):
    return lax.broadcasted_iota(jnp.int32, shape, axis)


def hat(lowest, along, count):
    where = iota((count, LANES), 0)
    return jnp.where(
        where == lowest, 1.0 - along, jnp.where(where == lowest + 1, along, 0.0)
    )


def planar_weights(element, along_r, along_p):
    weight_x = hat(element >> 10, along_r, 8)
    weight_y = hat((element >> 7) & 7, along_p, 8)
    return (weight_x[:, None, :] * weight_y[None]).reshape(64, LANES)


def interpolate_kernel(
    odd_ref, u_ref, element_ref, coords_ref, density_ref, class_ref,
    places_ref, high_ref, low_ref, modulus_ref, even_ref, odd_swap_ref,
):
    lane_block = iota((16, LANES), 1) >> 3
    pick = (lane_block == iota((16, LANES), 0)).astype(F32)
    kind = jnp.dot(
        jnp.broadcast_to(class_ref[...].astype(F32), (8, 16)), pick, preferred_element_type=F32
    )
    factor = jnp.zeros((8, LANES), F32)
    for index, value in enumerate(CLASS_VALUES):
        factor = factor + jnp.where(kind == float(index), value, 0.0)
    density = density_ref[...]
    modulus = factor[None] * density * density
    modulus_ref[...] = modulus
    odd = odd_ref[0, 0] != 0
    for comp in range(5):
        if comp < 3:
            first, last = u_ref[comp, 0], u_ref[comp, 7]
        else:
            source = modulus if comp == 3 else density
            first, last = source[0], source[7]
        even_ref[comp] = jnp.where(odd, first, last)
        odd_swap_ref[comp] = jnp.where(odd, last, first)

    field_high, field_low = split(u_ref[...].reshape(192, LANES))
    field = jnp.concatenate([field_high, field_low], axis=1)
    for pair in range(16):
        highs, lows = [], []
        for half in range(2):
            owner = 2 * pair + half
            element = element_ref[pl.ds(owner, 1), :]
            weight_z = hat(element & 127, coords_ref[2, pl.ds(owner, 1), :], LANES)
            high, low = split(weight_z)
            high_ref[owner] = high
            low_ref[owner] = low
            highs.append(high)
            lows.append(low)
        high = jnp.concatenate(highs, axis=1)
        low = jnp.concatenate(lows, axis=1)
        sums = jnp.dot(
            field, jnp.concatenate([high, high], axis=0), preferred_element_type=F32
        ) + jnp.dot(field_high, low, preferred_element_type=F32)
        for half in range(2):
            owner = 2 * pair + half
            planar = planar_weights(
                element_ref[pl.ds(owner, 1), :],
                coords_ref[0, pl.ds(owner, 1), :],
                coords_ref[1, pl.ds(owner, 1), :],
            )
            for comp in range(3):
                part = sums[64 * comp : 64 * comp + 64, LANES * half : LANES * half + LANES]
                places_ref[pl.ds(4 * owner + comp, 1), :] = jnp.sum(
                    part * planar, axis=0, keepdims=True
                )
            places_ref[pl.ds(4 * owner + 3, 1), :] = jnp.zeros((1, LANES), F32)


def fibre_tables_kernel(slots_ref, angles_ref, direction_ref, fibre_ref, node_ref):
    azimuth, elevation = angles_ref[0], angles_ref[1]
    flat = jnp.cos(elevation)
    direction_ref[0] = jnp.cos(azimuth) * flat
    direction_ref[1] = jnp.sin(azimuth) * flat
    direction_ref[2] = jnp.sin(elevation)
    lefts, rights = [], []
    nodes = iota((1, LANES), 1).astype(F32)
    for fibre in range(16):
        slots = slots_ref[pl.ds(fibre, 1), :]
        host = iota((32, LANES), 0) == (slots >> 7)
        lefts.append(
            jnp.concatenate(
                [jnp.where(host, float(fibre + 1), 0.0), jnp.where(host, nodes, 0.0)], axis=0
            ).astype(BF16)
        )
        rights.append((iota((LANES, LANES), 0) == (slots & 127)).astype(F32).astype(BF16))
    table = lax.dot_general(
        jnp.concatenate(lefts, axis=1),
        jnp.concatenate(rights, axis=1),
        (((1,), (1,)), ((), ())),
        preferred_element_type=F32,
    )
    table = table.astype(jnp.int32)
    fibre_ref[...] = table[:32]
    node_ref[...] = table[32:]


def lane_pick(row, index):
    return jnp.take_along_axis(jnp.broadcast_to(row, index.shape), index, axis=1)


def fibre_kernel(
    places_ref, slots_ref, direction_ref, stiffness_ref, fibre_ref, node_ref, pulls_ref
):
    slots = slots_ref[...]
    host, spot = slots >> 7, slots & 127
    places = [jnp.zeros(slots.shape, F32) for _ in range(3)]
    for step in range(32):
        here = host == step
        for comp in range(3):
            picked = lane_pick(places_ref[pl.ds(4 * step + comp, 1), :], spot)
            places[comp] = jnp.where(here, picked, places[comp])
    strain = jnp.zeros(slots.shape, F32)
    for comp in range(3):
        ahead = pltpu.roll(places[comp], LANES - 1, 1)
        strain = strain + direction_ref[comp] * (ahead - places[comp])
    live = iota(slots.shape, 1) < LANES - 1
    tension = jnp.where(live, stiffness_ref[...] * jnp.maximum(strain, 0.0), 0.0)
    forces = []
    for comp in range(3):
        pull = tension * direction_ref[comp]
        forces.append(pull - pltpu.roll(pull, 1, 1))
    for block in range(4):
        fibre = fibre_ref[pl.ds(8 * block, 8), :]
        node = node_ref[pl.ds(8 * block, 8), :]
        placed = [jnp.zeros((8, LANES), F32) for _ in range(3)]
        for step in range(16):
            here = fibre == step + 1
            for comp in range(3):
                picked = lane_pick(forces[comp][step : step + 1], node)
                placed[comp] = jnp.where(here, picked, placed[comp])
        for comp in range(3):
            pulls_ref[pl.ds(32 * block + comp, 8, stride=4), :] = placed[comp]
        pulls_ref[pl.ds(32 * block + 3, 8, stride=4), :] = jnp.zeros((8, LANES), F32)


def side_rows_kernel(
    odd_ref, u_ref, density_ref, modulus_ref, even_in_ref, odd_in_ref, even_ref, odd_swap_ref
):
    odd_dom = odd_ref[0, 0] != 0
    odd_blk = odd_ref[0, 1] != 0
    for comp in range(5):
        lower = jnp.where(odd_dom, even_in_ref[comp], odd_in_ref[comp])
        upper = jnp.where(odd_dom, odd_in_ref[comp], even_in_ref[comp])
        rows = []
        for at in (0, 7):
            if comp < 3:
                own = u_ref[comp, :, at, :]
            else:
                own = (modulus_ref if comp == 3 else density_ref)[:, at, :]
            rows.append(
                jnp.concatenate([lower[at : at + 1], own, upper[at : at + 1]], axis=0)
            )
        first, last = rows
        even_ref[pl.ds(10 * comp, 10), :] = jnp.where(odd_blk, first, last)
        odd_swap_ref[pl.ds(10 * comp, 10), :] = jnp.where(odd_blk, last, first)


def elastic_kernel(
    odd_ref, u_ref, velocity_ref, load_ref, density_ref, modulus_ref,
    even_x_ref, odd_x_ref, even_y_ref, odd_y_ref,
    velocity_out_ref, displacement_out_ref, inverse_mass_ref,
    nodes_ref, depth_ref, corner_ref,
):
    odd_dom = odd_ref[0, 0] != 0
    odd_blk = odd_ref[0, 1] != 0
    for comp in range(5):
        nodes_ref[comp, pl.ds(96, 24), :] = jnp.zeros((24, LANES), F32)
        lower = jnp.where(odd_dom, even_x_ref[comp], odd_x_ref[comp])
        upper = jnp.where(odd_dom, odd_x_ref[comp], even_x_ref[comp])
        nodes_ref[comp, pl.ds(1, 8), :] = lower
        nodes_ref[comp, pl.ds(91, 8), :] = upper
        for x in range(8):
            if comp < 3:
                own = u_ref[comp, x]
            else:
                own = (modulus_ref if comp == 3 else density_ref)[x]
            nodes_ref[comp, pl.ds(10 * x + 11, 8), :] = own
        even = even_y_ref[pl.ds(10 * comp, 10), :]
        odd = odd_y_ref[pl.ds(10 * comp, 10), :]
        left = jnp.where(odd_blk, even, odd)
        right = jnp.where(odd_blk, odd, even)
        for x in range(10):
            nodes_ref[comp, pl.ds(10 * x, 1), :] = left[x : x + 1]
            nodes_ref[comp, pl.ds(10 * x + 9, 1), :] = right[x : x + 1]
    last_lane = iota((8, LANES), 1) == LANES - 1
    first_lane = iota((8, LANES), 1) == 0
    for comp in range(3):
        for chunk in range(ROWS_PAD // 8):
            here = nodes_ref[comp, pl.ds(8 * chunk, 8), :]
            above = jnp.where(last_lane, 0.0, pltpu.roll(here, LANES - 1, 1))
            depth_ref[2 * comp, pl.ds(8 * chunk, 8), :] = above + here
            depth_ref[2 * comp + 1, pl.ds(8 * chunk, 8), :] = above - here

    long, cross, shear = (LAME + 2 * SHEAR) / 16, LAME / 16, SHEAR / 16
    long3, cross3, shear3 = (LAME + 3 * SHEAR) / 48, LAME / 48, SHEAR / 48
    long9 = (LAME + 4 * SHEAR) / 144
    for chunk in range(ROWS // 8):
        at = 8 * chunk
        mode = {}
        for comp in range(3):
            for c in range(2):
                a00 = depth_ref[2 * comp + c, pl.ds(at, 8), :]
                a01 = depth_ref[2 * comp + c, pl.ds(at + 1, 8), :]
                a10 = depth_ref[2 * comp + c, pl.ds(at + 10, 8), :]
                a11 = depth_ref[2 * comp + c, pl.ds(at + 11, 8), :]
                s0, d0, s1, d1 = a00 + a01, a01 - a00, a10 + a11, a11 - a10
                mode[comp, 0, 0, c] = s0 + s1
                mode[comp, 0, 1, c] = d0 + d1
                mode[comp, 1, 0, c] = s1 - s0
                mode[comp, 1, 1, c] = d1 - d0
        scale = nodes_ref[3, pl.ds(at, 8), :]
        u100, v010, w001 = mode[0, 1, 0, 0], mode[1, 0, 1, 0], mode[2, 0, 0, 1]
        trace = cross * (u100 + v010 + w001)
        f = {}
        f[0, 1, 0, 0] = (long - cross) * u100 + trace
        f[1, 0, 1, 0] = (long - cross) * v010 + trace
        f[2, 0, 0, 1] = (long - cross) * w001 + trace
        f[0, 0, 1, 0] = f[1, 1, 0, 0] = shear * (mode[0, 0, 1, 0] + mode[1, 1, 0, 0])
        f[0, 0, 0, 1] = f[2, 1, 0, 0] = shear * (mode[0, 0, 0, 1] + mode[2, 1, 0, 0])
        f[1, 0, 0, 1] = f[2, 0, 1, 0] = shear * (mode[1, 0, 0, 1] + mode[2, 0, 1, 0])
        for one, two in (
            ((0, 1, 1, 0), (2, 0, 1, 1)),
            ((0, 1, 0, 1), (1, 0, 1, 1)),
            ((1, 1, 1, 0), (2, 1, 0, 1)),
        ):
            f[one] = long3 * mode[one] + cross3 * mode[two]
            f[two] = long3 * mode[two] + cross3 * mode[one]
        twist = mode[0, 0, 1, 1] + mode[1, 1, 0, 1] + mode[2, 1, 1, 0]
        for key in ((0, 0, 1, 1), (1, 1, 0, 1), (2, 1, 1, 0)):
            f[key] = shear3 * (twist + mode[key])
        for comp in range(3):
            f[comp, 1, 1, 1] = long9 * mode[comp, 1, 1, 1]
        f = {key: value * scale for key, value in f.items()}
        for comp in range(3):
            for c in range(2):
                m01, m10, m11 = f[comp, 0, 1, c], f[comp, 1, 0, c], f[comp, 1, 1, c]
                total, other = m10 + m01, m10 - m01
                corners = (m11 - total, -m11 - other, other - m11, total + m11)
                if c == 1:
                    m00 = f[comp, 0, 0, 1]
                    corners = tuple(corner + m00 for corner in corners)
                for which in range(4):
                    corner_ref[8 * comp + 4 * c + which, pl.ds(at + 16, 8), :] = corners[which]

    shifts = (0, 1, 10, 11)
    for x in range(8):
        at = 10 * x + 11
        weight = sum(nodes_ref[4, pl.ds(at - shift, 8), :] for shift in shifts)
        below = jnp.where(first_lane, 0.0, pltpu.roll(weight, 1, 1))
        inverse = 1.0 / (0.125 * (weight + below))
        inverse_mass_ref[x] = inverse
        for comp in range(3):
            h0, h1 = (
                sum(
                    corner_ref[8 * comp + 4 * c + which, pl.ds(at + 16 - shift, 8), :]
                    for which, shift in enumerate(shifts)
                )
                for c in range(2)
            )
            below = jnp.where(first_lane, 0.0, pltpu.roll(h0 + h1, 1, 1))
            elastic = h0 - h1 + below
            velocity = velocity_ref[comp, x]
            acceleration = (load_ref[comp, x] - elastic) * inverse - DAMPING * velocity
            velocity = velocity + TIME_STEP * acceleration
            velocity_out_ref[comp, x] = velocity
            displacement_out_ref[comp, x] = u_ref[comp, x] + TIME_STEP * velocity


def spread_kernel(
    pulls_ref, element_ref, coords_ref, high_ref, low_ref,
    velocity_ref, displacement_ref, inverse_mass_ref,
    displacement_out_ref, velocity_out_ref,
):
    total = jnp.zeros((384, 256), F32)
    for pair in range(16):
        highs, lows, weights = [], [], []
        for half in range(2):
            owner = 2 * pair + half
            planar = planar_weights(
                element_ref[pl.ds(owner, 1), :],
                coords_ref[0, pl.ds(owner, 1), :],
                coords_ref[1, pl.ds(owner, 1), :],
            )
            terms = jnp.concatenate(
                [planar * pulls_ref[pl.ds(4 * owner + comp, 1), :] for comp in range(3)], axis=0
            )
            high, low = split(terms)
            highs.append(high)
            lows.append(low)
            weights.append(jnp.concatenate([high_ref[owner], low_ref[owner]], axis=0))
        left = jnp.concatenate(
            [jnp.concatenate(highs, axis=1), jnp.concatenate(lows, axis=1)], axis=0
        )
        total = total + lax.dot_general(
            left,
            jnp.concatenate(weights, axis=1),
            (((1,), (1,)), ((), ())),
            preferred_element_type=F32,
        )
    fibre = (total[:192, :LANES] + total[192:, :LANES]) + (
        total[:192, LANES:] + total[192:, LANES:]
    )
    for comp in range(3):
        for x in range(8):
            row = 64 * comp + 8 * x
            change = TIME_STEP * (fibre[row : row + 8] * inverse_mass_ref[x])
            velocity_out_ref[comp, x] = velocity_ref[comp, x] + change
            displacement_out_ref[comp, x] = displacement_ref[comp, x] + TIME_STEP * change


def call(kernel, outs, scratch=(), scalars=0, inputs=0):
    specs = [pl.BlockSpec(memory_space=pltpu.SMEM)] * scalars
    specs += [pl.BlockSpec(memory_space=pltpu.VMEM)] * inputs
    many = isinstance(outs, (tuple, list))
    vmem = pl.BlockSpec(memory_space=pltpu.VMEM)
    return pl.pallas_call(
        kernel,
        out_shape=outs,
        in_specs=specs,
        out_specs=type(outs)(vmem for _ in outs) if many else vmem,
        scratch_shapes=scratch,
    )


def swap(shard, axis, first):
    size = lax.axis_size(axis)
    pairs = [(i, i + 1) for i in range(first, size - 1, 2)]
    return lax.ppermute(shard, axis, pairs + [(b, a) for a, b in pairs])


def exchange(rows):
    blocks = rows.reshape(32, 4, LANES)
    return lax.all_to_all(blocks, DOM, split_axis=0, concat_axis=0, tiled=True).reshape(
        128, LANES
    )


def shards(
    displacement, velocity, load, density, block_class,
    host_element, host_coords, fibre_slot, fibre_angles, fibre_stiffness,
):
    odd = jnp.stack([lax.axis_index(DOM) % 2, lax.axis_index("blk") % 2]).reshape(1, 2)
    odd = odd.astype(jnp.int32)
    element = host_element.reshape(32, LANES)
    coords = host_coords.reshape(3, 32, LANES)
    slots = fibre_slot.reshape(16, LANES)
    grid = (3, 8, 8, LANES)
    weights = sds((32, LANES, LANES), BF16)
    places, high, low, modulus, even_x, odd_x = call(
        interpolate_kernel,
        (
            sds((128, LANES)), weights, weights, sds((8, 8, LANES)),
            sds((5, 8, LANES)), sds((5, 8, LANES)),
        ),
        scalars=1, inputs=5,
    )(odd, displacement, element, coords, density, block_class.reshape(1, 16))
    received = exchange(places)
    even_x = swap(even_x, DOM, 0)
    odd_x = swap(odd_x, DOM, 1)
    direction, fibre, node = call(
        fibre_tables_kernel,
        (sds((3, 16, LANES)), sds((32, LANES), jnp.int32), sds((32, LANES), jnp.int32)),
        inputs=2,
    )(slots, fibre_angles.reshape(2, 16, LANES))
    even_y, odd_y = call(
        side_rows_kernel, (sds((50, LANES)), sds((50, LANES))), scalars=1, inputs=5
    )(odd, displacement, density, modulus, even_x, odd_x)
    even_y = swap(even_y, "blk", 0)
    odd_y = swap(odd_y, "blk", 1)
    pulls = call(fibre_kernel, sds((128, LANES)), inputs=6)(
        received, slots, direction, fibre_stiffness.reshape(16, 1), fibre, node
    )
    returned = exchange(pulls)
    step_velocity, step_displacement, inverse_mass = call(
        elastic_kernel,
        (sds(grid), sds(grid), sds((8, 8, LANES))),
        scratch=(
            pltpu.VMEM((5, ROWS_PAD, LANES), F32),
            pltpu.VMEM((6, ROWS_PAD, LANES), F32),
            pltpu.VMEM((24, ROWS_PAD, LANES), F32),
        ),
        scalars=1, inputs=9,
    )(odd, displacement, velocity, load, density, modulus, even_x, odd_x, even_y, odd_y)
    return call(spread_kernel, (sds(grid), sds(grid)), inputs=8)(
        returned, element, coords, high, low, step_velocity, step_displacement, inverse_mass
    )


def solution(mesh):
    finer = Mesh(
        mesh.devices.reshape(4, 4, 2, mesh.shape["blk"]), ("dom_0", "dom_1", "dom_2", "blk")
    )
    in_specs = (
        P(None, DOM, "blk", None),
        P(None, DOM, "blk", None),
        P(None, DOM, "blk", None),
        P(DOM, "blk", None),
        P(DOM, "blk", None),
        P("blk", DOM),
        P(None, "blk", DOM),
        P(DOM, "blk", None),
        P(None, DOM, "blk", None),
        P(DOM, "blk"),
    )
    out_specs = (P(None, DOM, "blk", None), P(None, DOM, "blk", None))
    return jax.shard_map(
        shards, mesh=finer, in_specs=in_specs, out_specs=out_specs, check_vma=False
    )
```

time: 94.7 us -> 51.8 us (0.55); the launches traced: 93 us -> 51.3 us
  matrix products: 40.7 us -> 0 us
  Pallas kernels: 0 us -> 14.5 us
  blocking collectives: 5.05 us -> 0 us
  other arithmetic: 4.84 us -> 0.59 us
  starting transfers between devices: 23.7 us -> 20.5 us
  local copies, waits for them, and re-layouts: 4.52 us -> 3.16 us
    dot_general x18 -> x0, matrix products: 40.7 us -> none  [the longest x4 15.4 us: pick_single(): return jnp.dot(places, onehot.T, precision=lax.Precision.HIGHEST)]
    pallas_call x0 -> x6, Pallas kernels: none -> 14.5 us  [the longest x1 3.37 us: shards(): call(interpolate_kernel, (sds((128, LANES)), weights, weights, sds((8, 8,...]
    all_to_all x1 -> x0, blocking collectives: 5.05 us -> none  [moved_by_axis(): lax.all_to_all(parts, axes[k], split_axis=k, concat_axis=k, tiled=True)]
    ppermute x4, starting transfers between devices: 11 us -> 7.68 us  [swap(): return lax.ppermute(shard, axis, pairs + [(b, a) for a, b in pairs])]
    unnamed x38 -> x19, local copies, waits for them, and re-layouts: 0.86 us -> 3.16 us
    all_to_all x2, waiting for transfers between devices: 6.22 us -> 3.97 us  [exchange(): lax.all_to_all(blocks, DOM, split_axis=0, concat_axis=0, tiled=True)]
    slice x12 -> x0, local copies, waits for them, and re-layouts: 1.92 us -> none  [the longest x1 0.77 us: shards(): top_row = from_behind(displacement[:, :1], DOM, -1)]
    ppermute x4, waiting for transfers between devices: 6.49 us -> 7.88 us  [swap(): return lax.ppermute(shard, axis, pairs + [(b, a) for a, b in pairs])]
  transfers between devices with their start and end apart: 6 -> 6, of which waited for: 3 -> 4; matrix products, arithmetic and copies ran while one was open for 49% -> 1% of each run, Pallas kernels for 0% -> 11%
where the time goes in v1:
time: 51.8 us; the launch traced here: 51.3 us
  starting transfers between devices  20.5 us (40%)
  Pallas kernels  14.5 us (28%)
  waiting for transfers between devices  11.9 us (23%)
  local copies, waits for them, and re-layouts  3.16 us (6%)
  between operations  0.73 us (1%)
  other arithmetic  0.59 us (1%)
    all_to_all x2, starting transfers between devices, exchange(): lax.all_to_all(blocks, DOM, split_axis=0, concat_axis=0, tiled=True)  12.8 us
    ppermute x4, waiting for transfers between devices, swap(): return lax.ppermute(shard, axis, pairs + [(b, a) for a, b in pairs])  7.88 us
    ppermute x4, starting transfers between devices, swap(): return lax.ppermute(shard, axis, pairs + [(b, a) for a, b in pairs])  7.68 us
    all_to_all x2, waiting for transfers between devices, exchange(): lax.all_to_all(blocks, DOM, split_axis=0, concat_axis=0, tiled=True)  3.97 us
    pallas_call x1, Pallas kernels, shards(): call(interpolate_kernel, (sds((128, LANES)), weights, weights, sds((8, 8,...  3.37 us
    pallas_call x1, Pallas kernels, shards(): call(spread_kernel, (sds(grid), sds(grid)), inputs=8)  3.36 us
    unnamed x19, local copies, waits for them, and re-layouts  3.16 us
    pallas_call x1, Pallas kernels, shards(): call(elastic_kernel, (sds(grid), sds(grid), sds((8, 8, LANES))), scratch=...  2.33 us
  transfers between devices with their start and end apart: 6, of which 4 were waited for; matrix products, arithmetic and copies ran while one was open for 1% of the time, Pallas kernels for 11%

profile of v1, /device:TPU:136, one launch (start us, length us, event | category | flops | bytes accessed | tf_op | source)
XLA Modules:
  0.0 51.3 jit_solution(16033067464717073902)
XLA Ops:
  0.7 0.6 %add_bitcast_fusion.odd_ref = s32[1,2]{1,0:T(1,128)} fusion(s32[1]{0:T(128)} %bitcast.1, s32[1]{0:T(128)} %bitcast), kind=kLoop, calls=%fused_computation | loop fusion | flops 2 | bytes 16 | tf_op jit(solution)/shard_map/reshape | solution.py:381
  1.2 3.4 %shard_map.113 = (f32[128,128]{1,0:T(8,128)}, bf16[32,128,128]{2,1,0:T(8,128)(2,1)}, bf16[32,128,128]{2,1,0:T(8,128)(2,1)}, f32[8,8,128]{2,1,0:T(8,128)}, f32[5,8,128]{2,1,0:T(8,128)}, /*index=5*/f32[5,8,128]{2,1,0:T(8,128)}) custom-call(s32[1,2]{1,0:T(1,128)} %add_bitcast_fusion.odd_ref, f32[3,8,8,128]{3,2,1,0:T(8,128)} %u_ref.5, s32[32,128]{1,0:T(8,128)} %bitcast.18, ...), custom_call_target="tpu_custom_call" | custom-call | tf_op jit(solution)/shard_map/pallas_call | solution.py:388
  4.6 7.7 %all-to-all-start = ((f32[32,4,128]{2,1,0:T(4,128)}), f32[32,4,128]{2,1,0:T(4,128)S(1)}, u32[]{:S(2)}, u32[]{:S(2)}) async-start(f32[32,4,128]{2,1,0:T(4,128)} %bitcast.20), calls=%async_computation | async-start | bytes 131072 | tf_op jit(solution)/shard_map/all_to_all | solution.py:372
  12.3 0.7 %copy.12.stiffness_ref = f32[16,1]{1,0:T(8,128)} copy(f32[16,1]{0,1:T(1,128)S(1)} %copy-done.6) | data formatting | bytes 128 | tf_op args[9]
  13.0 1.6 %shard_map.114 = (f32[3,16,128]{2,1,0:T(8,128)}, s32[32,128]{1,0:T(8,128)}, s32[32,128]{1,0:T(8,128)}) custom-call(s32[16,128]{1,0:T(8,128)} %bitcast.21, f32[2,16,128]{2,1,0:T(8,128)} %bitcast.23), custom_call_target="tpu_custom_call" | custom-call | tf_op jit(solution)/shard_map/pallas_call | solution.py:399
  14.6 4.0 %all-to-all-done = f32[32,4,128]{2,1,0:T(4,128)S(1)} async-done(((f32[32,4,128]{2,1,0:T(4,128)}), f32[32,4,128]{2,1,0:T(4,128)S(1)}, u32[]{:S(2)}, u32[]{:S(2)}) %all-to-all-start) | async-done | bytes 65568 | tf_op jit(solution)/shard_map/all_to_all | solution.py:372
  18.6 0.6 %copy-done.1 = f32[32,4,128]{2,1,0:T(4,128)} copy-done((f32[32,4,128]{2,1,0:T(4,128)}, f32[32,4,128]{2,1,0:T(4,128)S(1)}, u32[]{:S(2)}) %copy-start.1) | copy-done | bytes 65560
  19.2 2.2 %shard_map.115 = f32[128,128]{1,0:T(8,128)} custom-call(f32[128,128]{1,0:T(8,128)} %bitcast.15, s32[16,128]{1,0:T(8,128)} %bitcast.22, f32[3,16,128]{2,1,0:T(8,128)} %get-tuple-element.17.direction_ref, f32[16,1]{1,0:T(8,128)} %copy.12.stiffness_ref, s32[32,128]{1,0:T(8,128)} %get-tuple-element.18.fibre_ref, s32[32,128]{1,0:T(8,128)} %get-tuple-element.19.node_ref), custom_call_target="tpu_custom_call" | custom-call | tf_op jit(solution)/shard_map/pallas_call | solution.py:409
  21.5 5.1 %all-to-all-start.1 = ((f32[32,4,128]{2,1,0:T(4,128)}), f32[32,4,128]{2,1,0:T(4,128)S(1)}, u32[]{:S(2)}, u32[]{:S(2)}) async-start(f32[32,4,128]{2,1,0:T(4,128)} %bitcast.14), calls=%async_computation.1 | async-start | bytes 131072 | tf_op jit(solution)/shard_map/all_to_all | solution.py:372
  26.6 0.2 collective-permute-start
  26.8 4.5 %collective-permute-start.1 = (f32[5,8,128]{2,1,0:T(8,128)S(1)}, f32[5,8,128]{2,1,0:T(8,128)S(1)}, u32[]{:S(2)}, u32[]{:S(2)}) collective-permute-start(f32[5,8,128]{2,1,0:T(8,128)S(1)} %copy-done.7), channel_id=1, source_target_pairs={{8,16},{24,32},{40,48},{56,64},{72,80},{88,96},{104,112},{120,128}... | collective-permute-start | bytes 61448 | tf_op jit(solution)/shard_map/ppermute | solution.py:367
  31.3 0.0 collective-permute-done.even_in_ref.even_x_ref
  31.4 2.6 %collective-permute-done.1.odd_in_ref.odd_x_ref = f32[5,8,128]{2,1,0:T(8,128)S(1)} collective-permute-done((f32[5,8,128]{2,1,0:T(8,128)S(1)}, f32[5,8,128]{2,1,0:T(8,128)S(1)}, u32[]{:S(2)}, u32[]{:S(2)}) %collective-permute-start.1) | collective-permute-done | bytes 20512 | tf_op jit(solution)/shard_map/ppermute | solution.py:367
  34.0 0.6 %copy-done.3 = f32[5,8,128]{2,1,0:T(8,128)} copy-done((f32[5,8,128]{2,1,0:T(8,128)}, f32[5,8,128]{2,1,0:T(8,128)S(1)}, u32[]{:S(2)}) %copy-start.3) | copy-done | bytes 20504
  34.6 1.6 %shard_map.116 = (f32[50,128]{1,0:T(8,128)}, f32[50,128]{1,0:T(8,128)}) custom-call(s32[1,2]{1,0:T(1,128)} %add_bitcast_fusion.odd_ref, f32[3,8,8,128]{3,2,1,0:T(8,128)} %u_ref.5, f32[8,8,128]{2,1,0:T(8,128)} %density_ref.5, f32[8,8,128]{2,1,0:T(8,128)} %get-tuple-element.22.modulus_ref, f32[5,8,128]{2,1,0:T(8,128)} %copy-done.2, f32[5,8,128]{2,1,0:T(8,128)} %copy-done.3), custom_call_target="tpu_custom_call" | custom-call | tf_op jit(solution)/shard_map/pallas_call | solution.py:404
  36.2 1.0 %collective-permute-start.2 = (f32[50,128]{1,0:T(8,128)}, f32[50,128]{1,0:T(8,128)S(1)}, u32[]{:S(2)}, u32[]{:S(2)}) collective-permute-start(f32[50,128]{1,0:T(8,128)} %get-tuple-element.25), channel_id=1, source_target_pairs={{0,1},{2,3},{4,5},{6,7},{1,0},{3,2},{5,4},{7,6},{8,9},{10,11},{12,... | collective-permute-start | bytes 76808 | tf_op jit(solution)/shard_map/ppermute | solution.py:367
  37.2 1.9 %collective-permute-start.3 = (f32[50,128]{1,0:T(8,128)}, f32[50,128]{1,0:T(8,128)S(1)}, u32[]{:S(2)}, u32[]{:S(2)}) collective-permute-start(f32[50,128]{1,0:T(8,128)} %get-tuple-element.26), channel_id=1, source_target_pairs={{1,2},{3,4},{5,6},{2,1},{4,3},{6,5},{9,10},{11,12},{13,14},{10,9},... | collective-permute-start | bytes 76808 | tf_op jit(solution)/shard_map/ppermute | solution.py:367
  39.1 1.2 %collective-permute-done.2.even_y_ref = f32[50,128]{1,0:T(8,128)S(1)} collective-permute-done((f32[50,128]{1,0:T(8,128)}, f32[50,128]{1,0:T(8,128)S(1)}, u32[]{:S(2)}, u32[]{:S(2)}) %collective-permute-start.2) | collective-permute-done | bytes 25632 | tf_op jit(solution)/shard_map/ppermute | solution.py:367
  40.3 4.1 %collective-permute-done.3.odd_y_ref = f32[50,128]{1,0:T(8,128)S(1)} collective-permute-done((f32[50,128]{1,0:T(8,128)}, f32[50,128]{1,0:T(8,128)S(1)}, u32[]{:S(2)}, u32[]{:S(2)}) %collective-permute-start.3) | collective-permute-done | bytes 25632 | tf_op jit(solution)/shard_map/ppermute | solution.py:367
  44.4 0.6 %copy-done.5 = f32[50,128]{1,0:T(8,128)} copy-done((f32[50,128]{1,0:T(8,128)}, f32[50,128]{1,0:T(8,128)S(1)}, u32[]{:S(2)}) %copy-start.5) | copy-done | bytes 25624
  45.0 2.3 %shard_map.117 = (f32[3,8,8,128]{3,2,1,0:T(8,128)}, f32[3,8,8,128]{3,2,1,0:T(8,128)}, f32[8,8,128]{2,1,0:T(8,128)}) custom-call(s32[1,2]{1,0:T(1,128)} %add_bitcast_fusion.odd_ref, f32[3,8,8,128]{3,2,1,0:T(8,128)} %u_ref.5, f32[3,8,8,128]{3,2,1,0:T(8,128)} %velocity_ref.1, f32[3,8,8,128]{3,2,1,0:T(8,128)} %load_ref.1, f32[8,8,128]{2,1,0:T(8,128)} %density_ref.5, ...), custom_call_target="tpu_custom_call" | custom-call | tf_op jit(solution)/shard_map/pallas_call | solution.py:413
  47.3 0.0 all-to-all-done.1
  47.3 0.6 %copy-done = f32[32,4,128]{2,1,0:T(4,128)} copy-done((f32[32,4,128]{2,1,0:T(4,128)}, f32[32,4,128]{2,1,0:T(4,128)S(1)}, u32[]{:S(2)}) %copy-start) | copy-done | bytes 65560
  48.0 3.4 %shard_map.118 = (f32[3,8,8,128]{3,2,1,0:T(8,128)}, f32[3,8,8,128]{3,2,1,0:T(8,128)}) custom-call(f32[128,128]{1,0:T(8,128)} %bitcast.13, s32[32,128]{1,0:T(8,128)} %bitcast.19, f32[3,32,128]{2,1,0:T(8,128)} %bitcast.17, bf16[32,128,128]{2,1,0:T(8,128)(2,1)} %get-tuple-element.20.high_ref, bf16[32,128,128]{2,1,0:T(8,128)(2,1)} %get-tuple-element.21.low_ref, ...), custom_call_target="tpu_custom_call" | custom-call | tf_op jit(solution)/shard_map/pallas_call | solution.py:423
  (14 shorter events, 0.0 us)
Async XLA Ops:
  4.6 7.7 %copy-start.6 = (f32[16,1]{0,1:T(1,128)S(1)}, f32[16,1]{0,1:T(1,128)}, u32[]{:S(2)}) copy-start(f32[16,1]{0,1:T(1,128)} %param.19) | copy-start | bytes 196
  4.6 14.0 %all-to-all-start = ((f32[32,4,128]{2,1,0:T(4,128)}), f32[32,4,128]{2,1,0:T(4,128)S(1)}, u32[]{:S(2)}, u32[]{:S(2)}) async-start(f32[32,4,128]{2,1,0:T(4,128)} %bitcast.20), calls=%async_computation | async-start | bytes 131072 | tf_op jit(solution)/shard_map/all_to_all | solution.py:372
  18.6 0.6 %copy-start.1 = (f32[32,4,128]{2,1,0:T(4,128)}, f32[32,4,128]{2,1,0:T(4,128)S(1)}, u32[]{:S(2)}) copy-start(f32[32,4,128]{2,1,0:T(4,128)S(1)} %all-to-all-done) | copy-start | bytes 196612
  21.5 5.1 %copy-start.8 = (f32[5,8,128]{2,1,0:T(8,128)S(1)}, f32[5,8,128]{2,1,0:T(8,128)}, u32[]{:S(2)}) copy-start(f32[5,8,128]{2,1,0:T(8,128)} %get-tuple-element.23) | copy-start | bytes 61444
  21.5 5.3 %copy-start.7 = (f32[5,8,128]{2,1,0:T(8,128)S(1)}, f32[5,8,128]{2,1,0:T(8,128)}, u32[]{:S(2)}) copy-start(f32[5,8,128]{2,1,0:T(8,128)} %get-tuple-element.24) | copy-start | bytes 61444
  21.5 25.9 %all-to-all-start.1 = ((f32[32,4,128]{2,1,0:T(4,128)}), f32[32,4,128]{2,1,0:T(4,128)S(1)}, u32[]{:S(2)}, u32[]{:S(2)}) async-start(f32[32,4,128]{2,1,0:T(4,128)} %bitcast.14), calls=%async_computation.1 | async-start | bytes 131072 | tf_op jit(solution)/shard_map/all_to_all | solution.py:372
  26.6 4.8 %collective-permute-start = (f32[5,8,128]{2,1,0:T(8,128)S(1)}, f32[5,8,128]{2,1,0:T(8,128)S(1)}, u32[]{:S(2)}, u32[]{:S(2)}) collective-permute-start(f32[5,8,128]{2,1,0:T(8,128)S(1)} %copy-done.8), channel_id=1, source_target_pairs={{0,8},{16,24},{32,40},{48,56},{64,72},{80,88},{96,104},{112,120},{... | collective-permute-start | bytes 61448 | tf_op jit(solution)/shard_map/ppermute | solution.py:367
  26.8 7.2 %collective-permute-start.1 = (f32[5,8,128]{2,1,0:T(8,128)S(1)}, f32[5,8,128]{2,1,0:T(8,128)S(1)}, u32[]{:S(2)}, u32[]{:S(2)}) collective-permute-start(f32[5,8,128]{2,1,0:T(8,128)S(1)} %copy-done.7), channel_id=1, source_target_pairs={{8,16},{24,32},{40,48},{56,64},{72,80},{88,96},{104,112},{120,128}... | collective-permute-start | bytes 61448 | tf_op jit(solution)/shard_map/ppermute | solution.py:367
  31.4 2.6 %copy-start.2 = (f32[5,8,128]{2,1,0:T(8,128)}, f32[5,8,128]{2,1,0:T(8,128)S(1)}, u32[]{:S(2)}) copy-start(f32[5,8,128]{2,1,0:T(8,128)S(1)} %collective-permute-done.even_in_ref.even_x_ref) | copy-start | bytes 61444
  34.0 0.6 %copy-start.3 = (f32[5,8,128]{2,1,0:T(8,128)}, f32[5,8,128]{2,1,0:T(8,128)S(1)}, u32[]{:S(2)}) copy-start(f32[5,8,128]{2,1,0:T(8,128)S(1)} %collective-permute-done.1.odd_in_ref.odd_x_ref) | copy-start | bytes 61444
  36.2 4.1 %collective-permute-start.2 = (f32[50,128]{1,0:T(8,128)}, f32[50,128]{1,0:T(8,128)S(1)}, u32[]{:S(2)}, u32[]{:S(2)}) collective-permute-start(f32[50,128]{1,0:T(8,128)} %get-tuple-element.25), channel_id=1, source_target_pairs={{0,1},{2,3},{4,5},{6,7},{1,0},{3,2},{5,4},{7,6},{8,9},{10,11},{12,... | collective-permute-start | bytes 76808 | tf_op jit(solution)/shard_map/ppermute | solution.py:367
  37.2 7.2 %collective-permute-start.3 = (f32[50,128]{1,0:T(8,128)}, f32[50,128]{1,0:T(8,128)S(1)}, u32[]{:S(2)}, u32[]{:S(2)}) collective-permute-start(f32[50,128]{1,0:T(8,128)} %get-tuple-element.26), channel_id=1, source_target_pairs={{1,2},{3,4},{5,6},{2,1},{4,3},{6,5},{9,10},{11,12},{13,14},{10,9},... | collective-permute-start | bytes 76808 | tf_op jit(solution)/shard_map/ppermute | solution.py:367
  40.3 4.1 %copy-start.4 = (f32[50,128]{1,0:T(8,128)}, f32[50,128]{1,0:T(8,128)S(1)}, u32[]{:S(2)}) copy-start(f32[50,128]{1,0:T(8,128)S(1)} %collective-permute-done.2.even_y_ref) | copy-start | bytes 76804
  44.4 0.6 %copy-start.5 = (f32[50,128]{1,0:T(8,128)}, f32[50,128]{1,0:T(8,128)S(1)}, u32[]{:S(2)}) copy-start(f32[50,128]{1,0:T(8,128)S(1)} %collective-permute-done.3.odd_y_ref) | copy-start | bytes 76804
  47.3 0.6 %copy-start = (f32[32,4,128]{2,1,0:T(4,128)}, f32[32,4,128]{2,1,0:T(4,128)S(1)}, u32[]{:S(2)}) copy-start(f32[32,4,128]{2,1,0:T(4,128)S(1)} %all-to-all-done.1) | copy-start | bytes 196612

commit v2 on v1

--- a/solution.py
+++ b/solution.py
@@ -20,8 +20,12 @@
 ROWS_PAD = 120
 
 
-def sds(shape, dtype=F32):
-    return jax.ShapeDtypeStruct(shape, dtype)
+def odd_dom_index():
+    return lax.axis_index("dom_2") == 1
+
+
+def odd_blk_index():
+    return (lax.axis_index("blk") & 1) == 1
 
 
 def split(value):
@@ -47,10 +51,19 @@
     return (weight_x[:, None, :] * weight_y[None]).reshape(64, LANES)
 
 
-def interpolate_kernel(
-    odd_ref, u_ref, element_ref, coords_ref, density_ref, class_ref,
-    places_ref, high_ref, low_ref, modulus_ref, even_ref, odd_swap_ref,
-):
+def interpolate_kernel(*refs):
+    count = (len(refs) - 5) // 2
+    sources, places_ref, modulus_ref, even_ref, odd_swap_ref = refs[:count], *refs[count : count + 4]
+    targets, semaphores = refs[count + 4 : -1], refs[-1]
+    copies = [
+        pltpu.make_async_copy(source, target, semaphores.at[index])
+        for index, (source, target) in enumerate(zip(sources, targets))
+    ]
+    for copy in copies:
+        copy.start()
+    u_ref, element_ref, coords_ref, density_ref, class_ref = targets[:5]
+    for copy in copies[:5]:
+        copy.wait()
     lane_block = iota((16, LANES), 1) >> 3
     pick = (lane_block == iota((16, LANES), 0)).astype(F32)
     kind = jnp.dot(
@@ -62,7 +75,7 @@
     density = density_ref[...]
     modulus = factor[None] * density * density
     modulus_ref[...] = modulus
-    odd = odd_ref[0, 0] != 0
+    odd = odd_dom_index()
     for comp in range(5):
         if comp < 3:
             first, last = u_ref[comp, 0], u_ref[comp, 7]
@@ -81,8 +94,6 @@
             element = element_ref[pl.ds(owner, 1), :]
             weight_z = hat(element & 127, coords_ref[2, pl.ds(owner, 1), :], LANES)
             high, low = split(weight_z)
-            high_ref[owner] = high
-            low_ref[owner] = low
             highs.append(high)
             lows.append(low)
         high = jnp.concatenate(highs, axis=1)
@@ -103,9 +114,30 @@
                     part * planar, axis=0, keepdims=True
                 )
             places_ref[pl.ds(4 * owner + 3, 1), :] = jnp.zeros((1, LANES), F32)
-
-
-def fibre_tables_kernel(slots_ref, angles_ref, direction_ref, fibre_ref, node_ref):
+    for copy in copies[5:]:
+        copy.wait()
+
+
+def weights_kernel(element_ref, coords_ref, depth_ref, weight_x_ref, weight_y_ref):
+    lowest, along = element_ref[...] >> 10, coords_ref[0]
+    for x in range(8):
+        weight_x_ref[x] = jnp.where(
+            lowest == x, 1.0 - along, jnp.where(lowest == x - 1, along, 0.0)
+        )
+    for owner in range(32):
+        element = element_ref[pl.ds(owner, 1), :]
+        high, low = split(hat(element & 127, coords_ref[2, pl.ds(owner, 1), :], LANES))
+        depth_ref[pl.ds(0, LANES), pl.ds(LANES * owner, LANES)] = high
+        depth_ref[pl.ds(LANES, LANES), pl.ds(LANES * owner, LANES)] = low
+        weight_y_ref[owner] = hat((element >> 7) & 7, coords_ref[1, pl.ds(owner, 1), :], 8)
+
+
+def fibre_tables_kernel(
+    slots_ref, angles_ref, stiffness_ref, direction_ref, stiff_ref, fibre_ref, node_ref
+):
+    square = iota((16, 16), 0) == iota((16, 16), 1)
+    stiffness = jnp.sum(jnp.where(square, stiffness_ref[...], 0.0), axis=1, keepdims=True)
+    stiff_ref[...] = jnp.where(iota((16, LANES), 1) < LANES - 1, stiffness, 0.0)
     azimuth, elevation = angles_ref[0], angles_ref[1]
     flat = jnp.cos(elevation)
     direction_ref[0] = jnp.cos(azimuth) * flat
@@ -138,7 +170,7 @@
 
 
 def fibre_kernel(
-    places_ref, slots_ref, direction_ref, stiffness_ref, fibre_ref, node_ref, pulls_ref
+    places_ref, slots_ref, direction_ref, stiff_ref, fibre_ref, node_ref, pulls_ref
 ):
     slots = slots_ref[...]
     host, spot = slots >> 7, slots & 127
@@ -152,8 +184,7 @@
     for comp in range(3):
         ahead = pltpu.roll(places[comp], LANES - 1, 1)
         strain = strain + direction_ref[comp] * (ahead - places[comp])
-    live = iota(slots.shape, 1) < LANES - 1
-    tension = jnp.where(live, stiffness_ref[...] * jnp.maximum(strain, 0.0), 0.0)
+    tension = stiff_ref[...] * jnp.maximum(strain, 0.0)
     forces = []
     for comp in range(3):
         pull = tension * direction_ref[comp]
@@ -173,10 +204,10 @@
 
 
 def side_rows_kernel(
-    odd_ref, u_ref, density_ref, modulus_ref, even_in_ref, odd_in_ref, even_ref, odd_swap_ref
-):
-    odd_dom = odd_ref[0, 0] != 0
-    odd_blk = odd_ref[0, 1] != 0
+    u_ref, density_ref, modulus_ref, even_in_ref, odd_in_ref, even_ref, odd_swap_ref
+):
+    odd_dom = odd_dom_index()
+    odd_blk = odd_blk_index()
     for comp in range(5):
         lower = jnp.where(odd_dom, even_in_ref[comp], odd_in_ref[comp])
         upper = jnp.where(odd_dom, odd_in_ref[comp], even_in_ref[comp])
@@ -195,13 +226,13 @@
 
 
 def elastic_kernel(
-    odd_ref, u_ref, velocity_ref, load_ref, density_ref, modulus_ref,
+    u_ref, velocity_ref, load_ref, density_ref, modulus_ref,
     even_x_ref, odd_x_ref, even_y_ref, odd_y_ref,
     velocity_out_ref, displacement_out_ref, inverse_mass_ref,
     nodes_ref, depth_ref, corner_ref,
 ):
-    odd_dom = odd_ref[0, 0] != 0
-    odd_blk = odd_ref[0, 1] != 0
+    odd_dom = odd_dom_index()
+    odd_blk = odd_blk_index()
     for comp in range(5):
         nodes_ref[comp, pl.ds(96, 24), :] = jnp.zeros((24, LANES), F32)
         lower = jnp.where(odd_dom, even_x_ref[comp], odd_x_ref[comp])
@@ -306,36 +337,23 @@
 
 
 def spread_kernel(
-    pulls_ref, element_ref, coords_ref, high_ref, low_ref,
+    pulls_ref, depth_ref, weight_x_ref, weight_y_ref,
     velocity_ref, displacement_ref, inverse_mass_ref,
-    displacement_out_ref, velocity_out_ref,
-):
-    total = jnp.zeros((384, 256), F32)
-    for pair in range(16):
-        highs, lows, weights = [], [], []
-        for half in range(2):
-            owner = 2 * pair + half
-            planar = planar_weights(
-                element_ref[pl.ds(owner, 1), :],
-                coords_ref[0, pl.ds(owner, 1), :],
-                coords_ref[1, pl.ds(owner, 1), :],
-            )
-            terms = jnp.concatenate(
-                [planar * pulls_ref[pl.ds(4 * owner + comp, 1), :] for comp in range(3)], axis=0
-            )
-            high, low = split(terms)
-            highs.append(high)
-            lows.append(low)
-            weights.append(jnp.concatenate([high_ref[owner], low_ref[owner]], axis=0))
-        left = jnp.concatenate(
-            [jnp.concatenate(highs, axis=1), jnp.concatenate(lows, axis=1)], axis=0
+    displacement_out_ref, velocity_out_ref, terms_ref,
+):
+    for owner in range(32):
+        at = pl.ds(LANES * owner, LANES)
+        weight_y = weight_y_ref[owner]
+        planar = jnp.concatenate(
+            [weight_y * weight_x_ref[x, pl.ds(owner, 1), :] for x in range(8)], axis=0
         )
-        total = total + lax.dot_general(
-            left,
-            jnp.concatenate(weights, axis=1),
-            (((1,), (1,)), ((), ())),
-            preferred_element_type=F32,
-        )
+        for comp in range(3):
+            high, low = split(planar * pulls_ref[pl.ds(4 * owner + comp, 1), :])
+            terms_ref[pl.ds(64 * comp, 64), at] = high
+            terms_ref[pl.ds(192 + 64 * comp, 64), at] = low
+    total = lax.dot_general(
+        terms_ref[...], depth_ref[...], (((1,), (1,)), ((), ())), preferred_element_type=F32
+    )
     fibre = (total[:192, :LANES] + total[192:, :LANES]) + (
         total[:192, LANES:] + total[192:, LANES:]
     )
@@ -347,18 +365,22 @@
             displacement_out_ref[comp, x] = displacement_ref[comp, x] + TIME_STEP * change
 
 
-def call(kernel, outs, scratch=(), scalars=0, inputs=0):
-    specs = [pl.BlockSpec(memory_space=pltpu.SMEM)] * scalars
-    specs += [pl.BlockSpec(memory_space=pltpu.VMEM)] * inputs
-    many = isinstance(outs, (tuple, list))
-    vmem = pl.BlockSpec(memory_space=pltpu.VMEM)
+VMEM = pl.BlockSpec(memory_space=pltpu.VMEM)
+
+
+def call(kernel, outs, ins, scratch=(), final=False, first=False):
+    space = jax.ShapeDtypeStruct if final else pltpu.VMEM
+    outs = tuple(space(shape, dtype) for shape, dtype in outs)
+    space_in = pltpu.HBM if first else pltpu.VMEM
+    ins = tuple(pltpu.with_memory_space_constraint(value, space_in) for value in ins)
     return pl.pallas_call(
         kernel,
         out_shape=outs,
-        in_specs=specs,
-        out_specs=type(outs)(vmem for _ in outs) if many else vmem,
+        in_specs=[pl.BlockSpec(memory_space=space_in)] * len(ins),
+        out_specs=(VMEM,) * len(outs),
         scratch_shapes=scratch,
-    )
+        compiler_params=pltpu.CompilerParams(vmem_limit_bytes=16 << 20),
+    )(*ins)
 
 
 def swap(shard, axis, first):
@@ -369,59 +391,80 @@
 
 def exchange(rows):
     blocks = rows.reshape(32, 4, LANES)
-    return lax.all_to_all(blocks, DOM, split_axis=0, concat_axis=0, tiled=True).reshape(
-        128, LANES
-    )
-
-
-def shards(
+    blocks = lax.all_to_all(blocks, DOM, split_axis=0, concat_axis=0, tiled=True)
+    return blocks.reshape(128, LANES)
+
+
+def step(
     displacement, velocity, load, density, block_class,
     host_element, host_coords, fibre_slot, fibre_angles, fibre_stiffness,
 ):
-    odd = jnp.stack([lax.axis_index(DOM) % 2, lax.axis_index("blk") % 2]).reshape(1, 2)
-    odd = odd.astype(jnp.int32)
-    element = host_element.reshape(32, LANES)
-    coords = host_coords.reshape(3, 32, LANES)
-    slots = fibre_slot.reshape(16, LANES)
     grid = (3, 8, 8, LANES)
-    weights = sds((32, LANES, LANES), BF16)
-    places, high, low, modulus, even_x, odd_x = call(
+    plane = (8, 8, LANES)
+    side = ((50, LANES), F32)
+    arguments = (
+        displacement,
+        host_element.reshape(32, LANES),
+        host_coords.reshape(3, 32, LANES),
+        density,
+        block_class.reshape(1, 16),
+        velocity,
+        load,
+        fibre_slot.reshape(16, LANES),
+        fibre_angles.reshape(2, 16, LANES),
+        fibre_stiffness.reshape(1, 16),
+    )
+    places, modulus, even_x, odd_x, *arguments = call(
         interpolate_kernel,
-        (
-            sds((128, LANES)), weights, weights, sds((8, 8, LANES)),
-            sds((5, 8, LANES)), sds((5, 8, LANES)),
-        ),
-        scalars=1, inputs=5,
-    )(odd, displacement, element, coords, density, block_class.reshape(1, 16))
-    received = exchange(places)
+        (((128, LANES), F32), (plane, F32), ((5, 8, LANES), F32), ((5, 8, LANES), F32))
+        + tuple((value.shape, value.dtype) for value in arguments),
+        arguments,
+        scratch=(pltpu.SemaphoreType.DMA((len(arguments),)),),
+        first=True,
+    )
+    displacement, element, coords, density, _, velocity, load, slots, angles, stiffness = arguments
     even_x = swap(even_x, DOM, 0)
     odd_x = swap(odd_x, DOM, 1)
-    direction, fibre, node = call(
+    received = exchange(places)
+    table = ((32, LANES), jnp.int32)
+    direction, stiff, fibre, node = call(
         fibre_tables_kernel,
-        (sds((3, 16, LANES)), sds((32, LANES), jnp.int32), sds((32, LANES), jnp.int32)),
-        inputs=2,
-    )(slots, fibre_angles.reshape(2, 16, LANES))
+        (((3, 16, LANES), F32), ((16, LANES), F32), table, table),
+        (slots, angles, stiffness),
+    )
     even_y, odd_y = call(
-        side_rows_kernel, (sds((50, LANES)), sds((50, LANES))), scalars=1, inputs=5
-    )(odd, displacement, density, modulus, even_x, odd_x)
+        side_rows_kernel, (side, side), (displacement, density, modulus, even_x, odd_x)
+    )
     even_y = swap(even_y, "blk", 0)
     odd_y = swap(odd_y, "blk", 1)
-    pulls = call(fibre_kernel, sds((128, LANES)), inputs=6)(
-        received, slots, direction, fibre_stiffness.reshape(16, 1), fibre, node
+    (pulls,) = call(
+        fibre_kernel, (((128, LANES), F32),),
+        (received, slots, direction, stiff, fibre, node),
     )
     returned = exchange(pulls)
-    step_velocity, step_displacement, inverse_mass = call(
+    depth, weight_x, weight_y = call(
+        weights_kernel,
+        (((256, 4096), BF16), ((8, 32, LANES), F32), ((32, 8, LANES), F32)),
+        (element, coords),
+    )
+    new_velocity, new_displacement, inverse_mass = call(
         elastic_kernel,
-        (sds(grid), sds(grid), sds((8, 8, LANES))),
+        ((grid, F32), (grid, F32), (plane, F32)),
+        (
+            displacement, velocity, load, density, modulus,
+            even_x, odd_x, even_y, odd_y,
+        ),
         scratch=(
             pltpu.VMEM((5, ROWS_PAD, LANES), F32),
             pltpu.VMEM((6, ROWS_PAD, LANES), F32),
             pltpu.VMEM((24, ROWS_PAD, LANES), F32),
         ),
-        scalars=1, inputs=9,
-    )(odd, displacement, velocity, load, density, modulus, even_x, odd_x, even_y, odd_y)
-    return call(spread_kernel, (sds(grid), sds(grid)), inputs=8)(
-        returned, element, coords, high, low, step_velocity, step_displacement, inverse_mass
+    )
+    return call(
+        spread_kernel, ((grid, F32), (grid, F32)),
+        (returned, depth, weight_x, weight_y, new_velocity, new_displacement, inverse_mass),
+        scratch=(pltpu.VMEM((384, 4096), BF16),),
+        final=True,
     )
 
 
@@ -442,6 +485,4 @@
         P(DOM, "blk"),
     )
     out_specs = (P(None, DOM, "blk", None), P(None, DOM, "blk", None))
-    return jax.shard_map(
-        shards, mesh=finer, in_specs=in_specs, out_specs=out_specs, check_vma=False
-    )
+    return jax.shard_map(step, mesh=finer, in_specs=in_specs, out_specs=out_specs, check_vma=False)

time: 51.8 us -> 42.1 us (0.81)
  Pallas kernels: 14.5 us -> 7.93 us
  local copies, waits for them, and re-layouts: 3.16 us -> 0 us
  waiting for transfers between devices: 11.9 us -> 12.9 us
  other arithmetic: 0.59 us -> 0 us
    pallas_call x6 -> x7, Pallas kernels: 14.5 us -> 7.93 us  [call(): pl.pallas_call(kernel, out_shape=outs, in_specs=[pl.BlockSpec(memory_spac...]
    unnamed x19 -> x0, local copies, waits for them, and re-layouts: 3.16 us -> none
    all_to_all x2, waiting for transfers between devices: 3.97 us -> 5.95 us  [exchange(): lax.all_to_all(blocks, DOM, split_axis=0, concat_axis=0, tiled=True)]
    ppermute x4, waiting for transfers between devices: 7.88 us -> 6.93 us  [swap(): return lax.ppermute(shard, axis, pairs + [(b, a) for a, b in pairs])]
    reshape x1 -> x0, other arithmetic: 0.59 us -> none  [shards(): jnp.stack([lax.axis_index(DOM) % 2, lax.axis_index('blk') % 2])]
  transfers between devices with their start and end apart: 6 -> 6, of which waited for: 4 -> 4; matrix products, arithmetic and copies ran while one was open for 1% -> 0% of each run, Pallas kernels for 11% -> 4%
where the time goes in v2:
time: 42.1 us; the launch traced here: 41.8 us
  starting transfers between devices  20.3 us (48%)
  waiting for transfers between devices  12.9 us (31%)
  Pallas kernels  7.93 us (19%)
  between operations  0.71 us (2%)
    all_to_all x2, starting transfers between devices, exchange(): lax.all_to_all(blocks, DOM, split_axis=0, concat_axis=0, tiled=True)  12.5 us
    pallas_call x7, Pallas kernels, call(): pl.pallas_call(kernel, out_shape=outs, in_specs=[pl.BlockSpec(memory_spac...  7.93 us
    ppermute x4, starting transfers between devices, swap(): return lax.ppermute(shard, axis, pairs + [(b, a) for a, b in pairs])  7.77 us
    ppermute x4, waiting for transfers between devices, swap(): return lax.ppermute(shard, axis, pairs + [(b, a) for a, b in pairs])  6.93 us
    all_to_all x2, waiting for transfers between devices, exchange(): lax.all_to_all(blocks, DOM, split_axis=0, concat_axis=0, tiled=True)  5.95 us
  transfers between devices with their start and end apart: 6, of which 4 were waited for; matrix products, arithmetic and copies ran while one was open for 0% of the time, Pallas kernels for 4%

profile of v2, /device:TPU:136, one launch (start us, length us, event | category | flops | bytes accessed | tf_op | source)
XLA Modules:
  0.0 41.8 jit_solution(13935238718381728980)
XLA Ops:
  0.6 3.0 %shard_map.113 = (f32[128,128]{1,0:T(8,128)}, f32[8,8,128]{2,1,0:T(8,128)S(1)}, f32[5,8,128]{2,1,0:T(8,128)S(1)}, f32[5,8,128]{2,1,0:T(8,128)S(1)}, f32[3,8,8,12...) custom-call(f32[3,8,8,128]{3,2,1,0:T(8,128)} %refs_0_.1, ...), custom_call_target="tpu_custom_call" | custom-call | tf_op jit(solution)/shard_map/pallas_call | solution.py:376
  3.6 7.6 %all-to-all-start = ((f32[32,4,128]{2,1,0:T(4,128)}), f32[32,4,128]{2,1,0:T(4,128)S(1)}, u32[]{:S(2)}, u32[]{:S(2)}) async-start(f32[32,4,128]{2,1,0:T(4,128)} %bitcast.6), calls=%async_computation | async-start | bytes 131072 | tf_op jit(solution)/shard_map/all_to_all | solution.py:394
  11.2 0.4 shard_map.114
  11.6 5.9 %all-to-all-done = f32[32,4,128]{2,1,0:T(4,128)S(1)} async-done(((f32[32,4,128]{2,1,0:T(4,128)}), f32[32,4,128]{2,1,0:T(4,128)S(1)}, u32[]{:S(2)}, u32[]{:S(2)}) %all-to-all-start) | async-done | bytes 65568 | tf_op jit(solution)/shard_map/all_to_all | solution.py:394
  17.5 1.3 %shard_map.115 = f32[128,128]{1,0:T(8,128)} custom-call(f32[128,128]{1,0:T(8,128)S(1)} %bitcast.10, s32[16,128]{1,0:T(8,128)S(1)} %get-tuple-element.28.slots_ref, f32[3,16,128]{2,1,0:T(8,128)S(1)} %get-tuple-element.31.direction_ref, f32[16,128]{1,0:T(8,128)S(1)} %get-tuple-element.32.stiff_ref, s32[32,128]{1,0:T(8,128)S(1)} %get-tuple-element.33.fibre_ref, ...), custom_call_target="tpu_custom_call" | custom-call | tf_op jit(solution)/shard_map/pallas_call | solution.py:376
  18.8 5.0 %all-to-all-start.1 = ((f32[32,4,128]{2,1,0:T(4,128)}), f32[32,4,128]{2,1,0:T(4,128)S(1)}, u32[]{:S(2)}, u32[]{:S(2)}) async-start(f32[32,4,128]{2,1,0:T(4,128)} %bitcast.8), calls=%async_computation.1 | async-start | bytes 131072 | tf_op jit(solution)/shard_map/all_to_all | solution.py:394
  23.8 0.2 collective-permute-start
  24.0 4.5 %collective-permute-start.1 = (f32[5,8,128]{2,1,0:T(8,128)S(1)}, f32[5,8,128]{2,1,0:T(8,128)S(1)}, u32[]{:S(2)}, u32[]{:S(2)}) collective-permute-start(f32[5,8,128]{2,1,0:T(8,128)S(1)} %get-tuple-element.46), channel_id=1, source_target_pairs={{8,16},{24,32},{40,48},{56,64},{72,80},{88,96},{104,112},{120,128}... | collective-permute-start | bytes 61448 | tf_op jit(solution)/shard_map/ppermute | solution.py:389
  28.6 0.0 collective-permute-done.even_in_ref.even_x_ref
  28.6 2.6 %collective-permute-done.1.odd_in_ref.odd_x_ref = f32[5,8,128]{2,1,0:T(8,128)S(1)} collective-permute-done((f32[5,8,128]{2,1,0:T(8,128)S(1)}, f32[5,8,128]{2,1,0:T(8,128)S(1)}, u32[]{:S(2)}, u32[]{:S(2)}) %collective-permute-start.1) | collective-permute-done | bytes 20512 | tf_op jit(solution)/shard_map/ppermute | solution.py:389
  31.3 1.1 %collective-permute-start.2 = (f32[50,128]{1,0:T(8,128)S(1)}, f32[50,128]{1,0:T(8,128)S(1)}, u32[]{:S(2)}, u32[]{:S(2)}) collective-permute-start(f32[50,128]{1,0:T(8,128)S(1)} %get-tuple-element.47), channel_id=1, source_target_pairs={{0,1},{2,3},{4,5},{6,7},{1,0},{3,2},{5,4},{7,6},{8,9},{10,11},{12,... | collective-permute-start | bytes 76808 | tf_op jit(solution)/shard_map/ppermute | solution.py:389
  32.4 1.9 %collective-permute-start.3 = (f32[50,128]{1,0:T(8,128)S(1)}, f32[50,128]{1,0:T(8,128)S(1)}, u32[]{:S(2)}, u32[]{:S(2)}) collective-permute-start(f32[50,128]{1,0:T(8,128)S(1)} %get-tuple-element.48), channel_id=1, source_target_pairs={{1,2},{3,4},{5,6},{2,1},{4,3},{6,5},{9,10},{11,12},{13,14},{10,9},... | collective-permute-start | bytes 76808 | tf_op jit(solution)/shard_map/ppermute | solution.py:389
  34.3 0.7 %shard_map.116 = (bf16[256,4096]{1,0:T(8,128)(2,1)S(1)}, f32[8,32,128]{2,1,0:T(8,128)S(1)}, f32[32,8,128]{2,1,0:T(8,128)S(1)}) custom-call(s32[32,128]{1,0:T(8,128)S(1)} %get-tuple-element.35.element_ref, f32[3,32,128]{2,1,0:T(8,128)S(1)} %get-tuple-element.36.coords_ref), custom_call_target="tpu_custom_call" | custom-call | tf_op jit(solution)/shard_map/pallas_call | solution.py:376
  35.0 0.2 collective-permute-done.2.even_y_ref
  35.2 4.1 %collective-permute-done.3.odd_y_ref = f32[50,128]{1,0:T(8,128)S(1)} collective-permute-done((f32[50,128]{1,0:T(8,128)S(1)}, f32[50,128]{1,0:T(8,128)S(1)}, u32[]{:S(2)}, u32[]{:S(2)}) %collective-permute-start.3) | collective-permute-done | bytes 25632 | tf_op jit(solution)/shard_map/ppermute | solution.py:389
  39.3 0.6 %shard_map.118 = (f32[3,8,8,128]{3,2,1,0:T(8,128)S(1)}, f32[3,8,8,128]{3,2,1,0:T(8,128)S(1)}, f32[8,8,128]{2,1,0:T(8,128)S(1)}) custom-call(f32[3,8,8,128]{3,2,1,0:T(8,128)S(1)} %get-tuple-element.40.u_ref, f32[3,8,8,128]{3,2,1,0:T(8,128)S(1)} %get-tuple-element.41.velocity_ref, f32[3,8,8,128]{3,2,1,0:T(8,128)S(1)} %get-tuple-element.42.load_ref, ...), custom_call_target="tpu_custom_call" | custom-call | tf_op jit(solution)/shard_map/pallas_call | solution.py:376
  39.9 0.0 all-to-all-done.1
  39.9 1.9 %shard_map.119 = (f32[3,8,8,128]{3,2,1,0:T(8,128)}, f32[3,8,8,128]{3,2,1,0:T(8,128)}) custom-call(f32[128,128]{1,0:T(8,128)S(1)} %bitcast.11, bf16[256,4096]{1,0:T(8,128)(2,1)S(1)} %get-tuple-element.37.depth_ref, f32[8,32,128]{2,1,0:T(8,128)S(1)} %get-tuple-element.38.weight_x_ref, f32[32,8,128]{2,1,0:T(8,128)S(1)} %get-tuple-element.39.weight_y_ref, ...), custom_call_target="tpu_custom_call" | custom-call | tf_op jit(solution)/shard_map/pallas_call | solution.py:376
  (1 shorter events, 0.0 us)
Async XLA Ops:
  3.6 13.9 %all-to-all-start = ((f32[32,4,128]{2,1,0:T(4,128)}), f32[32,4,128]{2,1,0:T(4,128)S(1)}, u32[]{:S(2)}, u32[]{:S(2)}) async-start(f32[32,4,128]{2,1,0:T(4,128)} %bitcast.6), calls=%async_computation | async-start | bytes 131072 | tf_op jit(solution)/shard_map/all_to_all | solution.py:394
  18.8 21.0 %all-to-all-start.1 = ((f32[32,4,128]{2,1,0:T(4,128)}), f32[32,4,128]{2,1,0:T(4,128)S(1)}, u32[]{:S(2)}, u32[]{:S(2)}) async-start(f32[32,4,128]{2,1,0:T(4,128)} %bitcast.8), calls=%async_computation.1 | async-start | bytes 131072 | tf_op jit(solution)/shard_map/all_to_all | solution.py:394
  23.8 4.8 %collective-permute-start = (f32[5,8,128]{2,1,0:T(8,128)S(1)}, f32[5,8,128]{2,1,0:T(8,128)S(1)}, u32[]{:S(2)}, u32[]{:S(2)}) collective-permute-start(f32[5,8,128]{2,1,0:T(8,128)S(1)} %get-tuple-element.45), channel_id=1, source_target_pairs={{0,8},{16,24},{32,40},{48,56},{64,72},{80,88},{96,104},{112,120},{... | collective-permute-start | bytes 61448 | tf_op jit(solution)/shard_map/ppermute | solution.py:389
  24.0 7.2 %collective-permute-start.1 = (f32[5,8,128]{2,1,0:T(8,128)S(1)}, f32[5,8,128]{2,1,0:T(8,128)S(1)}, u32[]{:S(2)}, u32[]{:S(2)}) collective-permute-start(f32[5,8,128]{2,1,0:T(8,128)S(1)} %get-tuple-element.46), channel_id=1, source_target_pairs={{8,16},{24,32},{40,48},{56,64},{72,80},{88,96},{104,112},{120,128}... | collective-permute-start | bytes 61448 | tf_op jit(solution)/shard_map/ppermute | solution.py:389
  31.3 4.0 %collective-permute-start.2 = (f32[50,128]{1,0:T(8,128)S(1)}, f32[50,128]{1,0:T(8,128)S(1)}, u32[]{:S(2)}, u32[]{:S(2)}) collective-permute-start(f32[50,128]{1,0:T(8,128)S(1)} %get-tuple-element.47), channel_id=1, source_target_pairs={{0,1},{2,3},{4,5},{6,7},{1,0},{3,2},{5,4},{7,6},{8,9},{10,11},{12,... | collective-permute-start | bytes 76808 | tf_op jit(solution)/shard_map/ppermute | solution.py:389
  32.4 7.0 %collective-permute-start.3 = (f32[50,128]{1,0:T(8,128)S(1)}, f32[50,128]{1,0:T(8,128)S(1)}, u32[]{:S(2)}, u32[]{:S(2)}) collective-permute-start(f32[50,128]{1,0:T(8,128)S(1)} %get-tuple-element.48), channel_id=1, source_target_pairs={{1,2},{3,4},{5,6},{2,1},{4,3},{6,5},{9,10},{11,12},{13,14},{10,9},... | collective-permute-start | bytes 76808 | tf_op jit(solution)/shard_map/ppermute | solution.py:389

commit v3 on v2

--- a/solution.py
+++ b/solution.py
@@ -45,16 +45,26 @@
     )
 
 
-def planar_weights(element, along_r, along_p):
-    weight_x = hat(element >> 10, along_r, 8)
-    weight_y = hat((element >> 7) & 7, along_p, 8)
-    return (weight_x[:, None, :] * weight_y[None]).reshape(64, LANES)
+def depth_weights(element, along):
+    shape = (LANES, LANES)
+    lowest = jnp.broadcast_to(element & (LANES - 1), shape).astype(jnp.int16)
+    where = lax.broadcasted_iota(jnp.int16, shape, 0)
+    here, above = where == lowest, where == lowest + jnp.int16(1)
+    zero = jnp.zeros(shape, BF16)
+    parts = []
+    for lower, upper in zip(split(1.0 - along), split(along)):
+        lower = jnp.broadcast_to(lower.astype(F32), shape).astype(BF16)
+        upper = jnp.broadcast_to(upper.astype(F32), shape).astype(BF16)
+        parts.append(jnp.where(here, lower, jnp.where(above, upper, zero)))
+    return parts
 
 
 def interpolate_kernel(*refs):
-    count = (len(refs) - 5) // 2
-    sources, places_ref, modulus_ref, even_ref, odd_swap_ref = refs[:count], *refs[count : count + 4]
-    targets, semaphores = refs[count + 4 : -1], refs[-1]
+    count = (len(refs) - 7) // 2
+    sources, targets, semaphores = refs[:count], refs[count + 6 : -1], refs[-1]
+    places_ref, modulus_ref, even_ref, odd_ref, weight_x_ref, weight_y_ref = refs[
+        count : count + 6
+    ]
     copies = [
         pltpu.make_async_copy(source, target, semaphores.at[index])
         for index, (source, target) in enumerate(zip(sources, targets))
@@ -64,72 +74,62 @@
     u_ref, element_ref, coords_ref, density_ref, class_ref = targets[:5]
     for copy in copies[:5]:
         copy.wait()
-    lane_block = iota((16, LANES), 1) >> 3
-    pick = (lane_block == iota((16, LANES), 0)).astype(F32)
-    kind = jnp.dot(
-        jnp.broadcast_to(class_ref[...].astype(F32), (8, 16)), pick, preferred_element_type=F32
-    )
-    factor = jnp.zeros((8, LANES), F32)
-    for index, value in enumerate(CLASS_VALUES):
-        factor = factor + jnp.where(kind == float(index), value, 0.0)
-    density = density_ref[...]
-    modulus = factor[None] * density * density
-    modulus_ref[...] = modulus
-    odd = odd_dom_index()
-    for comp in range(5):
-        if comp < 3:
-            first, last = u_ref[comp, 0], u_ref[comp, 7]
-        else:
-            source = modulus if comp == 3 else density
-            first, last = source[0], source[7]
-        even_ref[comp] = jnp.where(odd, first, last)
-        odd_swap_ref[comp] = jnp.where(odd, last, first)
-
-    field_high, field_low = split(u_ref[...].reshape(192, LANES))
-    field = jnp.concatenate([field_high, field_low], axis=1)
-    for pair in range(16):
-        highs, lows = [], []
-        for half in range(2):
-            owner = 2 * pair + half
-            element = element_ref[pl.ds(owner, 1), :]
-            weight_z = hat(element & 127, coords_ref[2, pl.ds(owner, 1), :], LANES)
-            high, low = split(weight_z)
-            highs.append(high)
-            lows.append(low)
-        high = jnp.concatenate(highs, axis=1)
-        low = jnp.concatenate(lows, axis=1)
-        sums = jnp.dot(
-            field, jnp.concatenate([high, high], axis=0), preferred_element_type=F32
-        ) + jnp.dot(field_high, low, preferred_element_type=F32)
-        for half in range(2):
-            owner = 2 * pair + half
-            planar = planar_weights(
-                element_ref[pl.ds(owner, 1), :],
-                coords_ref[0, pl.ds(owner, 1), :],
-                coords_ref[1, pl.ds(owner, 1), :],
-            )
-            for comp in range(3):
-                part = sums[64 * comp : 64 * comp + 64, LANES * half : LANES * half + LANES]
-                places_ref[pl.ds(4 * owner + comp, 1), :] = jnp.sum(
-                    part * planar, axis=0, keepdims=True
-                )
-            places_ref[pl.ds(4 * owner + 3, 1), :] = jnp.zeros((1, LANES), F32)
-    for copy in copies[5:]:
-        copy.wait()
-
-
-def weights_kernel(element_ref, coords_ref, depth_ref, weight_x_ref, weight_y_ref):
     lowest, along = element_ref[...] >> 10, coords_ref[0]
     for x in range(8):
         weight_x_ref[x] = jnp.where(
             lowest == x, 1.0 - along, jnp.where(lowest == x - 1, along, 0.0)
         )
+    field_high, field_low = split(u_ref[...].reshape(192, LANES))
+    field = jnp.concatenate([field_high, field_low, field_high], axis=1)
+    for pair in range(16):
+        parts = []
+        for owner in (2 * pair, 2 * pair + 1):
+            row = pl.ds(owner, 1)
+            high, low = depth_weights(element_ref[row, :], coords_ref[2, row, :])
+            parts.append(jnp.concatenate([high, high, low], axis=0))
+        sums = jnp.dot(field, jnp.concatenate(parts, axis=1), preferred_element_type=F32)
+        for half in range(2):
+            owner = 2 * pair + half
+            row = pl.ds(owner, 1)
+            weight_y = hat((element_ref[row, :] >> 7) & 7, coords_ref[1, row, :], 8)
+            weight_y_ref[owner] = weight_y
+            rows = [weight_x_ref[x, row, :] for x in range(8)]
+            for comp in range(3):
+                total = sum(
+                    sums[64 * comp + 8 * x :, LANES * half : LANES * half + LANES][:8] * rows[x]
+                    for x in range(8)
+                )
+                places_ref[pl.ds(4 * owner + comp, 1), :] = jnp.sum(
+                    total * weight_y, axis=0, keepdims=True
+                )
+            places_ref[pl.ds(4 * owner + 3, 1), :] = jnp.zeros((1, LANES), F32)
+
+    lane_block = iota((16, LANES), 1) >> 3
+    pick = (lane_block == iota((16, LANES), 0)).astype(F32)
+    kind = jnp.dot(
+        jnp.broadcast_to(class_ref[...].astype(F32), (8, 16)), pick, preferred_element_type=F32
+    )
+    factor = jnp.zeros((8, LANES), F32)
+    for index, value in enumerate(CLASS_VALUES):
+        factor = factor + jnp.where(kind == float(index), value, 0.0)
+    density = density_ref[...]
+    modulus_ref[...] = factor[None] * density * density
+    odd_blk = odd_blk_index()
+    for comp in range(5):
+        source = modulus_ref if comp == 3 else density_ref if comp == 4 else u_ref.at[comp]
+        first, last = source[:, 0, :], source[:, 7, :]
+        even_ref[comp] = jnp.where(odd_blk, first, last)
+        odd_ref[comp] = jnp.where(odd_blk, last, first)
+    for copy in copies[5:]:
+        copy.wait()
+
+
+def weights_kernel(element_ref, coords_ref, depth_ref):
     for owner in range(32):
-        element = element_ref[pl.ds(owner, 1), :]
-        high, low = split(hat(element & 127, coords_ref[2, pl.ds(owner, 1), :], LANES))
-        depth_ref[pl.ds(0, LANES), pl.ds(LANES * owner, LANES)] = high
-        depth_ref[pl.ds(LANES, LANES), pl.ds(LANES * owner, LANES)] = low
-        weight_y_ref[owner] = hat((element >> 7) & 7, coords_ref[1, pl.ds(owner, 1), :], 8)
+        row = pl.ds(owner, 1)
+        high, low = depth_weights(element_ref[row, :], coords_ref[2, row, :])
+        depth_ref[owner, pl.ds(0, LANES), :] = high
+        depth_ref[owner, pl.ds(LANES, LANES), :] = low
 
 
 def fibre_tables_kernel(
@@ -203,26 +203,18 @@
         pulls_ref[pl.ds(32 * block + 3, 8, stride=4), :] = jnp.zeros((8, LANES), F32)
 
 
-def side_rows_kernel(
-    u_ref, density_ref, modulus_ref, even_in_ref, odd_in_ref, even_ref, odd_swap_ref
-):
-    odd_dom = odd_dom_index()
-    odd_blk = odd_blk_index()
+def sides_kernel(u_ref, density_ref, modulus_ref, even_y_ref, odd_y_ref, even_ref, odd_ref):
+    odd_dom, odd_blk = odd_dom_index(), odd_blk_index()
     for comp in range(5):
-        lower = jnp.where(odd_dom, even_in_ref[comp], odd_in_ref[comp])
-        upper = jnp.where(odd_dom, odd_in_ref[comp], even_in_ref[comp])
-        rows = []
-        for at in (0, 7):
-            if comp < 3:
-                own = u_ref[comp, :, at, :]
-            else:
-                own = (modulus_ref if comp == 3 else density_ref)[:, at, :]
-            rows.append(
-                jnp.concatenate([lower[at : at + 1], own, upper[at : at + 1]], axis=0)
-            )
-        first, last = rows
-        even_ref[pl.ds(10 * comp, 10), :] = jnp.where(odd_blk, first, last)
-        odd_swap_ref[pl.ds(10 * comp, 10), :] = jnp.where(odd_blk, last, first)
+        left = jnp.where(odd_blk, even_y_ref[comp], odd_y_ref[comp])
+        right = jnp.where(odd_blk, odd_y_ref[comp], even_y_ref[comp])
+        source = modulus_ref if comp == 3 else density_ref if comp == 4 else u_ref.at[comp]
+        first, last = (
+            jnp.concatenate([left[at : at + 1], source[at], right[at : at + 1]], axis=0)
+            for at in (0, 7)
+        )
+        even_ref[pl.ds(10 * comp, 10), :] = jnp.where(odd_dom, first, last)
+        odd_ref[pl.ds(10 * comp, 10), :] = jnp.where(odd_dom, last, first)
 
 
 def elastic_kernel(
@@ -235,23 +227,16 @@
     odd_blk = odd_blk_index()
     for comp in range(5):
         nodes_ref[comp, pl.ds(96, 24), :] = jnp.zeros((24, LANES), F32)
-        lower = jnp.where(odd_dom, even_x_ref[comp], odd_x_ref[comp])
-        upper = jnp.where(odd_dom, odd_x_ref[comp], even_x_ref[comp])
-        nodes_ref[comp, pl.ds(1, 8), :] = lower
-        nodes_ref[comp, pl.ds(91, 8), :] = upper
+        even, odd = even_x_ref[pl.ds(10 * comp, 10), :], odd_x_ref[pl.ds(10 * comp, 10), :]
+        nodes_ref[comp, pl.ds(0, 10), :] = jnp.where(odd_dom, even, odd)
+        nodes_ref[comp, pl.ds(90, 10), :] = jnp.where(odd_dom, odd, even)
+        left = jnp.where(odd_blk, even_y_ref[comp], odd_y_ref[comp])
+        right = jnp.where(odd_blk, odd_y_ref[comp], even_y_ref[comp])
+        source = modulus_ref if comp == 3 else density_ref if comp == 4 else u_ref.at[comp]
         for x in range(8):
-            if comp < 3:
-                own = u_ref[comp, x]
-            else:
-                own = (modulus_ref if comp == 3 else density_ref)[x]
-            nodes_ref[comp, pl.ds(10 * x + 11, 8), :] = own
-        even = even_y_ref[pl.ds(10 * comp, 10), :]
-        odd = odd_y_ref[pl.ds(10 * comp, 10), :]
-        left = jnp.where(odd_blk, even, odd)
-        right = jnp.where(odd_blk, odd, even)
-        for x in range(10):
-            nodes_ref[comp, pl.ds(10 * x, 1), :] = left[x : x + 1]
-            nodes_ref[comp, pl.ds(10 * x + 9, 1), :] = right[x : x + 1]
+            nodes_ref[comp, pl.ds(10 * x + 10, 1), :] = left[x : x + 1]
+            nodes_ref[comp, pl.ds(10 * x + 11, 8), :] = source[x]
+            nodes_ref[comp, pl.ds(10 * x + 19, 1), :] = right[x : x + 1]
     last_lane = iota((8, LANES), 1) == LANES - 1
     first_lane = iota((8, LANES), 1) == 0
     for comp in range(3):
@@ -342,17 +327,19 @@
     displacement_out_ref, velocity_out_ref, terms_ref,
 ):
     for owner in range(32):
-        at = pl.ds(LANES * owner, LANES)
         weight_y = weight_y_ref[owner]
         planar = jnp.concatenate(
             [weight_y * weight_x_ref[x, pl.ds(owner, 1), :] for x in range(8)], axis=0
         )
         for comp in range(3):
             high, low = split(planar * pulls_ref[pl.ds(4 * owner + comp, 1), :])
-            terms_ref[pl.ds(64 * comp, 64), at] = high
-            terms_ref[pl.ds(192 + 64 * comp, 64), at] = low
+            terms_ref[owner, pl.ds(64 * comp, 64), :] = high
+            terms_ref[owner, pl.ds(192 + 64 * comp, 64), :] = low
     total = lax.dot_general(
-        terms_ref[...], depth_ref[...], (((1,), (1,)), ((), ())), preferred_element_type=F32
+        jnp.concatenate([terms_ref[owner] for owner in range(32)], axis=1),
+        jnp.concatenate([depth_ref[owner] for owner in range(32)], axis=1),
+        (((1,), (1,)), ((), ())),
+        preferred_element_type=F32,
     )
     fibre = (total[:192, :LANES] + total[192:, :LANES]) + (
         total[:192, LANES:] + total[192:, LANES:]
@@ -414,17 +401,20 @@
         fibre_angles.reshape(2, 16, LANES),
         fibre_stiffness.reshape(1, 16),
     )
-    places, modulus, even_x, odd_x, *arguments = call(
+    places, modulus, even_y, odd_y, weight_x, weight_y, *arguments = call(
         interpolate_kernel,
-        (((128, LANES), F32), (plane, F32), ((5, 8, LANES), F32), ((5, 8, LANES), F32))
+        (
+            ((128, LANES), F32), (plane, F32), ((5, 8, LANES), F32), ((5, 8, LANES), F32),
+            ((8, 32, LANES), F32), ((32, 8, LANES), F32),
+        )
         + tuple((value.shape, value.dtype) for value in arguments),
         arguments,
         scratch=(pltpu.SemaphoreType.DMA((len(arguments),)),),
         first=True,
     )
     displacement, element, coords, density, _, velocity, load, slots, angles, stiffness = arguments
-    even_x = swap(even_x, DOM, 0)
-    odd_x = swap(odd_x, DOM, 1)
+    even_y = swap(even_y, "blk", 0)
+    odd_y = swap(odd_y, "blk", 1)
     received = exchange(places)
     table = ((32, LANES), jnp.int32)
     direction, stiff, fibre, node = call(
@@ -432,21 +422,17 @@
         (((3, 16, LANES), F32), ((16, LANES), F32), table, table),
         (slots, angles, stiffness),
     )
-    even_y, odd_y = call(
-        side_rows_kernel, (side, side), (displacement, density, modulus, even_x, odd_x)
-    )
-    even_y = swap(even_y, "blk", 0)
-    odd_y = swap(odd_y, "blk", 1)
+    even_x, odd_x = call(
+        sides_kernel, (side, side), (displacement, density, modulus, even_y, odd_y)
+    )
+    even_x = swap(even_x, DOM, 0)
+    odd_x = swap(odd_x, DOM, 1)
     (pulls,) = call(
         fibre_kernel, (((128, LANES), F32),),
         (received, slots, direction, stiff, fibre, node),
     )
     returned = exchange(pulls)
-    depth, weight_x, weight_y = call(
-        weights_kernel,
-        (((256, 4096), BF16), ((8, 32, LANES), F32), ((32, 8, LANES), F32)),
-        (element, coords),
-    )
+    (depth,) = call(weights_kernel, (((32, 256, LANES), BF16),), (element, coords))
     new_velocity, new_displacement, inverse_mass = call(
         elastic_kernel,
         ((grid, F32), (grid, F32), (plane, F32)),
@@ -463,7 +449,7 @@
     return call(
         spread_kernel, ((grid, F32), (grid, F32)),
         (returned, depth, weight_x, weight_y, new_velocity, new_displacement, inverse_mass),
-        scratch=(pltpu.VMEM((384, 4096), BF16),),
+        scratch=(pltpu.VMEM((32, 384, LANES), BF16),),
         final=True,
     )
 

time: 42.1 us -> 42.2 us (level)
  the two profiles are of different devices: /device:TPU:136 before, /device:TPU:135 now
where the time goes in v3:
time: 42.2 us; the launch traced here: 41.9 us
  starting transfers between devices  21.1 us (50%)
  waiting for transfers between devices  12.9 us (31%)
  Pallas kernels  7.18 us (17%)
  between operations  0.71 us (2%)
    all_to_all x2, starting transfers between devices, exchange(): lax.all_to_all(blocks, DOM, split_axis=0, concat_axis=0, tiled=True)  13.4 us
    ppermute x4, starting transfers between devices, swap(): return lax.ppermute(shard, axis, pairs + [(b, a) for a, b in pairs])  7.65 us
    ppermute x4, waiting for transfers between devices, swap(): return lax.ppermute(shard, axis, pairs + [(b, a) for a, b in pairs])  7.58 us
    pallas_call x7, Pallas kernels, call(): pl.pallas_call(kernel, out_shape=outs, in_specs=[pl.BlockSpec(memory_spac...  7.18 us
    all_to_all x2, waiting for transfers between devices, exchange(): lax.all_to_all(blocks, DOM, split_axis=0, concat_axis=0, tiled=True)  5.35 us
  transfers between devices with their start and end apart: 6, of which 4 were waited for; matrix products, arithmetic and copies ran while one was open for 0% of the time, Pallas kernels for 3%

profile of v3, /device:TPU:135, one launch (start us, length us, event | category | flops | bytes accessed | tf_op | source)
XLA Modules:
  0.0 41.9 jit_solution(8124255679000054369)
XLA Ops:
  0.6 2.7 %shard_map.113 = (f32[128,128]{1,0:T(8,128)}, f32[8,8,128]{2,1,0:T(8,128)S(1)}, f32[5,8,128]{2,1,0:T(8,128)S(1)}, f32[5,8,128]{2,1,0:T(8,128)S(1)}, f32[8,32,128...) custom-call(f32[3,8,8,128]{3,2,1,0:T(8,128)} %refs_0_.1, ...), custom_call_target="tpu_custom_call" | custom-call | tf_op jit(solution)/shard_map/pallas_call | solution.py:363
  3.3 7.9 %all-to-all-start = ((f32[32,4,128]{2,1,0:T(4,128)}), f32[32,4,128]{2,1,0:T(4,128)S(1)}, u32[]{:S(2)}, u32[]{:S(2)}) async-start(f32[32,4,128]{2,1,0:T(4,128)} %bitcast.6), calls=%async_computation | async-start | bytes 131072 | tf_op jit(solution)/shard_map/all_to_all | solution.py:381
  11.2 0.4 shard_map.114
  11.6 5.3 %all-to-all-done = f32[32,4,128]{2,1,0:T(4,128)S(1)} async-done(((f32[32,4,128]{2,1,0:T(4,128)}), f32[32,4,128]{2,1,0:T(4,128)S(1)}, u32[]{:S(2)}, u32[]{:S(2)}) %all-to-all-start) | async-done | bytes 65568 | tf_op jit(solution)/shard_map/all_to_all | solution.py:381
  16.9 1.3 %shard_map.115 = f32[128,128]{1,0:T(8,128)} custom-call(f32[128,128]{1,0:T(8,128)S(1)} %bitcast.10, s32[16,128]{1,0:T(8,128)S(1)} %get-tuple-element.27.slots_ref, f32[3,16,128]{2,1,0:T(8,128)S(1)} %get-tuple-element.30.direction_ref, f32[16,128]{1,0:T(8,128)S(1)} %get-tuple-element.31.stiff_ref, s32[32,128]{1,0:T(8,128)S(1)} %get-tuple-element.32.fibre_ref, ...), custom_call_target="tpu_custom_call" | custom-call | tf_op jit(solution)/shard_map/pallas_call | solution.py:363
  18.2 5.6 %all-to-all-start.1 = ((f32[32,4,128]{2,1,0:T(4,128)}), f32[32,4,128]{2,1,0:T(4,128)S(1)}, u32[]{:S(2)}, u32[]{:S(2)}) async-start(f32[32,4,128]{2,1,0:T(4,128)} %bitcast.8), calls=%async_computation.1 | async-start | bytes 131072 | tf_op jit(solution)/shard_map/all_to_all | solution.py:381
  23.8 0.8 %collective-permute-start = (f32[5,8,128]{2,1,0:T(8,128)S(1)}, f32[5,8,128]{2,1,0:T(8,128)S(1)}, u32[]{:S(2)}, u32[]{:S(2)}) collective-permute-start(f32[5,8,128]{2,1,0:T(8,128)S(1)} %get-tuple-element.43), channel_id=1, source_target_pairs={{0,1},{2,3},{4,5},{6,7},{1,0},{3,2},{5,4},{7,6},{8,9},{10,11},{12,... | collective-permute-start | bytes 61448 | tf_op jit(solution)/shard_map/ppermute | solution.py:376
  24.6 1.9 %collective-permute-start.1 = (f32[5,8,128]{2,1,0:T(8,128)S(1)}, f32[5,8,128]{2,1,0:T(8,128)S(1)}, u32[]{:S(2)}, u32[]{:S(2)}) collective-permute-start(f32[5,8,128]{2,1,0:T(8,128)S(1)} %get-tuple-element.44), channel_id=1, source_target_pairs={{1,2},{3,4},{5,6},{2,1},{4,3},{6,5},{9,10},{11,12},{13,14},{10,9},... | collective-permute-start | bytes 61448 | tf_op jit(solution)/shard_map/ppermute | solution.py:376
  26.6 0.3 collective-permute-done.even_y_ref
  26.8 3.5 %collective-permute-done.1.odd_y_ref = f32[5,8,128]{2,1,0:T(8,128)S(1)} collective-permute-done((f32[5,8,128]{2,1,0:T(8,128)S(1)}, f32[5,8,128]{2,1,0:T(8,128)S(1)}, u32[]{:S(2)}, u32[]{:S(2)}) %collective-permute-start.1) | collective-permute-done | bytes 20512 | tf_op jit(solution)/shard_map/ppermute | solution.py:376
  30.4 1.9 %collective-permute-start.2 = (f32[50,128]{1,0:T(8,128)S(1)}, f32[50,128]{1,0:T(8,128)S(1)}, u32[]{:S(2)}, u32[]{:S(2)}) collective-permute-start(f32[50,128]{1,0:T(8,128)S(1)} %get-tuple-element.45), channel_id=1, source_target_pairs={{0,8},{16,24},{32,40},{48,56},{64,72},{80,88},{96,104},{112,120},{... | collective-permute-start | bytes 76808 | tf_op jit(solution)/shard_map/ppermute | solution.py:376
  32.3 3.0 %collective-permute-start.3 = (f32[50,128]{1,0:T(8,128)S(1)}, f32[50,128]{1,0:T(8,128)S(1)}, u32[]{:S(2)}, u32[]{:S(2)}) collective-permute-start(f32[50,128]{1,0:T(8,128)S(1)} %get-tuple-element.46), channel_id=1, source_target_pairs={{8,16},{24,32},{40,48},{56,64},{72,80},{88,96},{104,112},{120,128}... | collective-permute-start | bytes 76808 | tf_op jit(solution)/shard_map/ppermute | solution.py:376
  35.3 0.5 %shard_map.116.depth_ref = bf16[32,256,128]{2,1,0:T(8,128)(2,1)S(1)} custom-call(s32[32,128]{1,0:T(8,128)S(1)} %get-tuple-element.34.element_ref, f32[3,32,128]{2,1,0:T(8,128)S(1)} %get-tuple-element.35.coords_ref), custom_call_target="tpu_custom_call" | custom-call | tf_op jit(solution)/shard_map/pallas_call | solution.py:363
  35.8 0.0 collective-permute-done.2.even_x_ref
  35.8 3.8 %collective-permute-done.3.odd_x_ref = f32[50,128]{1,0:T(8,128)S(1)} collective-permute-done((f32[50,128]{1,0:T(8,128)S(1)}, f32[50,128]{1,0:T(8,128)S(1)}, u32[]{:S(2)}, u32[]{:S(2)}) %collective-permute-start.3) | collective-permute-done | bytes 25632 | tf_op jit(solution)/shard_map/ppermute | solution.py:376
  39.6 0.6 %shard_map.118 = (f32[3,8,8,128]{3,2,1,0:T(8,128)S(1)}, f32[3,8,8,128]{3,2,1,0:T(8,128)S(1)}, f32[8,8,128]{2,1,0:T(8,128)S(1)}) custom-call(f32[3,8,8,128]{3,2,1,0:T(8,128)S(1)} %get-tuple-element.38.u_ref, f32[3,8,8,128]{3,2,1,0:T(8,128)S(1)} %get-tuple-element.39.velocity_ref, f32[3,8,8,128]{3,2,1,0:T(8,128)S(1)} %get-tuple-element.40.load_ref, ...), custom_call_target="tpu_custom_call" | custom-call | tf_op jit(solution)/shard_map/pallas_call | solution.py:363
  40.1 0.0 all-to-all-done.1
  40.2 1.7 %shard_map.119 = (f32[3,8,8,128]{3,2,1,0:T(8,128)}, f32[3,8,8,128]{3,2,1,0:T(8,128)}) custom-call(f32[128,128]{1,0:T(8,128)S(1)} %bitcast.11, bf16[32,256,128]{2,1,0:T(8,128)(2,1)S(1)} %shard_map.116.depth_ref, f32[8,32,128]{2,1,0:T(8,128)S(1)} %get-tuple-element.36.weight_x_ref, f32[32,8,128]{2,1,0:T(8,128)S(1)} %get-tuple-element.37.weight_y_ref, ...), custom_call_target="tpu_custom_call" | custom-call | tf_op jit(solution)/shard_map/pallas_call | solution.py:363
  (1 shorter events, 0.0 us)
Async XLA Ops:
  3.3 13.6 %all-to-all-start = ((f32[32,4,128]{2,1,0:T(4,128)}), f32[32,4,128]{2,1,0:T(4,128)S(1)}, u32[]{:S(2)}, u32[]{:S(2)}) async-start(f32[32,4,128]{2,1,0:T(4,128)} %bitcast.6), calls=%async_computation | async-start | bytes 131072 | tf_op jit(solution)/shard_map/all_to_all | solution.py:381
  18.2 21.9 %all-to-all-start.1 = ((f32[32,4,128]{2,1,0:T(4,128)}), f32[32,4,128]{2,1,0:T(4,128)S(1)}, u32[]{:S(2)}, u32[]{:S(2)}) async-start(f32[32,4,128]{2,1,0:T(4,128)} %bitcast.8), calls=%async_computation.1 | async-start | bytes 131072 | tf_op jit(solution)/shard_map/all_to_all | solution.py:381
  23.8 3.0 %collective-permute-start = (f32[5,8,128]{2,1,0:T(8,128)S(1)}, f32[5,8,128]{2,1,0:T(8,128)S(1)}, u32[]{:S(2)}, u32[]{:S(2)}) collective-permute-start(f32[5,8,128]{2,1,0:T(8,128)S(1)} %get-tuple-element.43), channel_id=1, source_target_pairs={{0,1},{2,3},{4,5},{6,7},{1,0},{3,2},{5,4},{7,6},{8,9},{10,11},{12,... | collective-permute-start | bytes 61448 | tf_op jit(solution)/shard_map/ppermute | solution.py:376
  24.6 5.7 %collective-permute-start.1 = (f32[5,8,128]{2,1,0:T(8,128)S(1)}, f32[5,8,128]{2,1,0:T(8,128)S(1)}, u32[]{:S(2)}, u32[]{:S(2)}) collective-permute-start(f32[5,8,128]{2,1,0:T(8,128)S(1)} %get-tuple-element.44), channel_id=1, source_target_pairs={{1,2},{3,4},{5,6},{2,1},{4,3},{6,5},{9,10},{11,12},{13,14},{10,9},... | collective-permute-start | bytes 61448 | tf_op jit(solution)/shard_map/ppermute | solution.py:376
  30.4 5.4 %collective-permute-start.2 = (f32[50,128]{1,0:T(8,128)S(1)}, f32[50,128]{1,0:T(8,128)S(1)}, u32[]{:S(2)}, u32[]{:S(2)}) collective-permute-start(f32[50,128]{1,0:T(8,128)S(1)} %get-tuple-element.45), channel_id=1, source_target_pairs={{0,8},{16,24},{32,40},{48,56},{64,72},{80,88},{96,104},{112,120},{... | collective-permute-start | bytes 76808 | tf_op jit(solution)/shard_map/ppermute | solution.py:376
  32.3 7.3 %collective-permute-start.3 = (f32[50,128]{1,0:T(8,128)S(1)}, f32[50,128]{1,0:T(8,128)S(1)}, u32[]{:S(2)}, u32[]{:S(2)}) collective-permute-start(f32[50,128]{1,0:T(8,128)S(1)} %get-tuple-element.46), channel_id=1, source_target_pairs={{8,16},{24,32},{40,48},{56,64},{72,80},{88,96},{104,112},{120,128}... | collective-permute-start | bytes 76808 | tf_op jit(solution)/shard_map/ppermute | solution.py:376

commit v4 on v3

--- a/solution.py
+++ b/solution.py
@@ -114,12 +114,12 @@
         factor = factor + jnp.where(kind == float(index), value, 0.0)
     density = density_ref[...]
     modulus_ref[...] = factor[None] * density * density
-    odd_blk = odd_blk_index()
+    odd_dom = odd_dom_index()
     for comp in range(5):
         source = modulus_ref if comp == 3 else density_ref if comp == 4 else u_ref.at[comp]
-        first, last = source[:, 0, :], source[:, 7, :]
-        even_ref[comp] = jnp.where(odd_blk, first, last)
-        odd_ref[comp] = jnp.where(odd_blk, last, first)
+        first, last = source[0], source[7]
+        even_ref[comp] = jnp.where(odd_dom, first, last)
+        odd_ref[comp] = jnp.where(odd_dom, last, first)
     for copy in copies[5:]:
         copy.wait()
 
@@ -203,18 +203,26 @@
         pulls_ref[pl.ds(32 * block + 3, 8, stride=4), :] = jnp.zeros((8, LANES), F32)
 
 
-def sides_kernel(u_ref, density_ref, modulus_ref, even_y_ref, odd_y_ref, even_ref, odd_ref):
-    odd_dom, odd_blk = odd_dom_index(), odd_blk_index()
+def sides_kernel(
+    u_ref, density_ref, modulus_ref, even_in_ref, odd_in_ref, even_ref, odd_swap_ref
+):
+    odd_dom = odd_dom_index()
+    odd_blk = odd_blk_index()
     for comp in range(5):
-        left = jnp.where(odd_blk, even_y_ref[comp], odd_y_ref[comp])
-        right = jnp.where(odd_blk, odd_y_ref[comp], even_y_ref[comp])
-        source = modulus_ref if comp == 3 else density_ref if comp == 4 else u_ref.at[comp]
-        first, last = (
-            jnp.concatenate([left[at : at + 1], source[at], right[at : at + 1]], axis=0)
-            for at in (0, 7)
-        )
-        even_ref[pl.ds(10 * comp, 10), :] = jnp.where(odd_dom, first, last)
-        odd_ref[pl.ds(10 * comp, 10), :] = jnp.where(odd_dom, last, first)
+        lower = jnp.where(odd_dom, even_in_ref[comp], odd_in_ref[comp])
+        upper = jnp.where(odd_dom, odd_in_ref[comp], even_in_ref[comp])
+        rows = []
+        for at in (0, 7):
+            if comp < 3:
+                own = u_ref[comp, :, at, :]
+            else:
+                own = (modulus_ref if comp == 3 else density_ref)[:, at, :]
+            rows.append(
+                jnp.concatenate([lower[at : at + 1], own, upper[at : at + 1]], axis=0)
+            )
+        first, last = rows
+        even_ref[pl.ds(10 * comp, 10), :] = jnp.where(odd_blk, first, last)
+        odd_swap_ref[pl.ds(10 * comp, 10), :] = jnp.where(odd_blk, last, first)
 
 
 def elastic_kernel(
@@ -227,16 +235,23 @@
     odd_blk = odd_blk_index()
     for comp in range(5):
         nodes_ref[comp, pl.ds(96, 24), :] = jnp.zeros((24, LANES), F32)
-        even, odd = even_x_ref[pl.ds(10 * comp, 10), :], odd_x_ref[pl.ds(10 * comp, 10), :]
-        nodes_ref[comp, pl.ds(0, 10), :] = jnp.where(odd_dom, even, odd)
-        nodes_ref[comp, pl.ds(90, 10), :] = jnp.where(odd_dom, odd, even)
-        left = jnp.where(odd_blk, even_y_ref[comp], odd_y_ref[comp])
-        right = jnp.where(odd_blk, odd_y_ref[comp], even_y_ref[comp])
-        source = modulus_ref if comp == 3 else density_ref if comp == 4 else u_ref.at[comp]
+        lower = jnp.where(odd_dom, even_x_ref[comp], odd_x_ref[comp])
+        upper = jnp.where(odd_dom, odd_x_ref[comp], even_x_ref[comp])
+        nodes_ref[comp, pl.ds(1, 8), :] = lower
+        nodes_ref[comp, pl.ds(91, 8), :] = upper
         for x in range(8):
-            nodes_ref[comp, pl.ds(10 * x + 10, 1), :] = left[x : x + 1]
-            nodes_ref[comp, pl.ds(10 * x + 11, 8), :] = source[x]
-            nodes_ref[comp, pl.ds(10 * x + 19, 1), :] = right[x : x + 1]
+            if comp < 3:
+                own = u_ref[comp, x]
+            else:
+                own = (modulus_ref if comp == 3 else density_ref)[x]
+            nodes_ref[comp, pl.ds(10 * x + 11, 8), :] = own
+        even = even_y_ref[pl.ds(10 * comp, 10), :]
+        odd = odd_y_ref[pl.ds(10 * comp, 10), :]
+        left = jnp.where(odd_blk, even, odd)
+        right = jnp.where(odd_blk, odd, even)
+        for x in range(10):
+            nodes_ref[comp, pl.ds(10 * x, 1), :] = left[x : x + 1]
+            nodes_ref[comp, pl.ds(10 * x + 9, 1), :] = right[x : x + 1]
     last_lane = iota((8, LANES), 1) == LANES - 1
     first_lane = iota((8, LANES), 1) == 0
     for comp in range(3):
@@ -401,7 +416,7 @@
         fibre_angles.reshape(2, 16, LANES),
         fibre_stiffness.reshape(1, 16),
     )
-    places, modulus, even_y, odd_y, weight_x, weight_y, *arguments = call(
+    places, modulus, even_x, odd_x, weight_x, weight_y, *arguments = call(
         interpolate_kernel,
         (
             ((128, LANES), F32), (plane, F32), ((5, 8, LANES), F32), ((5, 8, LANES), F32),
@@ -413,8 +428,8 @@
         first=True,
     )
     displacement, element, coords, density, _, velocity, load, slots, angles, stiffness = arguments
-    even_y = swap(even_y, "blk", 0)
-    odd_y = swap(odd_y, "blk", 1)
+    even_x = swap(even_x, DOM, 0)
+    odd_x = swap(odd_x, DOM, 1)
     received = exchange(places)
     table = ((32, LANES), jnp.int32)
     direction, stiff, fibre, node = call(
@@ -422,11 +437,11 @@
         (((3, 16, LANES), F32), ((16, LANES), F32), table, table),
         (slots, angles, stiffness),
     )
-    even_x, odd_x = call(
-        sides_kernel, (side, side), (displacement, density, modulus, even_y, odd_y)
-    )
-    even_x = swap(even_x, DOM, 0)
-    odd_x = swap(odd_x, DOM, 1)
+    even_y, odd_y = call(
+        sides_kernel, (side, side), (displacement, density, modulus, even_x, odd_x)
+    )
+    even_y = swap(even_y, "blk", 0)
+    odd_y = swap(odd_y, "blk", 1)
     (pulls,) = call(
         fibre_kernel, (((128, LANES), F32),),
         (received, slots, direction, stiff, fibre, node),

time: 42.2 us -> 41.6 us (0.986)
  the two profiles are of different devices: /device:TPU:135 before, /device:TPU:136 now
where the time goes in v4:
time: 41.6 us; the launch traced here: 41.3 us
  starting transfers between devices  20.3 us (49%)
  waiting for transfers between devices  13.1 us (31%)
  Pallas kernels  7.17 us (17%)
  between operations  0.71 us (2%)
    all_to_all x2, starting transfers between devices, exchange(): lax.all_to_all(blocks, DOM, split_axis=0, concat_axis=0, tiled=True)  12.5 us
    ppermute x4, starting transfers between devices, swap(): return lax.ppermute(shard, axis, pairs + [(b, a) for a, b in pairs])  7.77 us
    ppermute x4, waiting for transfers between devices, swap(): return lax.ppermute(shard, axis, pairs + [(b, a) for a, b in pairs])  7.18 us
    pallas_call x7, Pallas kernels, call(): pl.pallas_call(kernel, out_shape=outs, in_specs=[pl.BlockSpec(memory_spac...  7.17 us
    all_to_all x2, waiting for transfers between devices, exchange(): lax.all_to_all(blocks, DOM, split_axis=0, concat_axis=0, tiled=True)  5.95 us
  transfers between devices with their start and end apart: 6, of which 4 were waited for; matrix products, arithmetic and copies ran while one was open for 0% of the time, Pallas kernels for 3%

profile of v4, /device:TPU:136, one launch (start us, length us, event | category | flops | bytes accessed | tf_op | source)
XLA Modules:
  0.0 41.3 jit_solution(17756018471997148632)
XLA Ops:
  0.6 2.7 %shard_map.113 = (f32[128,128]{1,0:T(8,128)}, f32[8,8,128]{2,1,0:T(8,128)S(1)}, f32[5,8,128]{2,1,0:T(8,128)S(1)}, f32[5,8,128]{2,1,0:T(8,128)S(1)}, f32[8,32,128...) custom-call(f32[3,8,8,128]{3,2,1,0:T(8,128)} %refs_0_.1, ...), custom_call_target="tpu_custom_call" | custom-call | tf_op jit(solution)/shard_map/pallas_call | solution.py:378
  3.3 7.5 %all-to-all-start = ((f32[32,4,128]{2,1,0:T(4,128)}), f32[32,4,128]{2,1,0:T(4,128)S(1)}, u32[]{:S(2)}, u32[]{:S(2)}) async-start(f32[32,4,128]{2,1,0:T(4,128)} %bitcast.6), calls=%async_computation | async-start | bytes 131072 | tf_op jit(solution)/shard_map/all_to_all | solution.py:396
  10.9 0.4 shard_map.114
  11.2 5.9 %all-to-all-done = f32[32,4,128]{2,1,0:T(4,128)S(1)} async-done(((f32[32,4,128]{2,1,0:T(4,128)}), f32[32,4,128]{2,1,0:T(4,128)S(1)}, u32[]{:S(2)}, u32[]{:S(2)}) %all-to-all-start) | async-done | bytes 65568 | tf_op jit(solution)/shard_map/all_to_all | solution.py:396
  17.2 1.3 %shard_map.115 = f32[128,128]{1,0:T(8,128)} custom-call(f32[128,128]{1,0:T(8,128)S(1)} %bitcast.10, s32[16,128]{1,0:T(8,128)S(1)} %get-tuple-element.27.slots_ref, f32[3,16,128]{2,1,0:T(8,128)S(1)} %get-tuple-element.30.direction_ref, f32[16,128]{1,0:T(8,128)S(1)} %get-tuple-element.31.stiff_ref, s32[32,128]{1,0:T(8,128)S(1)} %get-tuple-element.32.fibre_ref, ...), custom_call_target="tpu_custom_call" | custom-call | tf_op jit(solution)/shard_map/pallas_call | solution.py:378
  18.5 5.0 %all-to-all-start.1 = ((f32[32,4,128]{2,1,0:T(4,128)}), f32[32,4,128]{2,1,0:T(4,128)S(1)}, u32[]{:S(2)}, u32[]{:S(2)}) async-start(f32[32,4,128]{2,1,0:T(4,128)} %bitcast.8), calls=%async_computation.1 | async-start | bytes 131072 | tf_op jit(solution)/shard_map/all_to_all | solution.py:396
  23.5 0.2 collective-permute-start
  23.7 4.5 %collective-permute-start.1 = (f32[5,8,128]{2,1,0:T(8,128)S(1)}, f32[5,8,128]{2,1,0:T(8,128)S(1)}, u32[]{:S(2)}, u32[]{:S(2)}) collective-permute-start(f32[5,8,128]{2,1,0:T(8,128)S(1)} %get-tuple-element.44), channel_id=1, source_target_pairs={{8,16},{24,32},{40,48},{56,64},{72,80},{88,96},{104,112},{120,128}... | collective-permute-start | bytes 61448 | tf_op jit(solution)/shard_map/ppermute | solution.py:391
  28.3 0.0 collective-permute-done.even_in_ref.even_x_ref
  28.3 2.6 %collective-permute-done.1.odd_in_ref.odd_x_ref = f32[5,8,128]{2,1,0:T(8,128)S(1)} collective-permute-done((f32[5,8,128]{2,1,0:T(8,128)S(1)}, f32[5,8,128]{2,1,0:T(8,128)S(1)}, u32[]{:S(2)}, u32[]{:S(2)}) %collective-permute-start.1) | collective-permute-done | bytes 20512 | tf_op jit(solution)/shard_map/ppermute | solution.py:391
  30.9 1.1 %collective-permute-start.2 = (f32[50,128]{1,0:T(8,128)S(1)}, f32[50,128]{1,0:T(8,128)S(1)}, u32[]{:S(2)}, u32[]{:S(2)}) collective-permute-start(f32[50,128]{1,0:T(8,128)S(1)} %get-tuple-element.45), channel_id=1, source_target_pairs={{0,1},{2,3},{4,5},{6,7},{1,0},{3,2},{5,4},{7,6},{8,9},{10,11},{12,... | collective-permute-start | bytes 76808 | tf_op jit(solution)/shard_map/ppermute | solution.py:391
  32.0 1.9 %collective-permute-start.3 = (f32[50,128]{1,0:T(8,128)S(1)}, f32[50,128]{1,0:T(8,128)S(1)}, u32[]{:S(2)}, u32[]{:S(2)}) collective-permute-start(f32[50,128]{1,0:T(8,128)S(1)} %get-tuple-element.46), channel_id=1, source_target_pairs={{1,2},{3,4},{5,6},{2,1},{4,3},{6,5},{9,10},{11,12},{13,14},{10,9},... | collective-permute-start | bytes 76808 | tf_op jit(solution)/shard_map/ppermute | solution.py:391
  34.0 0.5 %shard_map.116.depth_ref = bf16[32,256,128]{2,1,0:T(8,128)(2,1)S(1)} custom-call(s32[32,128]{1,0:T(8,128)S(1)} %get-tuple-element.34.element_ref, f32[3,32,128]{2,1,0:T(8,128)S(1)} %get-tuple-element.35.coords_ref), custom_call_target="tpu_custom_call" | custom-call | tf_op jit(solution)/shard_map/pallas_call | solution.py:378
  34.5 0.4 %collective-permute-done.2.even_y_ref = f32[50,128]{1,0:T(8,128)S(1)} collective-permute-done((f32[50,128]{1,0:T(8,128)S(1)}, f32[50,128]{1,0:T(8,128)S(1)}, u32[]{:S(2)}, u32[]{:S(2)}) %collective-permute-start.2) | collective-permute-done | bytes 25632 | tf_op jit(solution)/shard_map/ppermute | solution.py:391
  34.9 4.1 %collective-permute-done.3.odd_y_ref = f32[50,128]{1,0:T(8,128)S(1)} collective-permute-done((f32[50,128]{1,0:T(8,128)S(1)}, f32[50,128]{1,0:T(8,128)S(1)}, u32[]{:S(2)}, u32[]{:S(2)}) %collective-permute-start.3) | collective-permute-done | bytes 25632 | tf_op jit(solution)/shard_map/ppermute | solution.py:391
  39.0 0.6 %shard_map.118 = (f32[3,8,8,128]{3,2,1,0:T(8,128)S(1)}, f32[3,8,8,128]{3,2,1,0:T(8,128)S(1)}, f32[8,8,128]{2,1,0:T(8,128)S(1)}) custom-call(f32[3,8,8,128]{3,2,1,0:T(8,128)S(1)} %get-tuple-element.38.u_ref, f32[3,8,8,128]{3,2,1,0:T(8,128)S(1)} %get-tuple-element.39.velocity_ref, f32[3,8,8,128]{3,2,1,0:T(8,128)S(1)} %get-tuple-element.40.load_ref, ...), custom_call_target="tpu_custom_call" | custom-call | tf_op jit(solution)/shard_map/pallas_call | solution.py:378
  39.6 0.0 all-to-all-done.1
  39.6 1.7 %shard_map.119 = (f32[3,8,8,128]{3,2,1,0:T(8,128)}, f32[3,8,8,128]{3,2,1,0:T(8,128)}) custom-call(f32[128,128]{1,0:T(8,128)S(1)} %bitcast.11, bf16[32,256,128]{2,1,0:T(8,128)(2,1)S(1)} %shard_map.116.depth_ref, f32[8,32,128]{2,1,0:T(8,128)S(1)} %get-tuple-element.36.weight_x_ref, f32[32,8,128]{2,1,0:T(8,128)S(1)} %get-tuple-element.37.weight_y_ref, ...), custom_call_target="tpu_custom_call" | custom-call | tf_op jit(solution)/shard_map/pallas_call | solution.py:378
  (1 shorter events, 0.0 us)
Async XLA Ops:
  3.3 13.9 %all-to-all-start = ((f32[32,4,128]{2,1,0:T(4,128)}), f32[32,4,128]{2,1,0:T(4,128)S(1)}, u32[]{:S(2)}, u32[]{:S(2)}) async-start(f32[32,4,128]{2,1,0:T(4,128)} %bitcast.6), calls=%async_computation | async-start | bytes 131072 | tf_op jit(solution)/shard_map/all_to_all | solution.py:396
  18.5 21.0 %all-to-all-start.1 = ((f32[32,4,128]{2,1,0:T(4,128)}), f32[32,4,128]{2,1,0:T(4,128)S(1)}, u32[]{:S(2)}, u32[]{:S(2)}) async-start(f32[32,4,128]{2,1,0:T(4,128)} %bitcast.8), calls=%async_computation.1 | async-start | bytes 131072 | tf_op jit(solution)/shard_map/all_to_all | solution.py:396
  23.5 4.8 %collective-permute-start = (f32[5,8,128]{2,1,0:T(8,128)S(1)}, f32[5,8,128]{2,1,0:T(8,128)S(1)}, u32[]{:S(2)}, u32[]{:S(2)}) collective-permute-start(f32[5,8,128]{2,1,0:T(8,128)S(1)} %get-tuple-element.43), channel_id=1, source_target_pairs={{0,8},{16,24},{32,40},{48,56},{64,72},{80,88},{96,104},{112,120},{... | collective-permute-start | bytes 61448 | tf_op jit(solution)/shard_map/ppermute | solution.py:391
  23.7 7.2 %collective-permute-start.1 = (f32[5,8,128]{2,1,0:T(8,128)S(1)}, f32[5,8,128]{2,1,0:T(8,128)S(1)}, u32[]{:S(2)}, u32[]{:S(2)}) collective-permute-start(f32[5,8,128]{2,1,0:T(8,128)S(1)} %get-tuple-element.44), channel_id=1, source_target_pairs={{8,16},{24,32},{40,48},{56,64},{72,80},{88,96},{104,112},{120,128}... | collective-permute-start | bytes 61448 | tf_op jit(solution)/shard_map/ppermute | solution.py:391
  30.9 4.0 %collective-permute-start.2 = (f32[50,128]{1,0:T(8,128)S(1)}, f32[50,128]{1,0:T(8,128)S(1)}, u32[]{:S(2)}, u32[]{:S(2)}) collective-permute-start(f32[50,128]{1,0:T(8,128)S(1)} %get-tuple-element.45), channel_id=1, source_target_pairs={{0,1},{2,3},{4,5},{6,7},{1,0},{3,2},{5,4},{7,6},{8,9},{10,11},{12,... | collective-permute-start | bytes 76808 | tf_op jit(solution)/shard_map/ppermute | solution.py:391
  32.0 7.0 %collective-permute-start.3 = (f32[50,128]{1,0:T(8,128)S(1)}, f32[50,128]{1,0:T(8,128)S(1)}, u32[]{:S(2)}, u32[]{:S(2)}) collective-permute-start(f32[50,128]{1,0:T(8,128)S(1)} %get-tuple-element.46), channel_id=1, source_target_pairs={{1,2},{3,4},{5,6},{2,1},{4,3},{6,5},{9,10},{11,12},{13,14},{10,9},... | collective-permute-start | bytes 76808 | tf_op jit(solution)/shard_map/ppermute | solution.py:391

commit v5 on v4

--- a/solution.py
+++ b/solution.py
@@ -26,6 +26,15 @@
 
 def odd_blk_index():
     return (lax.axis_index("blk") & 1) == 1
+
+
+def at_end(axis):
+    axes = axis if isinstance(axis, tuple) else (axis,)
+    index, size = 0, 1
+    for name in axes:
+        index = index * lax.axis_size(name) + lax.axis_index(name)
+        size *= lax.axis_size(name)
+    return (index == 0) | (index == size - 1)
 
 
 def split(value):
@@ -114,12 +123,12 @@
         factor = factor + jnp.where(kind == float(index), value, 0.0)
     density = density_ref[...]
     modulus_ref[...] = factor[None] * density * density
-    odd_dom = odd_dom_index()
+    odd_dom, end = odd_dom_index(), at_end(DOM)
     for comp in range(5):
         source = modulus_ref if comp == 3 else density_ref if comp == 4 else u_ref.at[comp]
         first, last = source[0], source[7]
         even_ref[comp] = jnp.where(odd_dom, first, last)
-        odd_ref[comp] = jnp.where(odd_dom, last, first)
+        odd_ref[comp] = jnp.where(end, 0.0, jnp.where(odd_dom, last, first))
     for copy in copies[5:]:
         copy.wait()
 
@@ -207,7 +216,7 @@
     u_ref, density_ref, modulus_ref, even_in_ref, odd_in_ref, even_ref, odd_swap_ref
 ):
     odd_dom = odd_dom_index()
-    odd_blk = odd_blk_index()
+    odd_blk, end = odd_blk_index(), at_end("blk")
     for comp in range(5):
         lower = jnp.where(odd_dom, even_in_ref[comp], odd_in_ref[comp])
         upper = jnp.where(odd_dom, odd_in_ref[comp], even_in_ref[comp])
@@ -222,7 +231,9 @@
             )
         first, last = rows
         even_ref[pl.ds(10 * comp, 10), :] = jnp.where(odd_blk, first, last)
-        odd_swap_ref[pl.ds(10 * comp, 10), :] = jnp.where(odd_blk, last, first)
+        odd_swap_ref[pl.ds(10 * comp, 10), :] = jnp.where(
+            end, 0.0, jnp.where(odd_blk, last, first)
+        )
 
 
 def elastic_kernel(
@@ -386,9 +397,20 @@
 
 
 def swap(shard, axis, first):
-    size = lax.axis_size(axis)
-    pairs = [(i, i + 1) for i in range(first, size - 1, 2)]
-    return lax.ppermute(shard, axis, pairs + [(b, a) for a, b in pairs])
+    doms = lax.axis_size(DOM)
+    blks = lax.axis_size("blk")
+    pairs = []
+    for dom in range(doms):
+        for blk in range(blks):
+            at, size = (blk, blks) if axis == "blk" else (dom, doms)
+            low = (at - first) % 2 == 0
+            move = 1 if low else -1
+            along_blk = (axis == "blk") == (0 <= at + move < size)
+            if not 0 <= at + move < size:
+                move = 1 if (dom if axis == "blk" else blk) % 2 == 0 else -1
+            target = (dom, blk + move) if along_blk else (dom + move, blk)
+            pairs.append((dom * blks + blk, target[0] * blks + target[1]))
+    return lax.ppermute(shard, (*DOM, "blk"), pairs)
 
 
 def exchange(rows):

time: 41.6 us -> 37.8 us (0.909)
  starting transfers between devices: 20.3 us -> 16.5 us
    ppermute x4, starting transfers between devices: 7.77 us -> 3.97 us  [swap(): return lax.ppermute(shard, (*DOM, 'blk'), pairs)]
  transfers between devices with their start and end apart: 6 -> 6, of which waited for: 4 -> 4; matrix products, arithmetic and copies ran while one was open for 0% -> 0% of each run, Pallas kernels for 3% -> 4%
where the time goes in v5:
time: 37.8 us; the launch traced here: 37.5 us
  starting transfers between devices  16.5 us (44%)
  waiting for transfers between devices  13.2 us (35%)
  Pallas kernels  7.17 us (19%)
  between operations  0.69 us (2%)
    all_to_all x2, starting transfers between devices, exchange(): lax.all_to_all(blocks, DOM, split_axis=0, concat_axis=0, tiled=True)  12.5 us
    ppermute x4, waiting for transfers between devices, swap(): return lax.ppermute(shard, (*DOM, 'blk'), pairs)  7.25 us
    pallas_call x7, Pallas kernels, call(): pl.pallas_call(kernel, out_shape=outs, in_specs=[pl.BlockSpec(memory_spac...  7.17 us
    all_to_all x2, waiting for transfers between devices, exchange(): lax.all_to_all(blocks, DOM, split_axis=0, concat_axis=0, tiled=True)  5.95 us
    ppermute x4, starting transfers between devices, swap(): return lax.ppermute(shard, (*DOM, 'blk'), pairs)  3.97 us
  transfers between devices with their start and end apart: 6, of which 4 were waited for; matrix products, arithmetic and copies ran while one was open for 0% of the time, Pallas kernels for 4%

profile of v5, /device:TPU:136, one launch (start us, length us, event | category | flops | bytes accessed | tf_op | source)
XLA Modules:
  0.0 37.5 jit_solution(15719124566791029215)
XLA Ops:
  0.6 2.7 %shard_map.113 = (f32[128,128]{1,0:T(8,128)}, f32[8,8,128]{2,1,0:T(8,128)S(1)}, f32[5,8,128]{2,1,0:T(8,128)S(1)}, f32[5,8,128]{2,1,0:T(8,128)S(1)}, f32[8,32,128...) custom-call(f32[3,8,8,128]{3,2,1,0:T(8,128)} %refs_0_.1, ...), custom_call_target="tpu_custom_call" | custom-call | tf_op jit(solution)/shard_map/pallas_call | solution.py:389
  3.3 7.5 %all-to-all-start = ((f32[32,4,128]{2,1,0:T(4,128)}), f32[32,4,128]{2,1,0:T(4,128)S(1)}, u32[]{:S(2)}, u32[]{:S(2)}) async-start(f32[32,4,128]{2,1,0:T(4,128)} %bitcast.6), calls=%async_computation | async-start | bytes 131072 | tf_op jit(solution)/shard_map/all_to_all | solution.py:418
  10.9 0.4 shard_map.114
  11.2 5.9 %all-to-all-done = f32[32,4,128]{2,1,0:T(4,128)S(1)} async-done(((f32[32,4,128]{2,1,0:T(4,128)}), f32[32,4,128]{2,1,0:T(4,128)S(1)}, u32[]{:S(2)}, u32[]{:S(2)}) %all-to-all-start) | async-done | bytes 65568 | tf_op jit(solution)/shard_map/all_to_all | solution.py:418
  17.2 1.3 %shard_map.115 = f32[128,128]{1,0:T(8,128)} custom-call(f32[128,128]{1,0:T(8,128)S(1)} %bitcast.10, s32[16,128]{1,0:T(8,128)S(1)} %get-tuple-element.27.slots_ref, f32[3,16,128]{2,1,0:T(8,128)S(1)} %get-tuple-element.30.direction_ref, f32[16,128]{1,0:T(8,128)S(1)} %get-tuple-element.31.stiff_ref, s32[32,128]{1,0:T(8,128)S(1)} %get-tuple-element.32.fibre_ref, ...), custom_call_target="tpu_custom_call" | custom-call | tf_op jit(solution)/shard_map/pallas_call | solution.py:389
  18.5 5.0 %all-to-all-start.1 = ((f32[32,4,128]{2,1,0:T(4,128)}), f32[32,4,128]{2,1,0:T(4,128)S(1)}, u32[]{:S(2)}, u32[]{:S(2)}) async-start(f32[32,4,128]{2,1,0:T(4,128)} %bitcast.8), calls=%async_computation.1 | async-start | bytes 131072 | tf_op jit(solution)/shard_map/all_to_all | solution.py:418
  23.5 0.2 collective-permute-start
  23.7 2.7 %collective-permute-start.1 = (f32[5,8,128]{2,1,0:T(8,128)S(1)}, f32[5,8,128]{2,1,0:T(8,128)S(1)}, u32[]{:S(2)}, u32[]{:S(2)}) collective-permute-start(f32[5,8,128]{2,1,0:T(8,128)S(1)} %get-tuple-element.44), channel_id=1, source_target_pairs={{0,1},{1,0},{2,3},{3,2},{4,5},{5,4},{6,7},{7,6},{8,16},{9,17},{10,... | collective-permute-start | bytes 61448 | tf_op jit(solution)/shard_map/ppermute | solution.py:413
  26.3 0.0 collective-permute-done.even_in_ref.even_x_ref
  26.3 2.7 %collective-permute-done.1.odd_in_ref.odd_x_ref = f32[5,8,128]{2,1,0:T(8,128)S(1)} collective-permute-done((f32[5,8,128]{2,1,0:T(8,128)S(1)}, f32[5,8,128]{2,1,0:T(8,128)S(1)}, u32[]{:S(2)}, u32[]{:S(2)}) %collective-permute-start.1) | collective-permute-done | bytes 20512 | tf_op jit(solution)/shard_map/ppermute | solution.py:413
  29.0 1.1 %collective-permute-start.2 = (f32[50,128]{1,0:T(8,128)S(1)}, f32[50,128]{1,0:T(8,128)S(1)}, u32[]{:S(2)}, u32[]{:S(2)}) collective-permute-start(f32[50,128]{1,0:T(8,128)S(1)} %get-tuple-element.45), channel_id=1, source_target_pairs={{0,1},{1,0},{2,3},{3,2},{4,5},{5,4},{6,7},{7,6},{8,9},{9,8},{10,11... | collective-permute-start | bytes 76808 | tf_op jit(solution)/shard_map/ppermute | solution.py:413
  30.2 0.0 collective-permute-start.3
  30.2 0.5 %shard_map.116.depth_ref = bf16[32,256,128]{2,1,0:T(8,128)(2,1)S(1)} custom-call(s32[32,128]{1,0:T(8,128)S(1)} %get-tuple-element.34.element_ref, f32[3,32,128]{2,1,0:T(8,128)S(1)} %get-tuple-element.35.coords_ref), custom_call_target="tpu_custom_call" | custom-call | tf_op jit(solution)/shard_map/pallas_call | solution.py:389
  30.7 2.4 %collective-permute-done.2.even_y_ref = f32[50,128]{1,0:T(8,128)S(1)} collective-permute-done((f32[50,128]{1,0:T(8,128)S(1)}, f32[50,128]{1,0:T(8,128)S(1)}, u32[]{:S(2)}, u32[]{:S(2)}) %collective-permute-start.2) | collective-permute-done | bytes 25632 | tf_op jit(solution)/shard_map/ppermute | solution.py:413
  33.0 2.2 %collective-permute-done.3.odd_y_ref = f32[50,128]{1,0:T(8,128)S(1)} collective-permute-done((f32[50,128]{1,0:T(8,128)S(1)}, f32[50,128]{1,0:T(8,128)S(1)}, u32[]{:S(2)}, u32[]{:S(2)}) %collective-permute-start.3) | collective-permute-done | bytes 25632 | tf_op jit(solution)/shard_map/ppermute | solution.py:413
  35.2 0.6 %shard_map.118 = (f32[3,8,8,128]{3,2,1,0:T(8,128)S(1)}, f32[3,8,8,128]{3,2,1,0:T(8,128)S(1)}, f32[8,8,128]{2,1,0:T(8,128)S(1)}) custom-call(f32[3,8,8,128]{3,2,1,0:T(8,128)S(1)} %get-tuple-element.38.u_ref, f32[3,8,8,128]{3,2,1,0:T(8,128)S(1)} %get-tuple-element.39.velocity_ref, f32[3,8,8,128]{3,2,1,0:T(8,128)S(1)} %get-tuple-element.40.load_ref, ...), custom_call_target="tpu_custom_call" | custom-call | tf_op jit(solution)/shard_map/pallas_call | solution.py:389
  35.8 0.0 all-to-all-done.1
  35.8 1.7 %shard_map.119 = (f32[3,8,8,128]{3,2,1,0:T(8,128)}, f32[3,8,8,128]{3,2,1,0:T(8,128)}) custom-call(f32[128,128]{1,0:T(8,128)S(1)} %bitcast.11, bf16[32,256,128]{2,1,0:T(8,128)(2,1)S(1)} %shard_map.116.depth_ref, f32[8,32,128]{2,1,0:T(8,128)S(1)} %get-tuple-element.36.weight_x_ref, f32[32,8,128]{2,1,0:T(8,128)S(1)} %get-tuple-element.37.weight_y_ref, ...), custom_call_target="tpu_custom_call" | custom-call | tf_op jit(solution)/shard_map/pallas_call | solution.py:389
  (1 shorter events, 0.0 us)
Async XLA Ops:
  3.3 13.9 %all-to-all-start = ((f32[32,4,128]{2,1,0:T(4,128)}), f32[32,4,128]{2,1,0:T(4,128)S(1)}, u32[]{:S(2)}, u32[]{:S(2)}) async-start(f32[32,4,128]{2,1,0:T(4,128)} %bitcast.6), calls=%async_computation | async-start | bytes 131072 | tf_op jit(solution)/shard_map/all_to_all | solution.py:418
  18.5 17.3 %all-to-all-start.1 = ((f32[32,4,128]{2,1,0:T(4,128)}), f32[32,4,128]{2,1,0:T(4,128)S(1)}, u32[]{:S(2)}, u32[]{:S(2)}) async-start(f32[32,4,128]{2,1,0:T(4,128)} %bitcast.8), calls=%async_computation.1 | async-start | bytes 131072 | tf_op jit(solution)/shard_map/all_to_all | solution.py:418
  23.5 2.9 %collective-permute-start = (f32[5,8,128]{2,1,0:T(8,128)S(1)}, f32[5,8,128]{2,1,0:T(8,128)S(1)}, u32[]{:S(2)}, u32[]{:S(2)}) collective-permute-start(f32[5,8,128]{2,1,0:T(8,128)S(1)} %get-tuple-element.43), channel_id=1, source_target_pairs={{0,8},{1,9},{2,10},{3,11},{4,12},{5,13},{6,14},{7,15},{8,0},{9,1},... | collective-permute-start | bytes 61448 | tf_op jit(solution)/shard_map/ppermute | solution.py:413
  23.7 5.3 %collective-permute-start.1 = (f32[5,8,128]{2,1,0:T(8,128)S(1)}, f32[5,8,128]{2,1,0:T(8,128)S(1)}, u32[]{:S(2)}, u32[]{:S(2)}) collective-permute-start(f32[5,8,128]{2,1,0:T(8,128)S(1)} %get-tuple-element.44), channel_id=1, source_target_pairs={{0,1},{1,0},{2,3},{3,2},{4,5},{5,4},{6,7},{7,6},{8,16},{9,17},{10,... | collective-permute-start | bytes 61448 | tf_op jit(solution)/shard_map/ppermute | solution.py:413
  29.0 4.0 %collective-permute-start.2 = (f32[50,128]{1,0:T(8,128)S(1)}, f32[50,128]{1,0:T(8,128)S(1)}, u32[]{:S(2)}, u32[]{:S(2)}) collective-permute-start(f32[50,128]{1,0:T(8,128)S(1)} %get-tuple-element.45), channel_id=1, source_target_pairs={{0,1},{1,0},{2,3},{3,2},{4,5},{5,4},{6,7},{7,6},{8,9},{9,8},{10,11... | collective-permute-start | bytes 76808 | tf_op jit(solution)/shard_map/ppermute | solution.py:413
  30.2 5.1 %collective-permute-start.3 = (f32[50,128]{1,0:T(8,128)S(1)}, f32[50,128]{1,0:T(8,128)S(1)}, u32[]{:S(2)}, u32[]{:S(2)}) collective-permute-start(f32[50,128]{1,0:T(8,128)S(1)} %get-tuple-element.46), channel_id=1, source_target_pairs={{0,8},{1,2},{2,1},{3,4},{4,3},{5,6},{6,5},{7,15},{8,0},{9,10},{10,... | collective-permute-start | bytes 76808 | tf_op jit(solution)/shard_map/ppermute | solution.py:413

commit v6 on v5

--- a/solution.py
+++ b/solution.py
@@ -16,6 +16,7 @@
 F32 = jnp.float32
 BF16 = jnp.bfloat16
 LANES = 128
+GATHERED = (2, 5, 8, 11, 14)
 ROWS = 104
 ROWS_PAD = 120
 
@@ -66,6 +67,15 @@
         upper = jnp.broadcast_to(upper.astype(F32), shape).astype(BF16)
         parts.append(jnp.where(here, lower, jnp.where(above, upper, zero)))
     return parts
+
+
+def gathered(field_ref, index, rows):
+    return [
+        sum(
+            jnp.take_along_axis(field_ref[comp, x], index, axis=1) * rows[x] for x in range(8)
+        )
+        for comp in range(3)
+    ]
 
 
 def interpolate_kernel(*refs):
@@ -91,25 +101,39 @@
     field_high, field_low = split(u_ref[...].reshape(192, LANES))
     field = jnp.concatenate([field_high, field_low, field_high], axis=1)
     for pair in range(16):
-        parts = []
-        for owner in (2 * pair, 2 * pair + 1):
-            row = pl.ds(owner, 1)
-            high, low = depth_weights(element_ref[row, :], coords_ref[2, row, :])
-            parts.append(jnp.concatenate([high, high, low], axis=0))
-        sums = jnp.dot(field, jnp.concatenate(parts, axis=1), preferred_element_type=F32)
+        by_gather = pair in GATHERED
+        if not by_gather:
+            parts = []
+            for owner in (2 * pair, 2 * pair + 1):
+                row = pl.ds(owner, 1)
+                high, low = depth_weights(element_ref[row, :], coords_ref[2, row, :])
+                parts.append(jnp.concatenate([high, high, low], axis=0))
+            sums = jnp.dot(field, jnp.concatenate(parts, axis=1), preferred_element_type=F32)
         for half in range(2):
             owner = 2 * pair + half
             row = pl.ds(owner, 1)
-            weight_y = hat((element_ref[row, :] >> 7) & 7, coords_ref[1, row, :], 8)
+            element = element_ref[row, :]
+            weight_y = hat((element >> 7) & 7, coords_ref[1, row, :], 8)
             weight_y_ref[owner] = weight_y
             rows = [weight_x_ref[x, row, :] for x in range(8)]
+            if by_gather:
+                index = jnp.broadcast_to(element & (LANES - 1), (8, LANES))
+                lower = gathered(u_ref, index, rows)
+                upper = gathered(u_ref, index + 1, rows)
+                along = coords_ref[2, row, :]
+                totals = [low + along * (high - low) for low, high in zip(lower, upper)]
+            else:
+                totals = [
+                    sum(
+                        sums[64 * comp + 8 * x :, LANES * half : LANES * half + LANES][:8]
+                        * rows[x]
+                        for x in range(8)
+                    )
+                    for comp in range(3)
+                ]
             for comp in range(3):
-                total = sum(
-                    sums[64 * comp + 8 * x :, LANES * half : LANES * half + LANES][:8] * rows[x]
-                    for x in range(8)
-                )
                 places_ref[pl.ds(4 * owner + comp, 1), :] = jnp.sum(
-                    total * weight_y, axis=0, keepdims=True
+                    totals[comp] * weight_y, axis=0, keepdims=True
                 )
             places_ref[pl.ds(4 * owner + 3, 1), :] = jnp.zeros((1, LANES), F32)
 

time: 37.8 us -> 37.5 us (level)
  no operation moved by 1% of the time
where the time goes in v6:
time: 37.5 us; the launch traced here: 37.3 us
  starting transfers between devices  16.5 us (44%)
  waiting for transfers between devices  13.2 us (35%)
  Pallas kernels  6.96 us (19%)
  between operations  0.69 us (2%)
    all_to_all x2, starting transfers between devices, exchange(): lax.all_to_all(blocks, DOM, split_axis=0, concat_axis=0, tiled=True)  12.5 us
    ppermute x4, waiting for transfers between devices, swap(): return lax.ppermute(shard, (*DOM, 'blk'), pairs)  7.25 us
    pallas_call x7, Pallas kernels, call(): pl.pallas_call(kernel, out_shape=outs, in_specs=[pl.BlockSpec(memory_spac...  6.96 us
    all_to_all x2, waiting for transfers between devices, exchange(): lax.all_to_all(blocks, DOM, split_axis=0, concat_axis=0, tiled=True)  5.95 us
    ppermute x4, starting transfers between devices, swap(): return lax.ppermute(shard, (*DOM, 'blk'), pairs)  3.97 us
  transfers between devices with their start and end apart: 6, of which 4 were waited for; matrix products, arithmetic and copies ran while one was open for 0% of the time, Pallas kernels for 4%

profile of v6, /device:TPU:136, one launch (start us, length us, event | category | flops | bytes accessed | tf_op | source)
XLA Modules:
  0.0 37.3 jit_solution(5647756809247591171)
XLA Ops:
  0.6 2.5 %shard_map.113 = (f32[128,128]{1,0:T(8,128)}, f32[8,8,128]{2,1,0:T(8,128)S(1)}, f32[5,8,128]{2,1,0:T(8,128)S(1)}, f32[5,8,128]{2,1,0:T(8,128)S(1)}, f32[8,32,128...) custom-call(f32[3,8,8,128]{3,2,1,0:T(8,128)} %refs_0_.1, ...), custom_call_target="tpu_custom_call" | custom-call | tf_op jit(solution)/shard_map/pallas_call | solution.py:413
  3.1 7.5 %all-to-all-start = ((f32[32,4,128]{2,1,0:T(4,128)}), f32[32,4,128]{2,1,0:T(4,128)S(1)}, u32[]{:S(2)}, u32[]{:S(2)}) async-start(f32[32,4,128]{2,1,0:T(4,128)} %bitcast.6), calls=%async_computation | async-start | bytes 131072 | tf_op jit(solution)/shard_map/all_to_all | solution.py:442
  10.7 0.4 shard_map.114
  11.0 5.9 %all-to-all-done = f32[32,4,128]{2,1,0:T(4,128)S(1)} async-done(((f32[32,4,128]{2,1,0:T(4,128)}), f32[32,4,128]{2,1,0:T(4,128)S(1)}, u32[]{:S(2)}, u32[]{:S(2)}) %all-to-all-start) | async-done | bytes 65568 | tf_op jit(solution)/shard_map/all_to_all | solution.py:442
  17.0 1.3 %shard_map.115 = f32[128,128]{1,0:T(8,128)} custom-call(f32[128,128]{1,0:T(8,128)S(1)} %bitcast.10, s32[16,128]{1,0:T(8,128)S(1)} %get-tuple-element.27.slots_ref, f32[3,16,128]{2,1,0:T(8,128)S(1)} %get-tuple-element.30.direction_ref, f32[16,128]{1,0:T(8,128)S(1)} %get-tuple-element.31.stiff_ref, s32[32,128]{1,0:T(8,128)S(1)} %get-tuple-element.32.fibre_ref, ...), custom_call_target="tpu_custom_call" | custom-call | tf_op jit(solution)/shard_map/pallas_call | solution.py:413
  18.3 5.0 %all-to-all-start.1 = ((f32[32,4,128]{2,1,0:T(4,128)}), f32[32,4,128]{2,1,0:T(4,128)S(1)}, u32[]{:S(2)}, u32[]{:S(2)}) async-start(f32[32,4,128]{2,1,0:T(4,128)} %bitcast.8), calls=%async_computation.1 | async-start | bytes 131072 | tf_op jit(solution)/shard_map/all_to_all | solution.py:442
  23.3 0.2 collective-permute-start
  23.5 2.7 %collective-permute-start.1 = (f32[5,8,128]{2,1,0:T(8,128)S(1)}, f32[5,8,128]{2,1,0:T(8,128)S(1)}, u32[]{:S(2)}, u32[]{:S(2)}) collective-permute-start(f32[5,8,128]{2,1,0:T(8,128)S(1)} %get-tuple-element.44), channel_id=1, source_target_pairs={{0,1},{1,0},{2,3},{3,2},{4,5},{5,4},{6,7},{7,6},{8,16},{9,17},{10,... | collective-permute-start | bytes 61448 | tf_op jit(solution)/shard_map/ppermute | solution.py:437
  26.1 0.0 collective-permute-done.even_in_ref.even_x_ref
  26.1 2.7 %collective-permute-done.1.odd_in_ref.odd_x_ref = f32[5,8,128]{2,1,0:T(8,128)S(1)} collective-permute-done((f32[5,8,128]{2,1,0:T(8,128)S(1)}, f32[5,8,128]{2,1,0:T(8,128)S(1)}, u32[]{:S(2)}, u32[]{:S(2)}) %collective-permute-start.1) | collective-permute-done | bytes 20512 | tf_op jit(solution)/shard_map/ppermute | solution.py:437
  28.8 1.1 %collective-permute-start.2 = (f32[50,128]{1,0:T(8,128)S(1)}, f32[50,128]{1,0:T(8,128)S(1)}, u32[]{:S(2)}, u32[]{:S(2)}) collective-permute-start(f32[50,128]{1,0:T(8,128)S(1)} %get-tuple-element.45), channel_id=1, source_target_pairs={{0,1},{1,0},{2,3},{3,2},{4,5},{5,4},{6,7},{7,6},{8,9},{9,8},{10,11... | collective-permute-start | bytes 76808 | tf_op jit(solution)/shard_map/ppermute | solution.py:437
  29.9 0.0 collective-permute-start.3
  29.9 0.5 %shard_map.116.depth_ref = bf16[32,256,128]{2,1,0:T(8,128)(2,1)S(1)} custom-call(s32[32,128]{1,0:T(8,128)S(1)} %get-tuple-element.34.element_ref, f32[3,32,128]{2,1,0:T(8,128)S(1)} %get-tuple-element.35.coords_ref), custom_call_target="tpu_custom_call" | custom-call | tf_op jit(solution)/shard_map/pallas_call | solution.py:413
  30.4 2.4 %collective-permute-done.2.even_y_ref = f32[50,128]{1,0:T(8,128)S(1)} collective-permute-done((f32[50,128]{1,0:T(8,128)S(1)}, f32[50,128]{1,0:T(8,128)S(1)}, u32[]{:S(2)}, u32[]{:S(2)}) %collective-permute-start.2) | collective-permute-done | bytes 25632 | tf_op jit(solution)/shard_map/ppermute | solution.py:437
  32.8 2.2 %collective-permute-done.3.odd_y_ref = f32[50,128]{1,0:T(8,128)S(1)} collective-permute-done((f32[50,128]{1,0:T(8,128)S(1)}, f32[50,128]{1,0:T(8,128)S(1)}, u32[]{:S(2)}, u32[]{:S(2)}) %collective-permute-start.3) | collective-permute-done | bytes 25632 | tf_op jit(solution)/shard_map/ppermute | solution.py:437
  35.0 0.6 %shard_map.118 = (f32[3,8,8,128]{3,2,1,0:T(8,128)S(1)}, f32[3,8,8,128]{3,2,1,0:T(8,128)S(1)}, f32[8,8,128]{2,1,0:T(8,128)S(1)}) custom-call(f32[3,8,8,128]{3,2,1,0:T(8,128)S(1)} %get-tuple-element.38.u_ref, f32[3,8,8,128]{3,2,1,0:T(8,128)S(1)} %get-tuple-element.39.velocity_ref, f32[3,8,8,128]{3,2,1,0:T(8,128)S(1)} %get-tuple-element.40.load_ref, ...), custom_call_target="tpu_custom_call" | custom-call | tf_op jit(solution)/shard_map/pallas_call | solution.py:413
  35.6 0.0 all-to-all-done.1
  35.6 1.7 %shard_map.119 = (f32[3,8,8,128]{3,2,1,0:T(8,128)}, f32[3,8,8,128]{3,2,1,0:T(8,128)}) custom-call(f32[128,128]{1,0:T(8,128)S(1)} %bitcast.11, bf16[32,256,128]{2,1,0:T(8,128)(2,1)S(1)} %shard_map.116.depth_ref, f32[8,32,128]{2,1,0:T(8,128)S(1)} %get-tuple-element.36.weight_x_ref, f32[32,8,128]{2,1,0:T(8,128)S(1)} %get-tuple-element.37.weight_y_ref, ...), custom_call_target="tpu_custom_call" | custom-call | tf_op jit(solution)/shard_map/pallas_call | solution.py:413
  (1 shorter events, 0.0 us)
Async XLA Ops:
  3.1 13.9 %all-to-all-start = ((f32[32,4,128]{2,1,0:T(4,128)}), f32[32,4,128]{2,1,0:T(4,128)S(1)}, u32[]{:S(2)}, u32[]{:S(2)}) async-start(f32[32,4,128]{2,1,0:T(4,128)} %bitcast.6), calls=%async_computation | async-start | bytes 131072 | tf_op jit(solution)/shard_map/all_to_all | solution.py:442
  18.3 17.3 %all-to-all-start.1 = ((f32[32,4,128]{2,1,0:T(4,128)}), f32[32,4,128]{2,1,0:T(4,128)S(1)}, u32[]{:S(2)}, u32[]{:S(2)}) async-start(f32[32,4,128]{2,1,0:T(4,128)} %bitcast.8), calls=%async_computation.1 | async-start | bytes 131072 | tf_op jit(solution)/shard_map/all_to_all | solution.py:442
  23.3 2.9 %collective-permute-start = (f32[5,8,128]{2,1,0:T(8,128)S(1)}, f32[5,8,128]{2,1,0:T(8,128)S(1)}, u32[]{:S(2)}, u32[]{:S(2)}) collective-permute-start(f32[5,8,128]{2,1,0:T(8,128)S(1)} %get-tuple-element.43), channel_id=1, source_target_pairs={{0,8},{1,9},{2,10},{3,11},{4,12},{5,13},{6,14},{7,15},{8,0},{9,1},... | collective-permute-start | bytes 61448 | tf_op jit(solution)/shard_map/ppermute | solution.py:437
  23.5 5.3 %collective-permute-start.1 = (f32[5,8,128]{2,1,0:T(8,128)S(1)}, f32[5,8,128]{2,1,0:T(8,128)S(1)}, u32[]{:S(2)}, u32[]{:S(2)}) collective-permute-start(f32[5,8,128]{2,1,0:T(8,128)S(1)} %get-tuple-element.44), channel_id=1, source_target_pairs={{0,1},{1,0},{2,3},{3,2},{4,5},{5,4},{6,7},{7,6},{8,16},{9,17},{10,... | collective-permute-start | bytes 61448 | tf_op jit(solution)/shard_map/ppermute | solution.py:437
  28.8 4.0 %collective-permute-start.2 = (f32[50,128]{1,0:T(8,128)S(1)}, f32[50,128]{1,0:T(8,128)S(1)}, u32[]{:S(2)}, u32[]{:S(2)}) collective-permute-start(f32[50,128]{1,0:T(8,128)S(1)} %get-tuple-element.45), channel_id=1, source_target_pairs={{0,1},{1,0},{2,3},{3,2},{4,5},{5,4},{6,7},{7,6},{8,9},{9,8},{10,11... | collective-permute-start | bytes 76808 | tf_op jit(solution)/shard_map/ppermute | solution.py:437
  29.9 5.1 %collective-permute-start.3 = (f32[50,128]{1,0:T(8,128)S(1)}, f32[50,128]{1,0:T(8,128)S(1)}, u32[]{:S(2)}, u32[]{:S(2)}) collective-permute-start(f32[50,128]{1,0:T(8,128)S(1)} %get-tuple-element.46), channel_id=1, source_target_pairs={{0,8},{1,2},{2,1},{3,4},{4,3},{5,6},{6,5},{7,15},{8,0},{9,10},{10,... | collective-permute-start | bytes 76808 | tf_op jit(solution)/shard_map/ppermute | solution.py:437

commit v7 on v6

--- a/solution.py
+++ b/solution.py
@@ -79,19 +79,17 @@
 
 
 def interpolate_kernel(*refs):
-    count = (len(refs) - 7) // 2
-    sources, targets, semaphores = refs[:count], refs[count + 6 : -1], refs[-1]
-    places_ref, modulus_ref, even_ref, odd_ref, weight_x_ref, weight_y_ref = refs[
-        count : count + 6
-    ]
+    count = (len(refs) - 4) // 2
+    sources, targets, semaphores = refs[:count], refs[count + 3 : -1], refs[-1]
+    places_ref, weight_x_ref, weight_y_ref = refs[count : count + 3]
     copies = [
         pltpu.make_async_copy(source, target, semaphores.at[index])
         for index, (source, target) in enumerate(zip(sources, targets))
     ]
     for copy in copies:
         copy.start()
-    u_ref, element_ref, coords_ref, density_ref, class_ref = targets[:5]
-    for copy in copies[:5]:
+    u_ref, element_ref, coords_ref = targets[:3]
+    for copy in copies[:3]:
         copy.wait()
     lowest, along = element_ref[...] >> 10, coords_ref[0]
     for x in range(8):
@@ -137,6 +135,11 @@
                 )
             places_ref[pl.ds(4 * owner + 3, 1), :] = jnp.zeros((1, LANES), F32)
 
+    for copy in copies[3:]:
+        copy.wait()
+
+
+def rows_kernel(u_ref, density_ref, class_ref, modulus_ref, even_ref, odd_ref):
     lane_block = iota((16, LANES), 1) >> 3
     pick = (lane_block == iota((16, LANES), 0)).astype(F32)
     kind = jnp.dot(
@@ -153,8 +156,6 @@
         first, last = source[0], source[7]
         even_ref[comp] = jnp.where(odd_dom, first, last)
         odd_ref[comp] = jnp.where(end, 0.0, jnp.where(odd_dom, last, first))
-    for copy in copies[5:]:
-        copy.wait()
 
 
 def weights_kernel(element_ref, coords_ref, depth_ref):
@@ -462,18 +463,19 @@
         fibre_angles.reshape(2, 16, LANES),
         fibre_stiffness.reshape(1, 16),
     )
-    places, modulus, even_x, odd_x, weight_x, weight_y, *arguments = call(
+    places, weight_x, weight_y, *arguments = call(
         interpolate_kernel,
-        (
-            ((128, LANES), F32), (plane, F32), ((5, 8, LANES), F32), ((5, 8, LANES), F32),
-            ((8, 32, LANES), F32), ((32, 8, LANES), F32),
-        )
+        (((128, LANES), F32), ((8, 32, LANES), F32), ((32, 8, LANES), F32))
         + tuple((value.shape, value.dtype) for value in arguments),
         arguments,
         scratch=(pltpu.SemaphoreType.DMA((len(arguments),)),),
         first=True,
     )
-    displacement, element, coords, density, _, velocity, load, slots, angles, stiffness = arguments
+    displacement, element, coords, density, kinds, velocity, load, slots, angles, stiffness = arguments
+    modulus, even_x, odd_x = call(
+        rows_kernel, ((plane, F32), ((5, 8, LANES), F32), ((5, 8, LANES), F32)),
+        (displacement, density, kinds),
+    )
     even_x = swap(even_x, DOM, 0)
     odd_x = swap(odd_x, DOM, 1)
     received = exchange(places)

time: 37.5 us -> 37.6 us (level)
    pallas_call x7 -> x8, Pallas kernels: 6.96 us -> 7.07 us  [call(): pl.pallas_call(kernel, out_shape=outs, in_specs=[pl.BlockSpec(memory_spac...]
where the time goes in v7:
time: 37.6 us; the launch traced here: 37.4 us
  starting transfers between devices  16.4 us (44%)
  waiting for transfers between devices  13.2 us (35%)
  Pallas kernels  7.07 us (19%)
  between operations  0.69 us (2%)
    all_to_all x2, starting transfers between devices, exchange(): lax.all_to_all(blocks, DOM, split_axis=0, concat_axis=0, tiled=True)  12.5 us
    ppermute x4, waiting for transfers between devices, swap(): return lax.ppermute(shard, (*DOM, 'blk'), pairs)  7.25 us
    pallas_call x8, Pallas kernels, call(): pl.pallas_call(kernel, out_shape=outs, in_specs=[pl.BlockSpec(memory_spac...  7.07 us
    all_to_all x2, waiting for transfers between devices, exchange(): lax.all_to_all(blocks, DOM, split_axis=0, concat_axis=0, tiled=True)  5.95 us
    ppermute x4, starting transfers between devices, swap(): return lax.ppermute(shard, (*DOM, 'blk'), pairs)  3.88 us
  transfers between devices with their start and end apart: 6, of which 4 were waited for; matrix products, arithmetic and copies ran while one was open for 0% of the time, Pallas kernels for 4%

profile of v7, /device:TPU:136, one launch (start us, length us, event | category | flops | bytes accessed | tf_op | source)
XLA Modules:
  0.0 37.4 jit_solution(8859353700766601679)
XLA Ops:
  0.6 2.5 %shard_map.113 = (f32[128,128]{1,0:T(8,128)}, f32[8,32,128]{2,1,0:T(8,128)S(1)}, f32[32,8,128]{2,1,0:T(8,128)S(1)}, f32[3,8,8,128]{3,2,1,0:T(8,128)S(1)}, s32[32...) custom-call(f32[3,8,8,128]{3,2,1,0:T(8,128)} %refs_0_.1, ...), custom_call_target="tpu_custom_call" | custom-call | tf_op jit(solution)/shard_map/pallas_call | solution.py:414
  3.1 7.6 %all-to-all-start = ((f32[32,4,128]{2,1,0:T(4,128)}), f32[32,4,128]{2,1,0:T(4,128)S(1)}, u32[]{:S(2)}, u32[]{:S(2)}) async-start(f32[32,4,128]{2,1,0:T(4,128)} %bitcast.6), calls=%async_computation | async-start | bytes 131072 | tf_op jit(solution)/shard_map/all_to_all | solution.py:443
  10.7 0.4 shard_map.114
  11.0 5.9 %all-to-all-done = f32[32,4,128]{2,1,0:T(4,128)S(1)} async-done(((f32[32,4,128]{2,1,0:T(4,128)}), f32[32,4,128]{2,1,0:T(4,128)S(1)}, u32[]{:S(2)}, u32[]{:S(2)}) %all-to-all-start) | async-done | bytes 65568 | tf_op jit(solution)/shard_map/all_to_all | solution.py:443
  17.0 1.3 %shard_map.115 = f32[128,128]{1,0:T(8,128)} custom-call(f32[128,128]{1,0:T(8,128)S(1)} %bitcast.10, s32[16,128]{1,0:T(8,128)S(1)} %get-tuple-element.28.slots_ref, f32[3,16,128]{2,1,0:T(8,128)S(1)} %get-tuple-element.31.direction_ref, f32[16,128]{1,0:T(8,128)S(1)} %get-tuple-element.32.stiff_ref, s32[32,128]{1,0:T(8,128)S(1)} %get-tuple-element.33.fibre_ref, ...), custom_call_target="tpu_custom_call" | custom-call | tf_op jit(solution)/shard_map/pallas_call | solution.py:414
  18.3 5.0 %all-to-all-start.1 = ((f32[32,4,128]{2,1,0:T(4,128)}), f32[32,4,128]{2,1,0:T(4,128)S(1)}, u32[]{:S(2)}, u32[]{:S(2)}) async-start(f32[32,4,128]{2,1,0:T(4,128)} %bitcast.8), calls=%async_computation.1 | async-start | bytes 131072 | tf_op jit(solution)/shard_map/all_to_all | solution.py:443
  23.3 0.1 shard_map.117
  23.4 0.1 collective-permute-start
  23.5 2.7 %collective-permute-start.1 = (f32[5,8,128]{2,1,0:T(8,128)S(1)}, f32[5,8,128]{2,1,0:T(8,128)S(1)}, u32[]{:S(2)}, u32[]{:S(2)}) collective-permute-start(f32[5,8,128]{2,1,0:T(8,128)S(1)} %get-tuple-element.46), channel_id=1, source_target_pairs={{0,1},{1,0},{2,3},{3,2},{4,5},{5,4},{6,7},{7,6},{8,16},{9,17},{10,... | collective-permute-start | bytes 61448 | tf_op jit(solution)/shard_map/ppermute | solution.py:438
  26.2 0.0 collective-permute-done.even_in_ref.even_x_ref
  26.2 2.7 %collective-permute-done.1.odd_in_ref.odd_x_ref = f32[5,8,128]{2,1,0:T(8,128)S(1)} collective-permute-done((f32[5,8,128]{2,1,0:T(8,128)S(1)}, f32[5,8,128]{2,1,0:T(8,128)S(1)}, u32[]{:S(2)}, u32[]{:S(2)}) %collective-permute-start.1) | collective-permute-done | bytes 20512 | tf_op jit(solution)/shard_map/ppermute | solution.py:438
  28.9 1.1 %collective-permute-start.2 = (f32[50,128]{1,0:T(8,128)S(1)}, f32[50,128]{1,0:T(8,128)S(1)}, u32[]{:S(2)}, u32[]{:S(2)}) collective-permute-start(f32[50,128]{1,0:T(8,128)S(1)} %get-tuple-element.47), channel_id=1, source_target_pairs={{0,1},{1,0},{2,3},{3,2},{4,5},{5,4},{6,7},{7,6},{8,9},{9,8},{10,11... | collective-permute-start | bytes 76808 | tf_op jit(solution)/shard_map/ppermute | solution.py:438
  30.0 0.0 collective-permute-start.3
  30.0 0.5 %shard_map.116.depth_ref = bf16[32,256,128]{2,1,0:T(8,128)(2,1)S(1)} custom-call(s32[32,128]{1,0:T(8,128)S(1)} %get-tuple-element.35.element_ref, f32[3,32,128]{2,1,0:T(8,128)S(1)} %get-tuple-element.36.coords_ref), custom_call_target="tpu_custom_call" | custom-call | tf_op jit(solution)/shard_map/pallas_call | solution.py:414
  30.5 2.4 %collective-permute-done.2.even_y_ref = f32[50,128]{1,0:T(8,128)S(1)} collective-permute-done((f32[50,128]{1,0:T(8,128)S(1)}, f32[50,128]{1,0:T(8,128)S(1)}, u32[]{:S(2)}, u32[]{:S(2)}) %collective-permute-start.2) | collective-permute-done | bytes 25632 | tf_op jit(solution)/shard_map/ppermute | solution.py:438
  32.8 2.2 %collective-permute-done.3.odd_y_ref = f32[50,128]{1,0:T(8,128)S(1)} collective-permute-done((f32[50,128]{1,0:T(8,128)S(1)}, f32[50,128]{1,0:T(8,128)S(1)}, u32[]{:S(2)}, u32[]{:S(2)}) %collective-permute-start.3) | collective-permute-done | bytes 25632 | tf_op jit(solution)/shard_map/ppermute | solution.py:438
  35.1 0.6 %shard_map.119 = (f32[3,8,8,128]{3,2,1,0:T(8,128)S(1)}, f32[3,8,8,128]{3,2,1,0:T(8,128)S(1)}, f32[8,8,128]{2,1,0:T(8,128)S(1)}) custom-call(f32[3,8,8,128]{3,2,1,0:T(8,128)S(1)} %get-tuple-element.39.u_ref, f32[3,8,8,128]{3,2,1,0:T(8,128)S(1)} %get-tuple-element.40.velocity_ref, f32[3,8,8,128]{3,2,1,0:T(8,128)S(1)} %get-tuple-element.41.load_ref, ...), custom_call_target="tpu_custom_call" | custom-call | tf_op jit(solution)/shard_map/pallas_call | solution.py:414
  35.6 0.0 all-to-all-done.1
  35.6 1.7 %shard_map.120 = (f32[3,8,8,128]{3,2,1,0:T(8,128)}, f32[3,8,8,128]{3,2,1,0:T(8,128)}) custom-call(f32[128,128]{1,0:T(8,128)S(1)} %bitcast.11, bf16[32,256,128]{2,1,0:T(8,128)(2,1)S(1)} %shard_map.116.depth_ref, f32[8,32,128]{2,1,0:T(8,128)S(1)} %get-tuple-element.37.weight_x_ref, f32[32,8,128]{2,1,0:T(8,128)S(1)} %get-tuple-element.38.weight_y_ref, ...), custom_call_target="tpu_custom_call" | custom-call | tf_op jit(solution)/shard_map/pallas_call | solution.py:414
  (1 shorter events, 0.0 us)
Async XLA Ops:
  3.1 13.9 %all-to-all-start = ((f32[32,4,128]{2,1,0:T(4,128)}), f32[32,4,128]{2,1,0:T(4,128)S(1)}, u32[]{:S(2)}, u32[]{:S(2)}) async-start(f32[32,4,128]{2,1,0:T(4,128)} %bitcast.6), calls=%async_computation | async-start | bytes 131072 | tf_op jit(solution)/shard_map/all_to_all | solution.py:443
  18.3 17.3 %all-to-all-start.1 = ((f32[32,4,128]{2,1,0:T(4,128)}), f32[32,4,128]{2,1,0:T(4,128)S(1)}, u32[]{:S(2)}, u32[]{:S(2)}) async-start(f32[32,4,128]{2,1,0:T(4,128)} %bitcast.8), calls=%async_computation.1 | async-start | bytes 131072 | tf_op jit(solution)/shard_map/all_to_all | solution.py:443
  23.4 2.8 %collective-permute-start = (f32[5,8,128]{2,1,0:T(8,128)S(1)}, f32[5,8,128]{2,1,0:T(8,128)S(1)}, u32[]{:S(2)}, u32[]{:S(2)}) collective-permute-start(f32[5,8,128]{2,1,0:T(8,128)S(1)} %get-tuple-element.45), channel_id=1, source_target_pairs={{0,8},{1,9},{2,10},{3,11},{4,12},{5,13},{6,14},{7,15},{8,0},{9,1},... | collective-permute-start | bytes 61448 | tf_op jit(solution)/shard_map/ppermute | solution.py:438
  23.5 5.3 %collective-permute-start.1 = (f32[5,8,128]{2,1,0:T(8,128)S(1)}, f32[5,8,128]{2,1,0:T(8,128)S(1)}, u32[]{:S(2)}, u32[]{:S(2)}) collective-permute-start(f32[5,8,128]{2,1,0:T(8,128)S(1)} %get-tuple-element.46), channel_id=1, source_target_pairs={{0,1},{1,0},{2,3},{3,2},{4,5},{5,4},{6,7},{7,6},{8,16},{9,17},{10,... | collective-permute-start | bytes 61448 | tf_op jit(solution)/shard_map/ppermute | solution.py:438
  28.9 4.0 %collective-permute-start.2 = (f32[50,128]{1,0:T(8,128)S(1)}, f32[50,128]{1,0:T(8,128)S(1)}, u32[]{:S(2)}, u32[]{:S(2)}) collective-permute-start(f32[50,128]{1,0:T(8,128)S(1)} %get-tuple-element.47), channel_id=1, source_target_pairs={{0,1},{1,0},{2,3},{3,2},{4,5},{5,4},{6,7},{7,6},{8,9},{9,8},{10,11... | collective-permute-start | bytes 76808 | tf_op jit(solution)/shard_map/ppermute | solution.py:438
  30.0 5.1 %collective-permute-start.3 = (f32[50,128]{1,0:T(8,128)S(1)}, f32[50,128]{1,0:T(8,128)S(1)}, u32[]{:S(2)}, u32[]{:S(2)}) collective-permute-start(f32[50,128]{1,0:T(8,128)S(1)} %get-tuple-element.48), channel_id=1, source_target_pairs={{0,8},{1,2},{2,1},{3,4},{4,3},{5,6},{6,5},{7,15},{8,0},{9,10},{10,... | collective-permute-start | bytes 76808 | tf_op jit(solution)/shard_map/ppermute | solution.py:438
